TPU v7x, 32 devices: a whole 2x2x4 slice. The times are simulated.
32 devices in a mesh: wide: 8 (over y, x, core), blk: 4 (over z).
Axes of the slice: x: 2, y: 2, z: 4, core: 2. Of those that a mesh axis runs over, the one named last changes fastest.
Arguments:
- left_points: float32 [4096], P(('wide', 'blk')), may hold values from -1 to 1, as said below
- left_ports: int32 [4096], P(('wide', 'blk')), may hold values from 0 to 63
- left_values: bfloat16 [4096, 64], P(('wide', 'blk')), may hold values from -6 to 6
- right_points: float32 [2048], P('blk'), may hold values from -1 to 1
- right_ports: int32 [2048], P('blk'), may hold values from 0 to 63
- right_values: bfloat16 [2048, 64], P('blk'), may hold values from -6 to 6
- sketch_block: int32 [2048], P('blk'), may hold values from 0 to 63, as said below
- sketch_weight: bfloat16 [2048], P('blk'), may hold values from -1 to 1
Outputs:
- basis: float32 [4096, 64], P(('wide', 'blk'))
- projected: float32 [64, 64], replicated
Inputs may be any that keep to these rules, and one draw needn't show every extreme that they name: `left_points`: no left point lies closer than 0.6 / 2048 to any right point. `sketch_block`: in every aligned run of 64 right samples each sketch column appears exactly once.
All inputs are finite; a program needn't handle non-finite values.
Results may differ from a plain program's by a relative error of at most 0.0019.
Values sent between devices are 32-bit elements; how exact they have to be, the bound alone decides.
No kernel may reach another device: no remote copies, remote signals or barrier semaphores. Data moves between devices by JAX's collectives and lax.ppermute only.
A program may use at most 64 MiB of HBM per device.

v0:
```python
import jax
import jax.numpy as jnp
from jax import lax
from jax.sharding import PartitionSpec as P

K = 64


def cholesky_lower(gram):
    order = gram.shape[0]
    index_ids = jnp.arange(order, dtype=jnp.int32)

    def column_step(j, lower):
        row_j = lax.dynamic_slice_in_dim(lower, j, 1, 0)[0]
        column = lax.dynamic_slice_in_dim(gram, j, 1, 1)[:, 0] - jnp.dot(
            lower, row_j, precision=lax.Precision.HIGHEST
        )
        pivot = jnp.sqrt(lax.dynamic_slice_in_dim(column, j, 1, 0)[0])
        fresh = jnp.where(
            index_ids > j,
            column / pivot,
            jnp.where(index_ids == j, pivot, jnp.zeros((), gram.dtype)),
        )
        marker = (index_ids == j).astype(gram.dtype)
        return lower + fresh[:, None] * marker[None, :]

    return lax.fori_loop(0, order, column_step, jnp.zeros_like(gram))


def solve_lower(lower, rhs):
    order = lower.shape[0]
    index_ids = jnp.arange(order, dtype=jnp.int32)

    def row_step(j, result):
        row_j = lax.dynamic_slice_in_dim(lower, j, 1, 0)[0]
        pivot = lax.dynamic_slice_in_dim(row_j, j, 1, 0)[0]
        target = lax.dynamic_slice_in_dim(rhs, j, 1, 0)[0]
        value = (target - jnp.dot(row_j, result, precision=lax.Precision.HIGHEST)) / pivot
        marker = (index_ids == j).astype(rhs.dtype)
        return result + marker[:, None] * value[None, :]

    return lax.fori_loop(0, order, row_step, jnp.zeros_like(rhs))


def solve_upper(upper, rhs):
    order = upper.shape[0]
    index_ids = jnp.arange(order, dtype=jnp.int32)

    def row_step(step, result):
        j = order - 1 - step
        row_j = lax.dynamic_slice_in_dim(upper, j, 1, 0)[0]
        pivot = lax.dynamic_slice_in_dim(row_j, j, 1, 0)[0]
        target = lax.dynamic_slice_in_dim(rhs, j, 1, 0)[0]
        value = (target - jnp.dot(row_j, result, precision=lax.Precision.HIGHEST)) / pivot
        marker = (index_ids == j).astype(rhs.dtype)
        return result + marker[:, None] * value[None, :]

    return lax.fori_loop(0, order, row_step, jnp.zeros_like(rhs))


def tile_sketch(left_freq, left_onehot, left_values, points, ports, values_block, columns, weights):
    amount = points.shape[0]
    block_count = amount // amount
    port_ids = jnp.arange(left_values.shape[1], dtype=jnp.int32)
    column_ids = jnp.arange(K, dtype=jnp.int32)

    def absorb(carry, items):
        freq, port_block, value_rows, column_block, weight_block = items
        onehot_right = (port_ids[:, None] == port_block[None, :]).astype(jnp.float32)
        num_v = jnp.dot(
            left_values,
            onehot_right,
            precision=lax.Precision.HIGHEST,
            preferred_element_type=jnp.float32,
        )
        num_w = lax.dot_general(
            left_onehot,
            value_rows,
            (((1,), (1,)), ((), ())),
            precision=lax.Precision.HIGHEST,
            preferred_element_type=jnp.float32,
        )
        inverse = 1.0 / (left_freq[:, None] - freq[None, :])
        loewner = (num_v - num_w) * inverse
        shifted = (left_freq[:, None] * num_v - freq[None, :] * num_w) * inverse
        omega = jnp.where(
            column_block[:, None] == column_ids[None, :],
            weight_block[:, None],
            jnp.zeros((), jnp.float32),
        )
        sketch_part = jnp.dot(
            loewner, omega, precision=lax.Precision.HIGHEST, preferred_element_type=jnp.float32
        )
        shift_part = jnp.dot(
            shifted, omega, precision=lax.Precision.HIGHEST, preferred_element_type=jnp.float32
        )
        return ((carry[0] + sketch_part, carry[1] + shift_part), None)

    row_count = left_values.shape[0]
    start_carry = (jnp.zeros((row_count, K), jnp.float32), jnp.zeros((row_count, K), jnp.float32))
    items = (
        points.reshape(block_count, amount),
        ports.reshape(block_count, amount),
        values_block.reshape(block_count, amount, values_block.shape[1]),
        columns.reshape(block_count, amount),
        weights.reshape(block_count, amount),
    )
    result, _ = lax.scan(absorb, start_carry, items)
    return result


def left_setup(points, ports, width):
    port_ids = jnp.arange(width, dtype=jnp.int32)
    onehot_left = (ports[:, None] == port_ids[None, :]).astype(jnp.float32)
    return (points, onehot_left)


def per_device(
    left_points,
    left_ports,
    left_values,
    right_points,
    right_ports,
    right_values,
    sketch_block,
    sketch_weight,
):
    row_count = left_points.shape[0]
    width = left_values.shape[1]
    left_wide = left_values.astype(jnp.float32)
    group_points, group_ports, group_values = (
        lax.all_gather(left_points, "blk", axis=0, tiled=True),
        lax.all_gather(left_ports, "blk", axis=0, tiled=True),
        lax.all_gather(left_wide, "blk", axis=0, tiled=True),
    )
    right_wide = right_values.astype(jnp.float32)
    weight_wide = sketch_weight.astype(jnp.float32)
    left_freq, left_onehot = left_setup(group_points, group_ports, width)
    sketch_part, shift_part = tile_sketch(
        left_freq,
        left_onehot,
        group_values,
        right_points,
        right_ports,
        right_wide,
        sketch_block,
        weight_wide,
    )
    stacked = lax.psum_scatter(
        jnp.concatenate([sketch_part, shift_part], axis=1), "blk", scatter_dimension=0, tiled=True
    )
    sketch = stacked[:, :K]
    shifted_sketch = stacked[:, K:]
    row_total = row_count * lax.axis_size("wide") * lax.axis_size("blk")
    gram_local = jnp.dot(sketch.T, sketch, precision=lax.Precision.HIGHEST)
    gram = lax.psum(gram_local, ("wide", "blk")) / row_total
    lower = cholesky_lower(gram)
    basis_t = solve_lower(lower, sketch.T)
    projection_local = jnp.dot(basis_t, shifted_sketch, precision=lax.Precision.HIGHEST)
    coefficient = lax.psum(projection_local, ("wide", "blk")) / row_total
    projected = solve_upper(lower.T, coefficient)
    return (basis_t.T, projected)


def solution(mesh):
    placed = (
        P(("wide", "blk")),
        P(("wide", "blk")),
        P(("wide", "blk"), None),
        P("blk"),
        P("blk"),
        P("blk", None),
        P("blk"),
        P("blk"),
    )
    return jax.shard_map(
        per_device,
        mesh=mesh,
        in_specs=placed,
        out_specs=(P(("wide", "blk"), None), P()),
        check_vma=False,
    )
```

profile of v0, /device:TPU:0, one launch (start us, length us, event | category | flops | bytes accessed | tf_op | source)
XLA Modules:
  0.0 438.6 jit_solution(5190188491721261414)
XLA Ops:
  7.9 15.1 %all_gather.9 = f32[512,64]{0,1:T(8,128)S(1)} all-gather(f32[128,64]{0,1:T(8,128)S(1)} %convert_element_type.55), channel_id=1, replica_groups=mesh['wide'=8,'blk'=4] {'blk'}, dimensions={0}, use_global_device_ids=true | all-gather | bytes 163840 | tf_op jit(solution)/shard_map/all_gather | solution.py:134
  23.7 11.2 %all-gather = s32[4,1,128]{2,1,0:T(1,128)S(1)} all-gather(s32[1,1,128]{2,1,0:T(1,128)S(1)} %bitcast.82), channel_id=1, replica_groups=mesh['wide'=8,'blk'=4] {'blk'}, dimensions={0}, use_global_device_ids=true | all-gather | bytes 2560 | tf_op jit(solution)/shard_map/all_gather | solution.py:133
  35.6 7.7 %all-gather.1 = f32[4,1,128]{2,1,0:T(1,128)S(1)} all-gather(f32[1,1,128]{2,1,0:T(1,128)S(1)} %bitcast.83), channel_id=1, replica_groups=mesh['wide'=8,'blk'=4] {'blk'}, dimensions={0}, use_global_device_ids=true | all-gather | bytes 2560 | tf_op jit(solution)/shard_map/all_gather | solution.py:132
  45.3 1.1 fusion.28
  46.4 1.0 fusion.33
  48.1 19.8 %reduce-scatter.2.cloned.1.call-done = f32[128,128]{0,1:T(8,128)} async-done(((f32[512,128]{0,1:T(8,128)}), f32[128,128]{0,1:T(8,128)}) %reduce-scatter.2.cloned.1.call-update) | async-done | bytes 65552 | tf_op jit(solution)/shard_map/reduce_scatter | solution.py:149
  67.9 1.0 fusion.55
  68.9 38.6 %psum.14 = f32[64,64]{1,0:T(8,128)S(1)} all-reduce(f32[64,64]{1,0:T(8,128)S(1)} %fusion.55), channel_id=1, replica_groups=mesh['wide'=8,'blk'=4] {'wide','blk'}, use_global_device_ids=true, to_apply=%region_1.2 | all-reduce | flops 4096 | bytes 32768 | tf_op jit(solution)/shard_map/psum | solution.py:156
  107.7 94.5 %while.57 = (s32[]{:T(128)}, f32[64,64]{1,0:T(8,128)S(1)}, f32[64,64]{0,1:T(8,128)S(1)}, s32[]{:T(128)}, s32[]{:T(128)}) while((s32[]{:T(128)}, f32[64,64]{1,0:T(8,128)S(1)}, f32[64,64]{0,1:T(8,128)S(1)}, s32[]{:T(128)}, s32[]{:T(128)}) %tuple.124), condition=%wide.region_3.4_spmd.clone.clone, body=%wide.region_2.3_spmd.clone.clone.sunk | while | flops 66051 | bytes 101992 | solution.py:27
  202.2 93.7 %while.55 = (s32[]{:T(128)}, f32[64,128]{1,0:T(8,128)S(1)}, f32[64,128]{1,0:T(8,128)S(1)}, f32[64,64]{1,0:T(8,128)S(1)}, s32[]{:T(128)}, /*index=5*/s32[]{:T(128)}, s32[]{:T(128)}) while((s32[]{:T(128)}, f32[64,128]{1,0:T(8,128)S(1)}, f32[64,128]{1,0:T(8,128)S(1)}, f32[64,64]{1,0:T(8,128)S(1)}, s32[]{:T(128)}, ...), condition=%wide.region_5.6_spmd.clone, body=%wide.region_4.5_spmd.clone.sunk | while | flops 131460 | bytes 102520 | solution.py:42
  202.8 0.8 fusion.76
  205.7 0.8 fusion.76
  224.8 0.8 fusion.76
  227.7 0.8 fusion.76
  230.6 0.8 fusion.76
  233.6 0.8 fusion.76
  252.6 0.8 fusion.76
  255.5 0.8 fusion.76
  258.5 0.8 fusion.76
  261.4 0.8 fusion.76
  280.4 0.8 fusion.76
  283.3 0.8 fusion.76
  286.3 0.8 fusion.76
  289.2 0.8 fusion.76
  296.6 40.8 %psum.15 = f32[64,64]{1,0:T(8,128)S(1)} all-reduce(f32[64,64]{1,0:T(8,128)S(1)} %fusion.53), channel_id=1, replica_groups=mesh['wide'=8,'blk'=4] {'wide','blk'}, use_global_device_ids=true, to_apply=%region_6.7 | all-reduce | flops 4096 | bytes 32768 | tf_op jit(solution)/shard_map/psum | solution.py:160
  337.5 93.7 %while.56 = (s32[]{:T(128)}, f32[64,64]{1,0:T(8,128)S(1)}, f32[64,64]{1,0:T(8,128)S(1)}, f32[64,64]{1,0:T(8,128)S(1)}, s32[]{:T(128)}, /*index=5*/s32[]{:T(128)}, s32[]{:T(128)}, s32[]{:T(128)}) while((s32[]{:T(128)}, f32[64,64]{1,0:T(8,128)S(1)}, f32[64,64]{1,0:T(8,128)S(1)}, f32[64,64]{1,0:T(8,128)S(1)}, s32[]{:T(128)}, ...), condition=%wide.region_8.9_spmd.clone, body=%wide.region_7.8_spmd.clone.sunk | while | flops 65800 | bytes 69297 | solution.py:58
  339.5 0.8 fusion.79
  346.9 0.8 fusion.79
  352.7 0.8 fusion.79
  360.0 0.8 fusion.79
  367.4 0.8 fusion.79
  374.7 0.8 fusion.79
  (912 shorter events, 232.1 us)
Async XLA Ops:
  7.2 37.4 %copy-start = (bf16[512,64]{0,1:T(8,128)(2,1)S(1)}, bf16[512,64]{0,1:T(8,128)(2,1)}, u32[]{:S(2)}) copy-start(bf16[512,64]{0,1:T(8,128)(2,1)} %param.19) | copy-start | bytes 196612
  7.2 60.7 %reduce-scatter.2.cloned.1.call-start = ((), (), s32[]{:S(2)}) async-start(), calls=%async_computation.1 | async-start | bytes 327680 | tf_op jit(solution)/shard_map/reduce_scatter | solution.py:149
  23.0 0.7 copy-start.6
  34.9 0.7 copy-start.7
  35.6 7.7 %copy-start.5 = (bf16[512]{0:T(512)(128)(2,1)S(1)}, bf16[512]{0:T(512)(128)(2,1)}, u32[]{:S(2)}) copy-start(bf16[512]{0:T(512)(128)(2,1)} %param.21) | copy-start | bytes 3076
  43.3 0.7 copy-start.4
  44.6 0.7 copy-start.8
  44.6 0.7 copy-start.9
  107.7 94.5 %copy-start.3 = (f32[128,128]{0,1:T(8,128)S(1)}, f32[128,128]{0,1:T(8,128)}, u32[]{:S(2)}) copy-start(f32[128,128]{0,1:T(8,128)} %reduce-scatter.2.cloned.1.call-done) | copy-start | bytes 196612
  295.9 0.6 copy-start.1
  431.2 0.6 copy-start.2
Sparse Core Ops, SparseCore 0:
  48.2 19.6 reduce-scatter.1
where the time goes:
time: 441 us; the launch traced here: 439 us
  local copies, waits for them, and re-layouts  119 us (27%)
  matrix products  114 us (26%)
  blocking collectives  113 us (26%)
  loops' own time  40.3 us (9%)
  waiting for transfers between devices  19.8 us (4%)
  other arithmetic  18.2 us (4%)
  between operations  14.2 us (3%)
    dot_general x128, matrix products, row_step(): jnp.dot(row_j, result, precision=lax.Precision.HIGHEST)  100 us
    dynamic_slice x128, local copies, waits for them, and re-layouts, row_step(): pivot = lax.dynamic_slice_in_dim(row_j, j, 1, 0)[0]  76.2 us
    psum x1, blocking collectives, per_device(): coefficient = lax.psum(projection_local, ('wide', 'blk')) / row_total  40.8 us
    another operation x1, loops' own time, cholesky_lower(): return lax.fori_loop(0, order, column_step, jnp.zeros_like(gram))  40 us
    dynamic_slice x64, local copies, waits for them, and re-layouts, column_step(): pivot = jnp.sqrt(lax.dynamic_slice_in_dim(column, j, 1, 0)[0])  39.2 us
    psum x1, blocking collectives, per_device(): gram = lax.psum(gram_local, ('wide', 'blk')) / row_total  38.6 us
    reduce_scatter x1, waiting for transfers between devices, per_device(): lax.psum_scatter(jnp.concatenate([sketch_part, shift_part], axis=1), 'blk...  19.8 us
    all_gather x1, blocking collectives, per_device(): lax.all_gather(left_wide, 'blk', axis=0, tiled=True)  15.1 us
  transfers between devices with their start and end apart: 1, of which 1 were waited for; matrix products, arithmetic and copies ran while one was open for 0% of the time, Pallas kernels for 0%

commit v1 on v0

v1 whole, which is shorter than its diff:
```python
import functools

import jax
import jax.numpy as jnp
from jax import lax
from jax.experimental import pallas as pl
from jax.experimental.pallas import tpu as pltpu
from jax.sharding import PartitionSpec as P

K = 64
LANES = 128
SUB = 8
HIGHEST = lax.Precision.HIGHEST


def swap(value, axis, distance):
    size = lax.axis_size(axis)
    return lax.ppermute(value, axis, [(i, i ^ distance) for i in range(size)])


def kernel_call(body, out_shape, **kw):
    return pl.pallas_call(body, out_shape=out_shape, **kw)


def pieces(value, count=3):
    out = []
    for _ in range(count - 1):
        top = value.astype(jnp.bfloat16)
        out.append(top)
        value = value - top.astype(jnp.float32)
    out.append(value.astype(jnp.bfloat16))
    return out


def dot(a, b, ca, cb, precision=None):
    return lax.dot_general(
        a, b, (((ca,), (cb,)), ((), ())), precision=precision, preferred_element_type=jnp.float32
    )


def pack_body(mu, lp, lv, lam, rp, rv, col, w, left, right):
    half = lv.shape[0] // 2
    left[:half, :K] = lv[:half, :].astype(jnp.float32)
    left[:half, K:] = lv[half:, :].astype(jnp.float32)
    left[half : half + 1, :] = mu[...]
    left[half + 1 : half + 2, :] = lp[...].astype(jnp.float32)
    left[half + 2 :, :] = jnp.zeros((left.shape[0] - half - 2, LANES), jnp.float32)
    half = rv.shape[0] // 2
    right[:half, :K] = rv[:half, :].astype(jnp.float32)
    right[:half, K:] = rv[half:, :].astype(jnp.float32)
    n = lam.shape[0]
    right[half : half + n, :] = lam[...]
    right[half + n : half + 2 * n, :] = rp[...].astype(jnp.float32)
    right[half + 2 * n : half + 3 * n, :] = col[...].astype(jnp.float32)
    right[half + 3 * n : half + 4 * n, :] = w[...]


def column(row):
    return jnp.broadcast_to(row, (LANES, LANES)).T


def sketch_body(n_left, n_right, *refs):
    lefts, rights, (pay, mu_out, hot_out) = refs[:n_left], refs[n_left : n_left + n_right], refs[n_left + n_right :]
    half = (lefts[0].shape[0] // SUB - 1) * SUB
    rows = LANES * n_left
    lane = lax.broadcasted_iota(jnp.int32, (LANES, LANES), 1).astype(jnp.float32)
    mus, hots, values = [], [], []
    for left in lefts:
        mus.append(column(left[half : half + 1, :]))
        ports = column(left[half + 1 : half + 2, :])
        hots.append(
            (
                jnp.where(ports == lane, 1.0, 0.0).astype(jnp.bfloat16),
                jnp.where(ports + K == lane, 1.0, 0.0).astype(jnp.bfloat16),
            )
        )
        values += [left[:half, :K].astype(jnp.bfloat16), left[:half, K:].astype(jnp.bfloat16)]
    values = jnp.concatenate(values, axis=0)
    low, high = jnp.concatenate([h[0] for h in hots], axis=0), jnp.concatenate([h[1] for h in hots], axis=0)
    total = jnp.zeros((rows, K), jnp.float32)
    cross = jnp.zeros((K, LANES), jnp.float32)
    first = lax.broadcasted_iota(jnp.int32, (K, LANES), 1) < K
    for right in rights:
        n = right.shape[0] * 2 // (LANES + SUB)
        depth = n * K
        table = right[:depth, :].astype(jnp.bfloat16)
        seconds = []
        for part in range(2):
            spots = range(part * n // 2, (part + 1) * n // 2)

            def along(which):
                return jnp.concatenate(
                    [right[depth + which * n + s : depth + which * n + s + 1, :] for s in spots], axis=1
                )

            width = LANES * len(spots)
            index = lax.broadcasted_iota(jnp.int32, (K, width), 0).astype(jnp.float32)
            lam = along(0)
            pick = jnp.where(along(1) == index, 1.0, 0.0).astype(jnp.bfloat16)
            omega = jnp.where(along(2) == index, along(3), 0.0).astype(jnp.bfloat16)
            upper = dot(values, pick, 1, 0)
            lower = dot(high if part else low, table, 1, 1)
            scale = jnp.concatenate(
                [jnp.concatenate([m] * len(spots), axis=1) for m in mus], axis=0
            ) - lam
            loewner = (upper - lower) / scale
            for piece in pieces(loewner):
                total = total + dot(piece, omega, 1, 1)
            seconds.append(dot(omega, table, 1, 0))
        cross = cross + jnp.where(first, seconds[0], seconds[1])
    cross = cross[:, :K] + cross[:, K:]
    pay[: rows // 2, :] = jnp.concatenate([total[: rows // 2], total[rows // 2 :]], axis=1)
    pay[rows // 2 :, :] = jnp.concatenate([cross[: K // 2], cross[K // 2 :]], axis=1)
    mus = jnp.concatenate(mus, axis=0)
    ohs = low[:, :K].astype(jnp.float32)
    mu_out[...] = jnp.concatenate([mus[: rows // 2, :K], mus[rows // 2 :, K:]], axis=1)
    hot_out[...] = jnp.concatenate([ohs[: rows // 2], ohs[rows // 2 :]], axis=1)


def moments_body(own, other, mu, hot, gc, full):
    depth = mu.shape[0]
    sketch = own[:depth, :] + other[:depth, :]
    cross = own[depth:, :] + other[depth:, :]
    cross = jnp.concatenate([cross[:, :K], cross[:, K:]], axis=0)
    zero = jnp.zeros_like(cross)
    wide = jnp.concatenate(
        [jnp.concatenate([cross, zero], axis=1), jnp.concatenate([zero, cross], axis=1)], axis=0
    )
    shifted = mu[...] * sketch
    ohs = hot[...].astype(jnp.bfloat16)
    for piece in pieces(wide):
        shifted = shifted + dot(ohs, piece, 1, 1)
    both = dot(sketch, jnp.concatenate([sketch, shifted], axis=1), 0, 0, HIGHEST)
    gc[...] = jnp.concatenate(
        [both[:K, :K] + both[K:, K:LANES], both[:K, LANES : LANES + K] + both[K:, LANES + K :]], axis=1
    )
    full[...] = sketch


def finish_body(scale, place, own, other, sketch, basis, projected):
    gc = (own[...] + other[...]) * scale
    lane = lax.broadcasted_iota(jnp.int32, (SUB, LANES), 1)
    sub = lax.broadcasted_iota(jnp.int32, (SUB, LANES), 0)
    blocks = []
    for r in range(K // SUB):
        blocks.append(
            jnp.where(lane < K, gc[r * SUB : (r + 1) * SUB, :], jnp.where(lane == sub + (K + r * SUB), 1.0, 0.0))
        )
    for j in range(K):
        r, s = divmod(j, SUB)
        row = blocks[r][s : s + 1, :]
        row = row / row[:, j : j + 1]
        for q in range(r, K // SUB):
            factor = blocks[q][:, j : j + 1]
            if q == r:
                if s == SUB - 1:
                    continue
                factor = jnp.where(sub[:, :1] > s, factor, 0.0)
            blocks[q] = blocks[q] - factor * row
    done = []
    for r in range(K // SUB):
        pivot = jnp.sum(jnp.where(lane == sub + r * SUB, blocks[r], 0.0), axis=1, keepdims=True)
        done.append(blocks[r][:, K:] / jnp.sqrt(pivot))
    inverse = jnp.concatenate(done, axis=0)
    rows = basis.shape[0]
    spots = sketch.shape[0] // rows
    mine = place[0]
    start = pl.multiple_of(lax.rem(mine, spots) * rows, rows)
    picked = sketch[pl.ds(start, rows), :]
    picked = jnp.where(mine < spots, picked[:, :K], picked[:, K:])
    basis[...] = dot(picked, inverse, 1, 1, HIGHEST)
    coefficient = dot(inverse, gc[:, K:], 1, 0, HIGHEST)
    projected[...] = dot(inverse, coefficient, 0, 0, HIGHEST)


def per_device(left_points, left_ports, left_values, right_points, right_ports, right_values, sketch_block, sketch_weight):
    f32 = jnp.float32
    rows, rights = left_points.shape[0], right_points.shape[0]
    blk, wide = lax.axis_size("blk"), lax.axis_size("wide")
    along = (rights // LANES, LANES)
    left, right = kernel_call(
        pack_body,
        (
            jax.ShapeDtypeStruct((rows // 2 + SUB, LANES), f32),
            jax.ShapeDtypeStruct((rights // 2 + 4 * along[0], LANES), f32),
        ),
    )(
        left_points.reshape(1, rows),
        left_ports.reshape(1, rows),
        left_values,
        right_points.reshape(along),
        right_ports.reshape(along),
        right_values,
        sketch_block.reshape(along),
        sketch_weight.astype(f32).reshape(along),
    )
    rights_held = [right, swap(right, "blk", 1)]
    place = lax.axis_index("blk")
    lefts, steps = [left], []
    distance = 2
    while distance < blk:
        got = [swap(v, "blk", distance) for v in lefts]
        here = (place // distance) % 2 == 0
        lefts = [jnp.where(here, a, b) for a, b in zip(lefts, got)] + [jnp.where(here, b, a) for a, b in zip(lefts, got)]
        steps.append(distance)
        distance *= 2
    held = rows * len(lefts)
    pay, mu, hot = kernel_call(
        functools.partial(sketch_body, len(lefts), len(rights_held)),
        (
            jax.ShapeDtypeStruct((held // 2 + K // 2, LANES), f32),
            jax.ShapeDtypeStruct((held // 2, LANES), f32),
            jax.ShapeDtypeStruct((held // 2, LANES), f32),
        ),
    )(*lefts, *rights_held)
    for distance in steps[:-1]:
        pay = pay + swap(pay, "blk", distance)
    gc, sketch = kernel_call(
        moments_body,
        (jax.ShapeDtypeStruct((K, LANES), f32), jax.ShapeDtypeStruct((held // 2, LANES), f32)),
    )(pay, swap(pay, "blk", steps[-1]), mu, hot)
    hops = [("blk", 1)]
    distance = 2
    while distance < wide:
        hops.append(("wide", distance))
        distance *= 2
    for axis, distance in hops:
        gc = gc + swap(gc, axis, distance)
    basis, projected = kernel_call(
        functools.partial(finish_body, 1.0 / (rows * blk * wide)),
        (jax.ShapeDtypeStruct((rows, K), f32), jax.ShapeDtypeStruct((K, K), f32)),
        in_specs=[pl.BlockSpec(memory_space=pltpu.SMEM)] + [pl.BlockSpec(memory_space=pltpu.VMEM)] * 3,
    )(jnp.reshape(place // 2, (1,)), gc, swap(gc, "wide", 1), sketch)
    return basis, projected


def solution(mesh):
    split = P(("wide", "blk"))
    return jax.shard_map(
        per_device,
        mesh=mesh,
        in_specs=(split, split, P(("wide", "blk"), None), P("blk"), P("blk"), P("blk", None), P("blk"), P("blk")),
        out_specs=(P(("wide", "blk"), None), P()),
        check_vma=False,
    )
```

time: 441 us -> 52.3 us (0.12)
  matrix products: 114 us -> 0 us
  blocking collectives: 113 us -> 0 us
  local copies, waits for them, and re-layouts: 119 us -> 6.45 us
  loops' own time: 40.3 us -> 0 us
  other arithmetic: 18.2 us -> 2.67 us
  Pallas kernels: 0 us -> 14.3 us
  between operations: 14.2 us -> 0.66 us
  starting transfers between devices: 0.04 us -> 11.7 us
    dynamic_slice x192 -> x0, local copies, waits for them, and re-layouts: 115 us -> none  [the longest x128 76.2 us: row_step(): pivot = lax.dynamic_slice_in_dim(row_j, j, 1, 0)[0]]
    dot_general x198 -> x0, matrix products: 114 us -> none  [the longest x128 100 us: row_step(): jnp.dot(row_j, result, precision=lax.Precision.HIGHEST)]
    psum x2 -> x0, blocking collectives: 79.5 us -> none  [the longest x1 40.8 us: per_device(): coefficient = lax.psum(projection_local, ('wide', 'blk')) / row_total]
    another operation x3 -> x0, loops' own time: 40.3 us -> none  [the longest x1 40 us: cholesky_lower(): return lax.fori_loop(0, order, column_step, jnp.zeros_like(gram))]
    all_gather x3 -> x0, blocking collectives: 34 us -> none  [the longest x1 15.1 us: per_device(): lax.all_gather(left_wide, 'blk', axis=0, tiled=True)]
    reduce_scatter x1 -> x0, waiting for transfers between devices: 19.8 us -> none  [per_device(): lax.psum_scatter(jnp.concatenate([sketch_part, shift_part], axis=1), 'blk...]
    ppermute x0 -> x7, waiting for transfers between devices: none -> 16 us  [swap(): return lax.ppermute(value, axis, [(i, i ^ distance) for i in range(size)])]
    add x192 -> x3, other arithmetic: 15.2 us -> 0.78 us  [per_device(): gc = gc + swap(gc, axis, distance)]
  transfers between devices with their start and end apart: 1 -> 7, of which waited for: 1 -> 7; matrix products, arithmetic and copies ran while one was open for 0% -> 1% of each run, Pallas kernels for 0% -> 0%
where the time goes in v1:
time: 52.3 us; the launch traced here: 51.8 us
  waiting for transfers between devices  16 us (31%)
  Pallas kernels  14.3 us (27%)
  starting transfers between devices  11.7 us (22%)
  local copies, waits for them, and re-layouts  6.45 us (12%)
  other arithmetic  2.67 us (5%)
  between operations  0.66 us (1%)
    ppermute x7, waiting for transfers between devices, swap(): return lax.ppermute(value, axis, [(i, i ^ distance) for i in range(size)])  16 us
    ppermute x7, starting transfers between devices, swap(): return lax.ppermute(value, axis, [(i, i ^ distance) for i in range(size)])  11.7 us
    pallas_call x1, Pallas kernels, per_device(): kernel_call(functools.partial(finish_body, 1.0 / (rows * blk * wide)), (j...  7.22 us
    unnamed x12, local copies, waits for them, and re-layouts  4.92 us
    pallas_call x1, Pallas kernels, per_device(): kernel_call(functools.partial(sketch_body, len(lefts), len(rights_held)),...  3.08 us
    pallas_call x1, Pallas kernels, per_device(): kernel_call(moments_body, (jax.ShapeDtypeStruct((K, LANES), f32), jax.Sha...  2.35 us
    pallas_call x1, Pallas kernels, per_device(): kernel_call(pack_body, (jax.ShapeDtypeStruct((rows // 2 + SUB, LANES), f3...  1.69 us
    pallas_call x1, local copies, waits for them, and re-layouts, per_device(): kernel_call(functools.partial(finish_body, 1.0 / (rows * blk * wide)), (j...  1.54 us
  transfers between devices with their start and end apart: 7, of which 7 were waited for; matrix products, arithmetic and copies ran while one was open for 1% of the time, Pallas kernels for 0%

profile of v1, /device:TPU:0, one launch (start us, length us, event | category | flops | bytes accessed | tf_op | source)
XLA Modules:
  0.0 51.8 jit_solution(15513575188178620645)
XLA Ops:
  0.6 1.3 %bitcast_convert_fusion.w = f32[4,128]{1,0:T(4,128)} fusion(bf16[512]{0:T(512)(128)(2,1)} %param.15), kind=kLoop, calls=%fused_computation.2 | loop fusion | flops 512 | bytes 3072 | tf_op jit(solution)/shard_map/reshape | solution.py:195
  1.9 1.4 %copy.10.lv = bf16[128,64]{1,0:T(8,128)(2,1)} copy(bf16[128,64]{0,1:T(8,128)(2,1)} %param.10) | data formatting | bytes 32768 | tf_op args[2]
  3.3 1.6 %copy.11.rv = bf16[512,64]{1,0:T(8,128)(2,1)} copy(bf16[512,64]{0,1:T(8,128)(2,1)} %param.13) | data formatting | bytes 131072 | tf_op args[5]
  4.9 1.7 %shard_map.95 = (f32[72,128]{1,0:T(8,128)}, f32[272,128]{1,0:T(8,128)}) custom-call(f32[1,128]{1,0:T(1,128)} %bitcast.12, s32[1,128]{1,0:T(1,128)} %bitcast.13, bf16[128,64]{1,0:T(8,128)(2,1)} %copy.10.lv, f32[4,128]{1,0:T(4,128)} %bitcast.9, s32[4,128]{1,0:T(4,128)} %bitcast.10, bf16[512,64]{1,0:T(8,128)(2,1)} %copy.11.rv, s32[4,128]{1,0:T(4,128)} %bitcast.11, ...), custom_call_target="tpu_custom_call" | custom-call | tf_op jit(solution)/shard_map/pallas_call | solution.py:181
  6.6 0.0 copy-start.3
  6.6 4.1 %collective-permute-start = (f32[72,128]{1,0:T(8,128)}, f32[72,128]{1,0:T(8,128)S(1)}, u32[]{:S(2)}, u32[]{:S(2)}) collective-permute-start(f32[72,128]{1,0:T(8,128)} %get-tuple-element.9), channel_id=1, source_target_pairs={{0,2},{1,3},{2,0},{3,1},{4,6},{5,7},{6,4},{7,5},{8,10},{9,11},{10,... | collective-permute-start | bytes 110600 | tf_op jit(solution)/shard_map/ppermute | solution.py:18
  10.7 1.6 %collective-permute-start.1 = (f32[272,128]{1,0:T(8,128)}, f32[272,128]{1,0:T(8,128)S(1)}, u32[]{:S(2)}, u32[]{:S(2)}) collective-permute-start(f32[272,128]{1,0:T(8,128)} %get-tuple-element.10.refs_2_), channel_id=1, source_target_pairs={{0,1},{1,0},{2,3},{3,2},{4,5},{5,4},{6,7},{7,6},{8,9},{9,8},{10,11... | collective-permute-start | bytes 417800 | tf_op jit(solution)/shard_map/ppermute | solution.py:18
  12.2 1.1 %collective-permute-done = f32[72,128]{1,0:T(8,128)S(1)} collective-permute-done((f32[72,128]{1,0:T(8,128)}, f32[72,128]{1,0:T(8,128)S(1)}, u32[]{:S(2)}, u32[]{:S(2)}) %collective-permute-start) | collective-permute-done | bytes 36896 | tf_op jit(solution)/shard_map/ppermute | solution.py:18
  13.4 0.0 copy-done.3
  13.4 0.6 %broadcast_select_fusion = (f32[72,128]{1,0:T(8,128)}, f32[72,128]{1,0:T(8,128)}) fusion(f32[72,128]{1,0:T(8,128)S(1)} %collective-permute-done, f32[72,128]{1,0:T(8,128)S(1)} %copy-done.3, pred[]{:T(512)S(6)} %eq.5), kind=kLoop, calls=%fused_computation | loop fusion | flops 18432 | bytes 147457 | tf_op jit(solution)/shard_map/jit(_where)/select_n | solution.py:204
  14.0 2.1 %collective-permute-done.1.refs_3_ = f32[272,128]{1,0:T(8,128)S(1)} collective-permute-done((f32[272,128]{1,0:T(8,128)}, f32[272,128]{1,0:T(8,128)S(1)}, u32[]{:S(2)}, u32[]{:S(2)}) %collective-permute-start.1) | collective-permute-done | bytes 139296 | tf_op jit(solution)/shard_map/ppermute | solution.py:18
  16.1 0.0 copy-start
  16.1 0.7 %copy-done = f32[272,128]{1,0:T(8,128)} copy-done((f32[272,128]{1,0:T(8,128)}, f32[272,128]{1,0:T(8,128)S(1)}, u32[]{:S(2)}) %copy-start) | copy-done | bytes 139288
  16.8 3.1 %shard_map.96 = (f32[160,128]{1,0:T(8,128)}, f32[128,128]{1,0:T(8,128)}, f32[128,128]{1,0:T(8,128)}) custom-call(f32[72,128]{1,0:T(8,128)} %get-tuple-element.19.refs_0_, f32[72,128]{1,0:T(8,128)} %get-tuple-element.18.refs_1_, f32[272,128]{1,0:T(8,128)} %get-tuple-element.10.refs_2_, f32[272,128]{1,0:T(8,128)} %copy-done), custom_call_target="tpu_custom_call" | custom-call | tf_op jit(solution)/shard_map/pallas_call | solution.py:208
  19.9 0.8 %collective-permute-start.2 = (f32[160,128]{1,0:T(8,128)}, f32[160,128]{1,0:T(8,128)S(1)}, u32[]{:S(2)}, u32[]{:S(2)}) collective-permute-start(f32[160,128]{1,0:T(8,128)} %get-tuple-element.11.own), channel_id=1, source_target_pairs={{0,2},{1,3},{2,0},{3,1},{4,6},{5,7},{6,4},{7,5},{8,10},{9,11},{10,... | collective-permute-start | bytes 245768 | tf_op jit(solution)/shard_map/ppermute | solution.py:18
  20.7 4.7 %collective-permute-done.2.other = f32[160,128]{1,0:T(8,128)S(1)} collective-permute-done((f32[160,128]{1,0:T(8,128)}, f32[160,128]{1,0:T(8,128)S(1)}, u32[]{:S(2)}, u32[]{:S(2)}) %collective-permute-start.2) | collective-permute-done | bytes 81952 | tf_op jit(solution)/shard_map/ppermute | solution.py:18
  25.4 0.0 copy-start.2
  25.4 0.6 %copy-done.2 = f32[160,128]{1,0:T(8,128)} copy-done((f32[160,128]{1,0:T(8,128)}, f32[160,128]{1,0:T(8,128)S(1)}, u32[]{:S(2)}) %copy-start.2) | copy-done | bytes 81944
  26.1 2.3 %shard_map.97 = (f32[64,128]{1,0:T(8,128)}, f32[128,128]{1,0:T(8,128)}) custom-call(f32[160,128]{1,0:T(8,128)} %get-tuple-element.11.own, f32[160,128]{1,0:T(8,128)} %copy-done.2, f32[128,128]{1,0:T(8,128)} %get-tuple-element.12.mu, f32[128,128]{1,0:T(8,128)} %get-tuple-element.13.hot), custom_call_target="tpu_custom_call" | custom-call | tf_op jit(solution)/shard_map/pallas_call | solution.py:218
  28.4 1.7 %collective-permute-start.3 = (f32[64,128]{1,0:T(8,128)}, f32[64,128]{1,0:T(8,128)S(1)}, u32[]{:S(2)}, u32[]{:S(2)}) collective-permute-start(f32[64,128]{1,0:T(8,128)} %get-tuple-element.14), channel_id=1, source_target_pairs={{0,1},{1,0},{2,3},{3,2},{4,5},{5,4},{6,7},{7,6},{8,9},{9,8},{10,11... | collective-permute-start | bytes 98312 | tf_op jit(solution)/shard_map/ppermute | solution.py:18
  30.1 2.5 %collective-permute-done.3 = f32[64,128]{1,0:T(8,128)S(1)} collective-permute-done((f32[64,128]{1,0:T(8,128)}, f32[64,128]{1,0:T(8,128)S(1)}, u32[]{:S(2)}, u32[]{:S(2)}) %collective-permute-start.3) | collective-permute-done | bytes 32800 | tf_op jit(solution)/shard_map/ppermute | solution.py:18
  32.5 0.8 %add.15 = f32[64,128]{1,0:T(8,128)S(1)} add(f32[64,128]{1,0:T(8,128)} %get-tuple-element.14, f32[64,128]{1,0:T(8,128)S(1)} %collective-permute-done.3) | non-fusion elementwise | flops 8192 | bytes 98304 | tf_op jit(solution)/shard_map/add | solution.py:228
  33.3 1.7 %collective-permute-start.4 = (f32[64,128]{1,0:T(8,128)S(1)}, f32[64,128]{1,0:T(8,128)S(1)}, u32[]{:S(2)}, u32[]{:S(2)}) collective-permute-start(f32[64,128]{1,0:T(8,128)S(1)} %add.15), channel_id=1, source_target_pairs={{0,8},{4,12},{8,0},{12,4},{16,24},{20,28},{24,16},{28,20},{1,9},{5... | collective-permute-start | bytes 98312 | tf_op jit(solution)/shard_map/ppermute | solution.py:18
  35.0 2.2 %collective-permute-done.4 = f32[64,128]{1,0:T(8,128)S(1)} collective-permute-done((f32[64,128]{1,0:T(8,128)S(1)}, f32[64,128]{1,0:T(8,128)S(1)}, u32[]{:S(2)}, u32[]{:S(2)}) %collective-permute-start.4) | collective-permute-done | bytes 32800 | tf_op jit(solution)/shard_map/ppermute | solution.py:18
  37.2 1.8 %collective-permute-start.5 = (f32[64,128]{1,0:T(8,128)S(1)}, f32[64,128]{1,0:T(8,128)S(1)}, u32[]{:S(2)}, u32[]{:S(2)}) collective-permute-start(f32[64,128]{1,0:T(8,128)S(1)} %add.16), channel_id=1, source_target_pairs={{0,16},{4,20},{8,24},{12,28},{16,0},{20,4},{24,8},{28,12},{1,17},{... | collective-permute-start | bytes 98312 | tf_op jit(solution)/shard_map/ppermute | solution.py:18
  39.0 2.2 %collective-permute-done.5 = f32[64,128]{1,0:T(8,128)S(1)} collective-permute-done((f32[64,128]{1,0:T(8,128)S(1)}, f32[64,128]{1,0:T(8,128)S(1)}, u32[]{:S(2)}, u32[]{:S(2)}) %collective-permute-start.5) | collective-permute-done | bytes 32800 | tf_op jit(solution)/shard_map/ppermute | solution.py:18
  41.2 0.1 collective-permute-start.6
  41.2 1.2 %collective-permute-done.6.other = f32[64,128]{1,0:T(8,128)S(1)} collective-permute-done((f32[64,128]{1,0:T(8,128)S(1)}, f32[64,128]{1,0:T(8,128)S(1)}, u32[]{:S(2)}, u32[]{:S(2)}) %collective-permute-start.6) | collective-permute-done | bytes 32800 | tf_op jit(solution)/shard_map/ppermute | solution.py:18
  42.4 0.0 copy-done.1
  42.4 0.6 %copy-done.4 = f32[64,128]{1,0:T(8,128)} copy-done((f32[64,128]{1,0:T(8,128)}, f32[64,128]{1,0:T(8,128)S(1)}, u32[]{:S(2)}) %copy-start.4) | copy-done | bytes 32792
  43.0 7.2 %shard_map.98 = (f32[128,64]{1,0:T(8,128)}, f32[64,64]{1,0:T(8,128)}) custom-call(s32[1]{0:T(128)} %bitcast.place, f32[64,128]{1,0:T(8,128)} %copy-done.1, f32[64,128]{1,0:T(8,128)} %copy-done.4, f32[128,128]{1,0:T(8,128)} %get-tuple-element.15.sketch), custom_call_target="tpu_custom_call" | custom-call | tf_op jit(solution)/shard_map/pallas_call | solution.py:229
  50.3 1.5 %copy.12 = f32[128,64]{0,1:T(8,128)} copy(f32[128,64]{1,0:T(8,128)} %get-tuple-element.16) | data formatting | bytes 65536 | tf_op jit(solution)/shard_map/pallas_call | solution.py:229
  (4 shorter events, 0.0 us)
Async XLA Ops:
  6.6 6.8 %copy-start.3 = (f32[72,128]{1,0:T(8,128)S(1)}, f32[72,128]{1,0:T(8,128)}, u32[]{:S(2)}) copy-start(f32[72,128]{1,0:T(8,128)} %get-tuple-element.9) | copy-start | bytes 110596
  6.6 6.8 %collective-permute-start = (f32[72,128]{1,0:T(8,128)}, f32[72,128]{1,0:T(8,128)S(1)}, u32[]{:S(2)}, u32[]{:S(2)}) collective-permute-start(f32[72,128]{1,0:T(8,128)} %get-tuple-element.9), channel_id=1, source_target_pairs={{0,2},{1,3},{2,0},{3,1},{4,6},{5,7},{6,4},{7,5},{8,10},{9,11},{10,... | collective-permute-start | bytes 110600 | tf_op jit(solution)/shard_map/ppermute | solution.py:18
  10.7 5.5 %collective-permute-start.1 = (f32[272,128]{1,0:T(8,128)}, f32[272,128]{1,0:T(8,128)S(1)}, u32[]{:S(2)}, u32[]{:S(2)}) collective-permute-start(f32[272,128]{1,0:T(8,128)} %get-tuple-element.10.refs_2_), channel_id=1, source_target_pairs={{0,1},{1,0},{2,3},{3,2},{4,5},{5,4},{6,7},{7,6},{8,9},{9,8},{10,11... | collective-permute-start | bytes 417800 | tf_op jit(solution)/shard_map/ppermute | solution.py:18
  16.1 0.7 %copy-start = (f32[272,128]{1,0:T(8,128)}, f32[272,128]{1,0:T(8,128)S(1)}, u32[]{:S(2)}) copy-start(f32[272,128]{1,0:T(8,128)S(1)} %collective-permute-done.1.refs_3_) | copy-start | bytes 417796
  19.9 5.6 %collective-permute-start.2 = (f32[160,128]{1,0:T(8,128)}, f32[160,128]{1,0:T(8,128)S(1)}, u32[]{:S(2)}, u32[]{:S(2)}) collective-permute-start(f32[160,128]{1,0:T(8,128)} %get-tuple-element.11.own), channel_id=1, source_target_pairs={{0,2},{1,3},{2,0},{3,1},{4,6},{5,7},{6,4},{7,5},{8,10},{9,11},{10,... | collective-permute-start | bytes 245768 | tf_op jit(solution)/shard_map/ppermute | solution.py:18
  25.4 0.6 %copy-start.2 = (f32[160,128]{1,0:T(8,128)}, f32[160,128]{1,0:T(8,128)S(1)}, u32[]{:S(2)}) copy-start(f32[160,128]{1,0:T(8,128)S(1)} %collective-permute-done.2.other) | copy-start | bytes 245764
  28.4 4.1 %collective-permute-start.3 = (f32[64,128]{1,0:T(8,128)}, f32[64,128]{1,0:T(8,128)S(1)}, u32[]{:S(2)}, u32[]{:S(2)}) collective-permute-start(f32[64,128]{1,0:T(8,128)} %get-tuple-element.14), channel_id=1, source_target_pairs={{0,1},{1,0},{2,3},{3,2},{4,5},{5,4},{6,7},{7,6},{8,9},{9,8},{10,11... | collective-permute-start | bytes 98312 | tf_op jit(solution)/shard_map/ppermute | solution.py:18
  33.3 3.9 %collective-permute-start.4 = (f32[64,128]{1,0:T(8,128)S(1)}, f32[64,128]{1,0:T(8,128)S(1)}, u32[]{:S(2)}, u32[]{:S(2)}) collective-permute-start(f32[64,128]{1,0:T(8,128)S(1)} %add.15), channel_id=1, source_target_pairs={{0,8},{4,12},{8,0},{12,4},{16,24},{20,28},{24,16},{28,20},{1,9},{5... | collective-permute-start | bytes 98312 | tf_op jit(solution)/shard_map/ppermute | solution.py:18
  37.2 3.9 %collective-permute-start.5 = (f32[64,128]{1,0:T(8,128)S(1)}, f32[64,128]{1,0:T(8,128)S(1)}, u32[]{:S(2)}, u32[]{:S(2)}) collective-permute-start(f32[64,128]{1,0:T(8,128)S(1)} %add.16), channel_id=1, source_target_pairs={{0,16},{4,20},{8,24},{12,28},{16,0},{20,4},{24,8},{28,12},{1,17},{... | collective-permute-start | bytes 98312 | tf_op jit(solution)/shard_map/ppermute | solution.py:18
  41.2 1.3 %copy-start.1 = (f32[64,128]{1,0:T(8,128)}, f32[64,128]{1,0:T(8,128)S(1)}, u32[]{:S(2)}) copy-start(f32[64,128]{1,0:T(8,128)S(1)} %add.17.own) | copy-start | bytes 98308
  41.2 1.3 %collective-permute-start.6 = (f32[64,128]{1,0:T(8,128)S(1)}, f32[64,128]{1,0:T(8,128)S(1)}, u32[]{:S(2)}, u32[]{:S(2)}) collective-permute-start(f32[64,128]{1,0:T(8,128)S(1)} %add.17.own), channel_id=1, source_target_pairs={{0,4},{4,0},{8,12},{12,8},{16,20},{20,16},{24,28},{28,24},{1,5},{5... | collective-permute-start | bytes 98312 | tf_op jit(solution)/shard_map/ppermute | solution.py:18
  42.4 0.6 %copy-start.4 = (f32[64,128]{1,0:T(8,128)}, f32[64,128]{1,0:T(8,128)S(1)}, u32[]{:S(2)}) copy-start(f32[64,128]{1,0:T(8,128)S(1)} %collective-permute-done.6.other) | copy-start | bytes 98308

commit v2 on v1

v2 whole, which is shorter than its diff:
```python
import functools

import jax
import jax.numpy as jnp
from jax import lax
from jax.experimental import pallas as pl
from jax.experimental.pallas import tpu as pltpu
from jax.sharding import PartitionSpec as P

K = 64
LANES = 128
SUB = 8
HIGHEST = lax.Precision.HIGHEST
VMEM_LIMIT = 8 << 20


def swap(value, axis, distance):
    size = lax.axis_size(axis)
    return lax.ppermute(value, axis, [(i, i ^ distance) for i in range(size)])


def kernel_call(body, out_shape, operands, limit=VMEM_LIMIT, **kw):
    return pl.pallas_call(
        body, out_shape=out_shape, compiler_params=pltpu.CompilerParams(vmem_limit_bytes=limit), **kw
    )(*operands)


def pieces(value, count=3):
    out = []
    for _ in range(count - 1):
        top = value.astype(jnp.bfloat16)
        out.append(top)
        value = value - top.astype(jnp.float32)
    out.append(value.astype(jnp.bfloat16))
    return out


def dot(a, b, ca, cb, precision=None):
    return lax.dot_general(
        a, b, (((ca,), (cb,)), ((), ())), precision=precision, preferred_element_type=jnp.float32
    )


def pack_body(mu, lp, lv, lam, rp, rv, col, w, left, right):
    left[:K, :] = lv[...].astype(jnp.float32)
    left[K : K + 1, :] = mu[...]
    left[K + 1 : K + 2, :] = lp[...].astype(jnp.float32)
    left[K + 2 :, :] = jnp.zeros((left.shape[0] - K - 2, LANES), jnp.float32)
    right[:K, :] = rv[...].astype(jnp.float32)
    weights = w[...].astype(jnp.float32)
    for s in range(lam.shape[0]):
        lanes = pl.ds(s * LANES, LANES)
        right[K : K + 1, lanes] = lam[s : s + 1, :]
        right[K + 1 : K + 2, lanes] = rp[s : s + 1, :].astype(jnp.float32)
        right[K + 2 : K + 3, lanes] = col[s : s + 1, :].astype(jnp.float32)
        right[K + 3 : K + 4, lanes] = weights[s : s + 1, :]
    right[K + 4 :, :] = jnp.zeros((right.shape[0] - K - 4, right.shape[1]), jnp.float32)


def in_order(lefts, distance):
    half = len(lefts) // 2
    here = lax.rem(lax.div(lax.axis_index("blk"), distance), 2) == 0
    own, got = [ref[...] for ref in lefts[:half]], [ref[...] for ref in lefts[half:]]
    return [jnp.where(here, a, b) for a, b in zip(own, got)] + [jnp.where(here, b, a) for a, b in zip(own, got)]


def sketch_body(n_left, distance, *refs):
    lefts, rights, (pay, freq, ports) = in_order(refs[:n_left], distance), refs[n_left:-3], refs[-3:]
    index = lax.broadcasted_iota(jnp.int32, (K, LANES), 0).astype(jnp.float32)
    mus, sides = [], []
    for q, left in enumerate(lefts):
        mu, port = left[K : K + 1, :], left[K + 1 : K + 2, :]
        freq[q : q + 1, :] = mu
        ports[q : q + 1, :] = port
        mus.append(jnp.broadcast_to(mu, (LANES, LANES)).T)
        sides.append(jnp.concatenate([left[:K, :], jnp.where(port == index, -1.0, 0.0)], axis=0).T.astype(jnp.bfloat16))
    side = jnp.concatenate(sides, axis=0)
    rows = side.shape[0]
    total = jnp.zeros((rows, K), jnp.float32)
    cross = jnp.zeros((K, K), jnp.float32)
    for right in rights:
        width = right.shape[1]
        index = lax.broadcasted_iota(jnp.int32, (K, width), 0).astype(jnp.float32)
        values = right[:K, :].astype(jnp.bfloat16)
        lam = right[K : K + 1, :]
        pick = jnp.where(right[K + 1 : K + 2, :] == index, 1.0, 0.0).astype(jnp.bfloat16)
        omega = jnp.where(right[K + 2 : K + 3, :] == index, right[K + 3 : K + 4, :], 0.0).astype(jnp.bfloat16)
        upper = dot(side, jnp.concatenate([pick, values], axis=0), 1, 0)
        scale = jnp.concatenate([jnp.concatenate([m] * (width // LANES), axis=1) for m in mus], axis=0) - lam
        loewner = upper / scale
        for piece in pieces(loewner):
            total = total + dot(piece, omega, 1, 1)
        cross = cross + dot(omega, values, 1, 1)
    for q in range(n_left):
        pay[q * K : (q + 1) * K, :] = total[q * LANES : (q + 1) * LANES, :].T
    pay[n_left * K :, :] = jnp.concatenate([cross[: K // 2], cross[K // 2 :]], axis=1)


def moments_body(own, other, freq, ports, gc, full):
    n_left = freq.shape[0]
    both = own[...] + other[...]
    index = lax.broadcasted_iota(jnp.int32, (K, LANES), 0).astype(jnp.float32)
    cross = both[n_left * K :, :]
    cross = pieces(jnp.concatenate([cross[:, :K], cross[:, K:]], axis=0))
    sketches, shifts = [], []
    for q in range(n_left):
        sketch = both[q * K : (q + 1) * K, :]
        hot = jnp.where(ports[q : q + 1, :] == index, 1.0, 0.0).astype(jnp.bfloat16)
        shift = freq[q : q + 1, :] * sketch
        for piece in cross:
            shift = shift + dot(piece, hot, 1, 0)
        sketches.append(sketch)
        shifts.append(shift)
    sketch = jnp.concatenate(sketches, axis=1)
    gc[...] = dot(sketch, jnp.concatenate([sketch, jnp.concatenate(shifts, axis=1)], axis=0), 1, 1, HIGHEST)
    full[...] = both[: n_left * K, :]


def finish_body(scale, own, other, sketch, basis, projected):
    gc = (own[...] + other[...]) * scale
    lane = lax.broadcasted_iota(jnp.int32, (SUB, LANES), 1)
    sub = lax.broadcasted_iota(jnp.int32, (SUB, LANES), 0)
    blocks = []
    for r in range(K // SUB):
        blocks.append(
            jnp.where(lane < K, gc[r * SUB : (r + 1) * SUB, :], jnp.where(lane == sub + (K + r * SUB), 1.0, 0.0))
        )
    for j in range(K):
        r, s = divmod(j, SUB)
        row = blocks[r][s : s + 1, :]
        row = row / row[:, j : j + 1]
        for q in range(r, K // SUB):
            factor = blocks[q][:, j : j + 1]
            if q == r:
                if s == SUB - 1:
                    continue
                factor = jnp.where(sub[:, :1] > s, factor, 0.0)
            blocks[q] = blocks[q] - factor * row
    done = []
    for r in range(K // SUB):
        pivot = jnp.sum(jnp.where(lane == sub + r * SUB, blocks[r], 0.0), axis=1, keepdims=True)
        done.append(blocks[r][:, K:] / jnp.sqrt(pivot))
    inverse = jnp.concatenate(done, axis=0)
    mine = pl.multiple_of(lax.div(lax.axis_index("blk"), 2) * K, K)
    basis[...] = dot(inverse, sketch[pl.ds(mine, K), :], 1, 0, HIGHEST)
    coefficient = dot(inverse, gc[:, K:], 1, 0, HIGHEST)
    projected[...] = dot(inverse, coefficient, 0, 0, HIGHEST)


def per_device(left_points, left_ports, left_values, right_points, right_ports, right_values, sketch_block, sketch_weight):
    f32 = jnp.float32
    rows, rights = left_points.shape[0], right_points.shape[0]
    blk, wide = lax.axis_size("blk"), lax.axis_size("wide")
    along = (rights // LANES, LANES)
    left, right = kernel_call(
        pack_body,
        (jax.ShapeDtypeStruct((K + SUB, LANES), f32), jax.ShapeDtypeStruct((K + SUB, rights), f32)),
        (
            left_points.reshape(1, rows),
            left_ports.reshape(1, rows),
            left_values.T,
            right_points.reshape(along),
            right_ports.reshape(along),
            right_values.T,
            sketch_block.reshape(along),
            sketch_weight.reshape(along),
        ),
    )
    place = lax.axis_index("blk")
    lefts, distance = [left], 2
    while True:
        got = [swap(v, "blk", distance) for v in lefts]
        if distance * 2 >= blk:
            break
        here = (place // distance) % 2 == 0
        lefts = [jnp.where(here, a, b) for a, b in zip(lefts, got)] + [jnp.where(here, b, a) for a, b in zip(lefts, got)]
        distance *= 2
    lefts = lefts + got
    rights_held = [right, swap(right, "blk", 1)]
    held = len(lefts)
    pay, freq, ports = kernel_call(
        functools.partial(sketch_body, held, distance),
        (
            jax.ShapeDtypeStruct((held * K + K // 2, LANES), f32),
            jax.ShapeDtypeStruct((held, LANES), f32),
            jax.ShapeDtypeStruct((held, LANES), f32),
        ),
        (*lefts, *rights_held),
        limit=max(VMEM_LIMIT, held * VMEM_LIMIT // 2),
    )
    step = 2
    while step < distance:
        pay = pay + swap(pay, "blk", step)
        step *= 2
    gc, sketch = kernel_call(
        moments_body,
        (jax.ShapeDtypeStruct((K, LANES), f32), jax.ShapeDtypeStruct((held * K, LANES), f32)),
        (pay, swap(pay, "blk", distance), freq, ports),
    )
    hops = [("blk", 1)]
    distance = 2
    while distance < wide:
        hops.append(("wide", distance))
        distance *= 2
    for axis, distance in hops:
        gc = gc + swap(gc, axis, distance)
    basis, projected = kernel_call(
        functools.partial(finish_body, 1.0 / (rows * blk * wide)),
        (jax.ShapeDtypeStruct((K, rows), f32), jax.ShapeDtypeStruct((K, K), f32)),
        (gc, swap(gc, "wide", 1), sketch),
    )
    return basis.T, projected


def solution(mesh):
    split = P(("wide", "blk"))
    return jax.shard_map(
        per_device,
        mesh=mesh,
        in_specs=(split, split, P(("wide", "blk"), None), P("blk"), P("blk"), P("blk", None), P("blk"), P("blk")),
        out_specs=(P(("wide", "blk"), None), P()),
        check_vma=False,
    )
```

time: 52.3 us -> 38.2 us (0.73)
  Pallas kernels: 14.3 us -> 8 us
  local copies, waits for them, and re-layouts: 6.45 us -> 2.25 us
  other arithmetic: 2.67 us -> 0.02 us
  waiting for transfers between devices: 16 us -> 13.5 us
  starting transfers between devices: 11.7 us -> 13.4 us
    pallas_call x4, Pallas kernels: 14.3 us -> 8 us  [kernel_call(): pl.pallas_call(body, out_shape=out_shape, compiler_params=pltpu.CompilerP...]
    unnamed x12 -> x16, local copies, waits for them, and re-layouts: 4.92 us -> 2.25 us
    ppermute x7, waiting for transfers between devices: 16 us -> 13.5 us  [swap(): return lax.ppermute(value, axis, [(i, i ^ distance) for i in range(size)])]
    ppermute x7, starting transfers between devices: 11.7 us -> 13.4 us  [swap(): return lax.ppermute(value, axis, [(i, i ^ distance) for i in range(size)])]
    pallas_call x1 -> x0, local copies, waits for them, and re-layouts: 1.54 us -> none  [per_device(): kernel_call(functools.partial(finish_body, 1.0 / (rows * blk * wide)), (j...]
    reshape x1 -> x0, other arithmetic: 1.26 us -> none  [per_device(): sketch_weight.astype(f32).reshape(along)]
    add x3, other arithmetic: 0.78 us -> 0.02 us  [per_device(): gc = gc + swap(gc, axis, distance)]
    select_n x1 -> x0, other arithmetic: 0.63 us -> none  [per_device(): jnp.where(here, b, a)]
  transfers between devices with their start and end apart: 7 -> 7, of which waited for: 7 -> 6; matrix products, arithmetic and copies ran while one was open for 1% -> 0% of each run, Pallas kernels for 0% -> 0%
where the time goes in v2:
time: 38.2 us; the launch traced here: 37.9 us
  waiting for transfers between devices  13.5 us (35%)
  starting transfers between devices  13.4 us (35%)
  Pallas kernels  8 us (21%)
  local copies, waits for them, and re-layouts  2.25 us (6%)
  between operations  0.7 us (2%)
    ppermute x7, waiting for transfers between devices, swap(): return lax.ppermute(value, axis, [(i, i ^ distance) for i in range(size)])  13.5 us
    ppermute x7, starting transfers between devices, swap(): return lax.ppermute(value, axis, [(i, i ^ distance) for i in range(size)])  13.4 us
    pallas_call x4, Pallas kernels, kernel_call(): pl.pallas_call(body, out_shape=out_shape, compiler_params=pltpu.CompilerP...  8 us
    unnamed x16, local copies, waits for them, and re-layouts  2.25 us
  transfers between devices with their start and end apart: 7, of which 6 were waited for; matrix products, arithmetic and copies ran while one was open for 0% of the time, Pallas kernels for 0%

profile of v2, /device:TPU:0, one launch (start us, length us, event | category | flops | bytes accessed | tf_op | source)
XLA Modules:
  0.0 37.9 jit_solution(10485830386716499097)
XLA Ops:
  0.6 0.0 copy-start.7
  0.6 0.0 copy-start.4
  0.7 0.0 copy-start.3
  0.7 0.0 copy-start.2
  0.7 0.0 copy-start.5
  0.7 0.0 copy-start.6
  0.7 0.6 %copy-done.7 = s32[128]{0:T(128)S(1)} copy-done((s32[128]{0:T(128)S(1)}, s32[128]{0:T(128)}, u32[]{:S(2)}) %copy-start.7) | copy-done | bytes 536
  1.3 0.0 copy-done.4
  1.3 0.0 copy-done.3
  1.3 0.0 copy-done.2
  1.4 0.0 copy-done.5
  1.4 0.0 copy-done.6
  1.4 0.0 copy-start
  1.4 0.8 %copy-done = bf16[512,64]{0,1:T(8,128)(2,1)S(1)} copy-done((bf16[512,64]{0,1:T(8,128)(2,1)S(1)}, bf16[512,64]{0,1:T(8,128)(2,1)}, u32[]{:S(2)}) %copy-start) | copy-done | bytes 65560
  2.2 0.7 %copy-done.1 = bf16[128,64]{0,1:T(8,128)(2,1)S(1)} copy-done((bf16[128,64]{0,1:T(8,128)(2,1)S(1)}, bf16[128,64]{0,1:T(8,128)(2,1)}, u32[]{:S(2)}) %copy-start.1) | copy-done | bytes 16408
  3.0 3.1 %collective-permute-start.1 = (f32[72,512]{1,0:T(8,128)S(1)}, f32[72,512]{1,0:T(8,128)S(1)}, u32[]{:S(2)}, u32[]{:S(2)}) collective-permute-start(f32[72,512]{1,0:T(8,128)S(1)} %get-tuple-element.12.refs_2_), channel_id=1, source_target_pairs={{0,1},{1,0},{2,3},{3,2},{4,5},{5,4},{6,7},{7,6},{8,9},{9,8},{10,11... | collective-permute-start | bytes 442376 | tf_op jit(solution)/shard_map/ppermute | solution.py:19
  6.1 2.6 %collective-permute-start = (f32[72,128]{1,0:T(8,128)S(1)}, f32[72,128]{1,0:T(8,128)S(1)}, u32[]{:S(2)}, u32[]{:S(2)}) collective-permute-start(f32[72,128]{1,0:T(8,128)S(1)} %get-tuple-element.11.refs_0_), channel_id=1, source_target_pairs={{0,2},{1,3},{2,0},{3,1},{4,6},{5,7},{6,4},{7,5},{8,10},{9,11},{10,... | collective-permute-start | bytes 110600 | tf_op jit(solution)/shard_map/ppermute | solution.py:19
  8.7 2.3 %collective-permute-done.refs_1_ = f32[72,128]{1,0:T(8,128)S(1)} collective-permute-done((f32[72,128]{1,0:T(8,128)S(1)}, f32[72,128]{1,0:T(8,128)S(1)}, u32[]{:S(2)}, u32[]{:S(2)}) %collective-permute-start) | collective-permute-done | bytes 36896 | tf_op jit(solution)/shard_map/ppermute | solution.py:19
  10.9 0.0 collective-permute-done.1.refs_3_
  10.9 1.2 %shard_map.96 = (f32[160,128]{1,0:T(8,128)S(1)}, f32[2,128]{1,0:T(2,128)S(1)}, f32[2,128]{1,0:T(2,128)S(1)}) custom-call(f32[72,128]{1,0:T(8,128)S(1)} %get-tuple-element.11.refs_0_, f32[72,128]{1,0:T(8,128)S(1)} %collective-permute-done.refs_1_, f32[72,512]{1,0:T(8,128)S(1)} %get-tuple-element.12.refs_2_, f32[72,512]{1,0:T(8,128)S(1)} %collective-permute-done.1.refs_3_), custom_call_target="tpu_custom_call" | custom-call | tf_op jit(solution)/shard_map/pallas_call | solution.py:23
  12.1 2.6 %collective-permute-start.2 = (f32[160,128]{1,0:T(8,128)S(1)}, f32[160,128]{1,0:T(8,128)S(1)}, u32[]{:S(2)}, u32[]{:S(2)}) collective-permute-start(f32[160,128]{1,0:T(8,128)S(1)} %get-tuple-element.13.own), channel_id=1, source_target_pairs={{0,2},{1,3},{2,0},{3,1},{4,6},{5,7},{6,4},{7,5},{8,10},{9,11},{10,... | collective-permute-start | bytes 245768 | tf_op jit(solution)/shard_map/ppermute | solution.py:19
  14.7 3.3 %collective-permute-done.2.other = f32[160,128]{1,0:T(8,128)S(1)} collective-permute-done((f32[160,128]{1,0:T(8,128)S(1)}, f32[160,128]{1,0:T(8,128)S(1)}, u32[]{:S(2)}, u32[]{:S(2)}) %collective-permute-start.2) | collective-permute-done | bytes 81952 | tf_op jit(solution)/shard_map/ppermute | solution.py:19
  18.1 0.5 %shard_map.97 = (f32[64,128]{1,0:T(8,128)S(1)}, f32[128,128]{1,0:T(8,128)S(1)}) custom-call(f32[160,128]{1,0:T(8,128)S(1)} %get-tuple-element.13.own, f32[160,128]{1,0:T(8,128)S(1)} %collective-permute-done.2.other, f32[2,128]{1,0:T(2,128)S(1)} %get-tuple-element.14.freq, f32[2,128]{1,0:T(2,128)S(1)} %get-tuple-element.15.ports), custom_call_target="tpu_custom_call" | custom-call | tf_op jit(solution)/shard_map/pallas_call | solution.py:23
  18.5 2.0 %collective-permute-start.3 = (f32[64,128]{1,0:T(8,128)S(1)}, f32[64,128]{1,0:T(8,128)S(1)}, u32[]{:S(2)}, u32[]{:S(2)}) collective-permute-start(f32[64,128]{1,0:T(8,128)S(1)} %get-tuple-element.16), channel_id=1, source_target_pairs={{0,1},{1,0},{2,3},{3,2},{4,5},{5,4},{6,7},{7,6},{8,9},{9,8},{10,11... | collective-permute-start | bytes 98312 | tf_op jit(solution)/shard_map/ppermute | solution.py:19
  20.6 1.9 %collective-permute-done.3 = f32[64,128]{1,0:T(8,128)S(1)} collective-permute-done((f32[64,128]{1,0:T(8,128)S(1)}, f32[64,128]{1,0:T(8,128)S(1)}, u32[]{:S(2)}, u32[]{:S(2)}) %collective-permute-start.3) | collective-permute-done | bytes 32800 | tf_op jit(solution)/shard_map/ppermute | solution.py:19
  22.5 1.5 %collective-permute-start.4 = (f32[64,128]{1,0:T(8,128)S(1)}, f32[64,128]{1,0:T(8,128)S(1)}, u32[]{:S(2)}, u32[]{:S(2)}) collective-permute-start(f32[64,128]{1,0:T(8,128)S(1)} %add.9), channel_id=1, source_target_pairs={{0,8},{4,12},{8,0},{12,4},{16,24},{20,28},{24,16},{28,20},{1,9},{5... | collective-permute-start | bytes 98312 | tf_op jit(solution)/shard_map/ppermute | solution.py:19
  24.0 2.4 %collective-permute-done.4 = f32[64,128]{1,0:T(8,128)S(1)} collective-permute-done((f32[64,128]{1,0:T(8,128)S(1)}, f32[64,128]{1,0:T(8,128)S(1)}, u32[]{:S(2)}, u32[]{:S(2)}) %collective-permute-start.4) | collective-permute-done | bytes 32800 | tf_op jit(solution)/shard_map/ppermute | solution.py:19
  26.4 1.5 %collective-permute-start.5 = (f32[64,128]{1,0:T(8,128)S(1)}, f32[64,128]{1,0:T(8,128)S(1)}, u32[]{:S(2)}, u32[]{:S(2)}) collective-permute-start(f32[64,128]{1,0:T(8,128)S(1)} %add.10), channel_id=1, source_target_pairs={{0,16},{4,20},{8,24},{12,28},{16,0},{20,4},{24,8},{28,12},{1,17},{... | collective-permute-start | bytes 98312 | tf_op jit(solution)/shard_map/ppermute | solution.py:19
  27.9 2.4 %collective-permute-done.5 = f32[64,128]{1,0:T(8,128)S(1)} collective-permute-done((f32[64,128]{1,0:T(8,128)S(1)}, f32[64,128]{1,0:T(8,128)S(1)}, u32[]{:S(2)}, u32[]{:S(2)}) %collective-permute-start.5) | collective-permute-done | bytes 32800 | tf_op jit(solution)/shard_map/ppermute | solution.py:19
  30.3 0.0 collective-permute-start.6
  30.4 1.2 %collective-permute-done.6.other = f32[64,128]{1,0:T(8,128)S(1)} collective-permute-done((f32[64,128]{1,0:T(8,128)S(1)}, f32[64,128]{1,0:T(8,128)S(1)}, u32[]{:S(2)}, u32[]{:S(2)}) %collective-permute-start.6) | collective-permute-done | bytes 32800 | tf_op jit(solution)/shard_map/ppermute | solution.py:19
  31.6 6.4 %shard_map.98 = (f32[64,128]{1,0:T(8,128)}, f32[64,64]{1,0:T(8,128)}) custom-call(f32[64,128]{1,0:T(8,128)S(1)} %add.11.own, f32[64,128]{1,0:T(8,128)S(1)} %collective-permute-done.6.other, f32[128,128]{1,0:T(8,128)S(1)} %get-tuple-element.17.sketch), custom_call_target="tpu_custom_call" | custom-call | tf_op jit(solution)/shard_map/pallas_call | solution.py:23
  (5 shorter events, 0.0 us)
Async XLA Ops:
  0.6 0.7 %copy-start.7 = (s32[128]{0:T(128)S(1)}, s32[128]{0:T(128)}, u32[]{:S(2)}) copy-start(s32[128]{0:T(128)} %param.9) | copy-start | bytes 1540
  0.6 0.7 %copy-start.4 = (s32[512]{0:T(512)S(1)}, s32[512]{0:T(512)}, u32[]{:S(2)}) copy-start(s32[512]{0:T(512)} %param.14) | copy-start | bytes 6148
  0.7 0.7 %copy-start.3 = (s32[512]{0:T(512)S(1)}, s32[512]{0:T(512)}, u32[]{:S(2)}) copy-start(s32[512]{0:T(512)} %param.12) | copy-start | bytes 6148
  0.7 0.7 %copy-start.2 = (f32[512]{0:T(512)S(1)}, f32[512]{0:T(512)}, u32[]{:S(2)}) copy-start(f32[512]{0:T(512)} %param.11) | copy-start | bytes 6148
  0.7 0.7 %copy-start.5 = (bf16[512]{0:T(512)(128)(2,1)S(1)}, bf16[512]{0:T(512)(128)(2,1)}, u32[]{:S(2)}) copy-start(bf16[512]{0:T(512)(128)(2,1)} %param.15) | copy-start | bytes 3076
  0.7 0.7 %copy-start.6 = (f32[128]{0:T(128)S(1)}, f32[128]{0:T(128)}, u32[]{:S(2)}) copy-start(f32[128]{0:T(128)} %param.8) | copy-start | bytes 1540
  1.4 0.8 %copy-start = (bf16[512,64]{0,1:T(8,128)(2,1)S(1)}, bf16[512,64]{0,1:T(8,128)(2,1)}, u32[]{:S(2)}) copy-start(bf16[512,64]{0,1:T(8,128)(2,1)} %param.13) | copy-start | bytes 196612
  2.2 0.7 %copy-start.1 = (bf16[128,64]{0,1:T(8,128)(2,1)S(1)}, bf16[128,64]{0,1:T(8,128)(2,1)}, u32[]{:S(2)}) copy-start(bf16[128,64]{0,1:T(8,128)(2,1)} %param.10) | copy-start | bytes 49156
  3.0 8.0 %collective-permute-start.1 = (f32[72,512]{1,0:T(8,128)S(1)}, f32[72,512]{1,0:T(8,128)S(1)}, u32[]{:S(2)}, u32[]{:S(2)}) collective-permute-start(f32[72,512]{1,0:T(8,128)S(1)} %get-tuple-element.12.refs_2_), channel_id=1, source_target_pairs={{0,1},{1,0},{2,3},{3,2},{4,5},{5,4},{6,7},{7,6},{8,9},{9,8},{10,11... | collective-permute-start | bytes 442376 | tf_op jit(solution)/shard_map/ppermute | solution.py:19
  6.1 4.9 %collective-permute-start = (f32[72,128]{1,0:T(8,128)S(1)}, f32[72,128]{1,0:T(8,128)S(1)}, u32[]{:S(2)}, u32[]{:S(2)}) collective-permute-start(f32[72,128]{1,0:T(8,128)S(1)} %get-tuple-element.11.refs_0_), channel_id=1, source_target_pairs={{0,2},{1,3},{2,0},{3,1},{4,6},{5,7},{6,4},{7,5},{8,10},{9,11},{10,... | collective-permute-start | bytes 110600 | tf_op jit(solution)/shard_map/ppermute | solution.py:19
  12.1 6.0 %collective-permute-start.2 = (f32[160,128]{1,0:T(8,128)S(1)}, f32[160,128]{1,0:T(8,128)S(1)}, u32[]{:S(2)}, u32[]{:S(2)}) collective-permute-start(f32[160,128]{1,0:T(8,128)S(1)} %get-tuple-element.13.own), channel_id=1, source_target_pairs={{0,2},{1,3},{2,0},{3,1},{4,6},{5,7},{6,4},{7,5},{8,10},{9,11},{10,... | collective-permute-start | bytes 245768 | tf_op jit(solution)/shard_map/ppermute | solution.py:19
  18.5 4.0 %collective-permute-start.3 = (f32[64,128]{1,0:T(8,128)S(1)}, f32[64,128]{1,0:T(8,128)S(1)}, u32[]{:S(2)}, u32[]{:S(2)}) collective-permute-start(f32[64,128]{1,0:T(8,128)S(1)} %get-tuple-element.16), channel_id=1, source_target_pairs={{0,1},{1,0},{2,3},{3,2},{4,5},{5,4},{6,7},{7,6},{8,9},{9,8},{10,11... | collective-permute-start | bytes 98312 | tf_op jit(solution)/shard_map/ppermute | solution.py:19
  22.5 3.9 %collective-permute-start.4 = (f32[64,128]{1,0:T(8,128)S(1)}, f32[64,128]{1,0:T(8,128)S(1)}, u32[]{:S(2)}, u32[]{:S(2)}) collective-permute-start(f32[64,128]{1,0:T(8,128)S(1)} %add.9), channel_id=1, source_target_pairs={{0,8},{4,12},{8,0},{12,4},{16,24},{20,28},{24,16},{28,20},{1,9},{5... | collective-permute-start | bytes 98312 | tf_op jit(solution)/shard_map/ppermute | solution.py:19
  26.4 3.9 %collective-permute-start.5 = (f32[64,128]{1,0:T(8,128)S(1)}, f32[64,128]{1,0:T(8,128)S(1)}, u32[]{:S(2)}, u32[]{:S(2)}) collective-permute-start(f32[64,128]{1,0:T(8,128)S(1)} %add.10), channel_id=1, source_target_pairs={{0,16},{4,20},{8,24},{12,28},{16,0},{20,4},{24,8},{28,12},{1,17},{... | collective-permute-start | bytes 98312 | tf_op jit(solution)/shard_map/ppermute | solution.py:19
  30.3 1.2 %collective-permute-start.6 = (f32[64,128]{1,0:T(8,128)S(1)}, f32[64,128]{1,0:T(8,128)S(1)}, u32[]{:S(2)}, u32[]{:S(2)}) collective-permute-start(f32[64,128]{1,0:T(8,128)S(1)} %add.11.own), channel_id=1, source_target_pairs={{0,4},{4,0},{8,12},{12,8},{16,20},{20,16},{24,28},{28,24},{1,5},{5... | collective-permute-start | bytes 98312 | tf_op jit(solution)/shard_map/ppermute | solution.py:19

commit v3 on v2

--- a/solution.py
+++ b/solution.py
@@ -14,9 +14,10 @@
 VMEM_LIMIT = 8 << 20
 
 
-def swap(value, axis, distance):
-    size = lax.axis_size(axis)
-    return lax.ppermute(value, axis, [(i, i ^ distance) for i in range(size)])
+def swap(value, blk=0, wide=0):
+    wides, blks = lax.axis_size("wide"), lax.axis_size("blk")
+    pairs = [(w * blks + b, (w ^ wide) * blks + (b ^ blk)) for w in range(wides) for b in range(blks)]
+    return lax.ppermute(value, ("wide", "blk"), pairs)
 
 
 def kernel_call(body, out_shape, operands, limit=VMEM_LIMIT, **kw):
@@ -41,11 +42,19 @@
     )
 
 
-def pack_body(mu, lp, lv, lam, rp, rv, col, w, left, right):
+def pack_body(*refs):
+    sources, (left, right), held, sems = refs[:8], refs[8:10], refs[10:18], refs[18]
+    copies = [pltpu.make_async_copy(a, b, sems.at[i]) for i, (a, b) in enumerate(zip(sources, held))]
+    for copy in copies:
+        copy.start()
+    mu, lp, lv, lam, rp, rv, col, w = held
+    left[K + 2 :, :] = jnp.zeros((left.shape[0] - K - 2, LANES), jnp.float32)
+    right[K + 4 :, :] = jnp.zeros((right.shape[0] - K - 4, right.shape[1]), jnp.float32)
+    for copy in copies:
+        copy.wait()
     left[:K, :] = lv[...].astype(jnp.float32)
     left[K : K + 1, :] = mu[...]
     left[K + 1 : K + 2, :] = lp[...].astype(jnp.float32)
-    left[K + 2 :, :] = jnp.zeros((left.shape[0] - K - 2, LANES), jnp.float32)
     right[:K, :] = rv[...].astype(jnp.float32)
     weights = w[...].astype(jnp.float32)
     for s in range(lam.shape[0]):
@@ -54,7 +63,6 @@
         right[K + 1 : K + 2, lanes] = rp[s : s + 1, :].astype(jnp.float32)
         right[K + 2 : K + 3, lanes] = col[s : s + 1, :].astype(jnp.float32)
         right[K + 3 : K + 4, lanes] = weights[s : s + 1, :]
-    right[K + 4 :, :] = jnp.zeros((right.shape[0] - K - 4, right.shape[1]), jnp.float32)
 
 
 def in_order(lefts, distance):
@@ -116,31 +124,52 @@
     full[...] = both[: n_left * K, :]
 
 
+def full(value):
+    return jnp.broadcast_to(value, (SUB, LANES))
+
+
+def inverse_factor(gram):
+    lane = lax.broadcasted_iota(jnp.int32, (SUB, LANES), 1)
+    sub = lax.broadcasted_iota(jnp.int32, (SUB, LANES), 0)
+    count = K // SUB
+    blocks = [
+        jnp.where(lane < K, gram[r * SUB : (r + 1) * SUB, :], jnp.where(lane == sub + (K + r * SUB), 1.0, 0.0))
+        for r in range(count)
+    ]
+    out = []
+    for r in range(count):
+        here, first = blocks[r], r * SUB
+        below = range(r + 1, count)
+        rows = [full(here[t : t + 1, :]) for t in range(SUB)]
+        part = {(t, u): full(here[t : t + 1, first + u : first + u + 1]) for t in range(SUB) for u in range(t + 1)}
+        cols = {q: [full(blocks[q][:, first + u : first + u + 1]) for u in range(SUB)] for q in below}
+        inverse = []
+        for u in range(SUB):
+            inverse.append(1.0 / part[u, u])
+            ratio = {t: part[t, u] * inverse[u] for t in range(u + 1, SUB)}
+            for t in range(u + 1, SUB):
+                for v in range(u + 1, t + 1):
+                    part[t, v] = part[t, v] - (part[t, u] * part[v, u]) * inverse[u]
+            for t in range(u + 1, SUB):
+                rows[t] = rows[t] - ratio[t] * rows[u]
+                for q in below:
+                    cols[q][t] = cols[q][t] - ratio[t] * cols[q][u]
+        done = jnp.zeros((SUB, LANES), jnp.float32)
+        for t in range(SUB):
+            done = jnp.where(sub == t, rows[t] * lax.rsqrt(part[t, t]), done)
+        out.append(done[:, K:])
+        rows = [row * inv for row, inv in zip(rows, inverse)]
+        for q in below:
+            terms = [col * row for col, row in zip(cols[q], rows)]
+            while len(terms) > 1:
+                terms = [a + b for a, b in zip(terms[::2], terms[1::2])]
+            blocks[q] = blocks[q] - terms[0]
+    return jnp.concatenate(out, axis=0)
+
+
 def finish_body(scale, own, other, sketch, basis, projected):
     gc = (own[...] + other[...]) * scale
-    lane = lax.broadcasted_iota(jnp.int32, (SUB, LANES), 1)
-    sub = lax.broadcasted_iota(jnp.int32, (SUB, LANES), 0)
-    blocks = []
-    for r in range(K // SUB):
-        blocks.append(
-            jnp.where(lane < K, gc[r * SUB : (r + 1) * SUB, :], jnp.where(lane == sub + (K + r * SUB), 1.0, 0.0))
-        )
-    for j in range(K):
-        r, s = divmod(j, SUB)
-        row = blocks[r][s : s + 1, :]
-        row = row / row[:, j : j + 1]
-        for q in range(r, K // SUB):
-            factor = blocks[q][:, j : j + 1]
-            if q == r:
-                if s == SUB - 1:
-                    continue
-                factor = jnp.where(sub[:, :1] > s, factor, 0.0)
-            blocks[q] = blocks[q] - factor * row
-    done = []
-    for r in range(K // SUB):
-        pivot = jnp.sum(jnp.where(lane == sub + r * SUB, blocks[r], 0.0), axis=1, keepdims=True)
-        done.append(blocks[r][:, K:] / jnp.sqrt(pivot))
-    inverse = jnp.concatenate(done, axis=0)
+    inverse = inverse_factor(gc)
     mine = pl.multiple_of(lax.div(lax.axis_index("blk"), 2) * K, K)
     basis[...] = dot(inverse, sketch[pl.ds(mine, K), :], 1, 0, HIGHEST)
     coefficient = dot(inverse, gc[:, K:], 1, 0, HIGHEST)
@@ -155,7 +184,7 @@
     left, right = kernel_call(
         pack_body,
         (jax.ShapeDtypeStruct((K + SUB, LANES), f32), jax.ShapeDtypeStruct((K + SUB, rights), f32)),
-        (
+        tuple(pltpu.with_memory_space_constraint(v, pltpu.HBM) for v in (
             left_points.reshape(1, rows),
             left_ports.reshape(1, rows),
             left_values.T,
@@ -164,19 +193,31 @@
             right_values.T,
             sketch_block.reshape(along),
             sketch_weight.reshape(along),
-        ),
+        )),
+        in_specs=[pl.BlockSpec(memory_space=pltpu.HBM)] * 8,
+        scratch_shapes=[
+            pltpu.VMEM((1, rows), f32),
+            pltpu.VMEM((1, rows), jnp.int32),
+            pltpu.VMEM((K, rows), left_values.dtype),
+            pltpu.VMEM(along, f32),
+            pltpu.VMEM(along, jnp.int32),
+            pltpu.VMEM((K, rights), right_values.dtype),
+            pltpu.VMEM(along, jnp.int32),
+            pltpu.VMEM(along, sketch_weight.dtype),
+            pltpu.SemaphoreType.DMA((8,)),
+        ],
     )
     place = lax.axis_index("blk")
     lefts, distance = [left], 2
     while True:
-        got = [swap(v, "blk", distance) for v in lefts]
+        got = [swap(v, distance) for v in lefts]
         if distance * 2 >= blk:
             break
         here = (place // distance) % 2 == 0
         lefts = [jnp.where(here, a, b) for a, b in zip(lefts, got)] + [jnp.where(here, b, a) for a, b in zip(lefts, got)]
         distance *= 2
     lefts = lefts + got
-    rights_held = [right, swap(right, "blk", 1)]
+    rights_held = [right, swap(right, 1)]
     held = len(lefts)
     pay, freq, ports = kernel_call(
         functools.partial(sketch_body, held, distance),
@@ -190,24 +231,24 @@
     )
     step = 2
     while step < distance:
-        pay = pay + swap(pay, "blk", step)
+        pay = pay + swap(pay, step)
         step *= 2
     gc, sketch = kernel_call(
         moments_body,
         (jax.ShapeDtypeStruct((K, LANES), f32), jax.ShapeDtypeStruct((held * K, LANES), f32)),
-        (pay, swap(pay, "blk", distance), freq, ports),
-    )
-    hops = [("blk", 1)]
-    distance = 2
+        (pay, swap(pay, distance), freq, ports),
+    )
+    gc = gc + swap(gc, 0, 1)
+    hops, distance = [(1, 1)], 2
     while distance < wide:
-        hops.append(("wide", distance))
+        hops.append((0, distance + 1))
         distance *= 2
-    for axis, distance in hops:
-        gc = gc + swap(gc, axis, distance)
+    for hop in hops[:-1]:
+        gc = gc + swap(gc, *hop)
     basis, projected = kernel_call(
         functools.partial(finish_body, 1.0 / (rows * blk * wide)),
         (jax.ShapeDtypeStruct((K, rows), f32), jax.ShapeDtypeStruct((K, K), f32)),
-        (gc, swap(gc, "wide", 1), sketch),
+        (gc, swap(gc, *hops[-1]), sketch),
     )
     return basis.T, projected
 

time: 38.2 us -> 31.5 us (0.82)
  Pallas kernels: 8 us -> 5.49 us
  local copies, waits for them, and re-layouts: 2.25 us -> 0 us
  waiting for transfers between devices: 13.5 us -> 12.1 us
    pallas_call x4, Pallas kernels: 8 us -> 5.49 us  [kernel_call(): pl.pallas_call(body, out_shape=out_shape, compiler_params=pltpu.CompilerP...]
    unnamed x16 -> x0, local copies, waits for them, and re-layouts: 2.25 us -> none
    ppermute x7, waiting for transfers between devices: 13.5 us -> 12.1 us  [swap(): return lax.ppermute(value, ('wide', 'blk'), pairs)]
where the time goes in v3:
time: 31.5 us; the launch traced here: 31.4 us
  starting transfers between devices  13.1 us (42%)
  waiting for transfers between devices  12.1 us (38%)
  Pallas kernels  5.49 us (17%)
  between operations  0.66 us (2%)
    ppermute x7, starting transfers between devices, swap(): return lax.ppermute(value, ('wide', 'blk'), pairs)  13.1 us
    ppermute x7, waiting for transfers between devices, swap(): return lax.ppermute(value, ('wide', 'blk'), pairs)  12.1 us
    pallas_call x4, Pallas kernels, kernel_call(): pl.pallas_call(body, out_shape=out_shape, compiler_params=pltpu.CompilerP...  5.49 us
  transfers between devices with their start and end apart: 7, of which 6 were waited for; matrix products, arithmetic and copies ran while one was open for 0% of the time, Pallas kernels for 0%

profile of v3, /device:TPU:0, one launch (start us, length us, event | category | flops | bytes accessed | tf_op | source)
XLA Modules:
  0.0 31.4 jit_solution(11810501345660887946)
XLA Ops:
  0.6 1.0 %shard_map.95 = (f32[72,128]{1,0:T(8,128)S(1)}, f32[72,512]{1,0:T(8,128)S(1)}) custom-call(f32[1,128]{1,0:T(1,128)} %bitcast.15, s32[1,128]{1,0:T(1,128)} %bitcast.16, bf16[64,128]{1,0:T(8,128)(2,1)} %bitcast.10, f32[4,128]{1,0:T(4,128)} %bitcast.11, s32[4,128]{1,0:T(4,128)} %bitcast.12, bf16[64,512]{1,0:T(8,128)(2,1)} %bitcast.9, s32[4,128]{1,0:T(4,128)} %bitcast.13, ...), custom_call_target="tpu_custom_call" | custom-call | tf_op jit(solution)/shard_map/pallas_call | solution.py:24
  1.7 3.1 %collective-permute-start.1 = (f32[72,512]{1,0:T(8,128)S(1)}, f32[72,512]{1,0:T(8,128)S(1)}, u32[]{:S(2)}, u32[]{:S(2)}) collective-permute-start(f32[72,512]{1,0:T(8,128)S(1)} %get-tuple-element.12.refs_2_), channel_id=1, source_target_pairs={{0,1},{1,0},{2,3},{3,2},{4,5},{5,4},{6,7},{7,6},{8,9},{9,8},{10,11... | collective-permute-start | bytes 442376 | tf_op jit(solution)/shard_map/ppermute | solution.py:20
  4.8 2.6 %collective-permute-start = (f32[72,128]{1,0:T(8,128)S(1)}, f32[72,128]{1,0:T(8,128)S(1)}, u32[]{:S(2)}, u32[]{:S(2)}) collective-permute-start(f32[72,128]{1,0:T(8,128)S(1)} %get-tuple-element.11.refs_0_), channel_id=1, source_target_pairs={{0,2},{1,3},{2,0},{3,1},{4,6},{5,7},{6,4},{7,5},{8,10},{9,11},{10,... | collective-permute-start | bytes 110600 | tf_op jit(solution)/shard_map/ppermute | solution.py:20
  7.4 2.3 %collective-permute-done.refs_1_ = f32[72,128]{1,0:T(8,128)S(1)} collective-permute-done((f32[72,128]{1,0:T(8,128)S(1)}, f32[72,128]{1,0:T(8,128)S(1)}, u32[]{:S(2)}, u32[]{:S(2)}) %collective-permute-start) | collective-permute-done | bytes 36896 | tf_op jit(solution)/shard_map/ppermute | solution.py:20
  9.6 0.0 collective-permute-done.1.refs_3_
  9.6 1.2 %shard_map.96 = (f32[160,128]{1,0:T(8,128)S(1)}, f32[2,128]{1,0:T(2,128)S(1)}, f32[2,128]{1,0:T(2,128)S(1)}) custom-call(f32[72,128]{1,0:T(8,128)S(1)} %get-tuple-element.11.refs_0_, f32[72,128]{1,0:T(8,128)S(1)} %collective-permute-done.refs_1_, f32[72,512]{1,0:T(8,128)S(1)} %get-tuple-element.12.refs_2_, f32[72,512]{1,0:T(8,128)S(1)} %collective-permute-done.1.refs_3_), custom_call_target="tpu_custom_call" | custom-call | tf_op jit(solution)/shard_map/pallas_call | solution.py:24
  10.8 2.6 %collective-permute-start.2 = (f32[160,128]{1,0:T(8,128)S(1)}, f32[160,128]{1,0:T(8,128)S(1)}, u32[]{:S(2)}, u32[]{:S(2)}) collective-permute-start(f32[160,128]{1,0:T(8,128)S(1)} %get-tuple-element.13.own), channel_id=1, source_target_pairs={{0,2},{1,3},{2,0},{3,1},{4,6},{5,7},{6,4},{7,5},{8,10},{9,11},{10,... | collective-permute-start | bytes 245768 | tf_op jit(solution)/shard_map/ppermute | solution.py:20
  13.4 3.3 %collective-permute-done.2.other = f32[160,128]{1,0:T(8,128)S(1)} collective-permute-done((f32[160,128]{1,0:T(8,128)S(1)}, f32[160,128]{1,0:T(8,128)S(1)}, u32[]{:S(2)}, u32[]{:S(2)}) %collective-permute-start.2) | collective-permute-done | bytes 81952 | tf_op jit(solution)/shard_map/ppermute | solution.py:20
  16.8 0.5 %shard_map.97 = (f32[64,128]{1,0:T(8,128)S(1)}, f32[128,128]{1,0:T(8,128)S(1)}) custom-call(f32[160,128]{1,0:T(8,128)S(1)} %get-tuple-element.13.own, f32[160,128]{1,0:T(8,128)S(1)} %collective-permute-done.2.other, f32[2,128]{1,0:T(2,128)S(1)} %get-tuple-element.14.freq, f32[2,128]{1,0:T(2,128)S(1)} %get-tuple-element.15.ports), custom_call_target="tpu_custom_call" | custom-call | tf_op jit(solution)/shard_map/pallas_call | solution.py:24
  17.2 0.1 collective-permute-start.3
  17.3 1.2 %collective-permute-done.3 = f32[64,128]{1,0:T(8,128)S(1)} collective-permute-done((f32[64,128]{1,0:T(8,128)S(1)}, f32[64,128]{1,0:T(8,128)S(1)}, u32[]{:S(2)}, u32[]{:S(2)}) %collective-permute-start.3) | collective-permute-done | bytes 32800 | tf_op jit(solution)/shard_map/ppermute | solution.py:20
  18.5 1.7 %collective-permute-start.4 = (f32[64,128]{1,0:T(8,128)S(1)}, f32[64,128]{1,0:T(8,128)S(1)}, u32[]{:S(2)}, u32[]{:S(2)}) collective-permute-start(f32[64,128]{1,0:T(8,128)S(1)} %add.9), channel_id=1, source_target_pairs={{0,5},{1,4},{2,7},{3,6},{4,1},{5,0},{6,3},{7,2},{8,13},{9,12},{10,... | collective-permute-start | bytes 98312 | tf_op jit(solution)/shard_map/ppermute | solution.py:20
  20.2 1.6 %collective-permute-done.4 = f32[64,128]{1,0:T(8,128)S(1)} collective-permute-done((f32[64,128]{1,0:T(8,128)S(1)}, f32[64,128]{1,0:T(8,128)S(1)}, u32[]{:S(2)}, u32[]{:S(2)}) %collective-permute-start.4) | collective-permute-done | bytes 32800 | tf_op jit(solution)/shard_map/ppermute | solution.py:20
  21.8 1.4 %collective-permute-start.5 = (f32[64,128]{1,0:T(8,128)S(1)}, f32[64,128]{1,0:T(8,128)S(1)}, u32[]{:S(2)}, u32[]{:S(2)}) collective-permute-start(f32[64,128]{1,0:T(8,128)S(1)} %add.10), channel_id=1, source_target_pairs={{0,12},{1,13},{2,14},{3,15},{4,8},{5,9},{6,10},{7,11},{8,4},{9,5},... | collective-permute-start | bytes 98312 | tf_op jit(solution)/shard_map/ppermute | solution.py:20
  23.3 1.9 %collective-permute-done.5 = f32[64,128]{1,0:T(8,128)S(1)} collective-permute-done((f32[64,128]{1,0:T(8,128)S(1)}, f32[64,128]{1,0:T(8,128)S(1)}, u32[]{:S(2)}, u32[]{:S(2)}) %collective-permute-start.5) | collective-permute-done | bytes 32800 | tf_op jit(solution)/shard_map/ppermute | solution.py:20
  25.2 1.5 %collective-permute-start.6 = (f32[64,128]{1,0:T(8,128)S(1)}, f32[64,128]{1,0:T(8,128)S(1)}, u32[]{:S(2)}, u32[]{:S(2)}) collective-permute-start(f32[64,128]{1,0:T(8,128)S(1)} %add.11.own), channel_id=1, source_target_pairs={{0,20},{1,21},{2,22},{3,23},{4,16},{5,17},{6,18},{7,19},{8,28},{9,... | collective-permute-start | bytes 98312 | tf_op jit(solution)/shard_map/ppermute | solution.py:20
  26.6 1.9 %collective-permute-done.6.other = f32[64,128]{1,0:T(8,128)S(1)} collective-permute-done((f32[64,128]{1,0:T(8,128)S(1)}, f32[64,128]{1,0:T(8,128)S(1)}, u32[]{:S(2)}, u32[]{:S(2)}) %collective-permute-start.6) | collective-permute-done | bytes 32800 | tf_op jit(solution)/shard_map/ppermute | solution.py:20
  28.5 2.9 %shard_map.98 = (f32[64,128]{1,0:T(8,128)}, f32[64,64]{1,0:T(8,128)}) custom-call(f32[64,128]{1,0:T(8,128)S(1)} %add.11.own, f32[64,128]{1,0:T(8,128)S(1)} %collective-permute-done.6.other, f32[128,128]{1,0:T(8,128)S(1)} %get-tuple-element.17.sketch), custom_call_target="tpu_custom_call" | custom-call | tf_op jit(solution)/shard_map/pallas_call | solution.py:24
  (3 shorter events, 0.0 us)
Async XLA Ops:
  1.7 8.0 %collective-permute-start.1 = (f32[72,512]{1,0:T(8,128)S(1)}, f32[72,512]{1,0:T(8,128)S(1)}, u32[]{:S(2)}, u32[]{:S(2)}) collective-permute-start(f32[72,512]{1,0:T(8,128)S(1)} %get-tuple-element.12.refs_2_), channel_id=1, source_target_pairs={{0,1},{1,0},{2,3},{3,2},{4,5},{5,4},{6,7},{7,6},{8,9},{9,8},{10,11... | collective-permute-start | bytes 442376 | tf_op jit(solution)/shard_map/ppermute | solution.py:20
  4.8 4.9 %collective-permute-start = (f32[72,128]{1,0:T(8,128)S(1)}, f32[72,128]{1,0:T(8,128)S(1)}, u32[]{:S(2)}, u32[]{:S(2)}) collective-permute-start(f32[72,128]{1,0:T(8,128)S(1)} %get-tuple-element.11.refs_0_), channel_id=1, source_target_pairs={{0,2},{1,3},{2,0},{3,1},{4,6},{5,7},{6,4},{7,5},{8,10},{9,11},{10,... | collective-permute-start | bytes 110600 | tf_op jit(solution)/shard_map/ppermute | solution.py:20
  10.8 6.0 %collective-permute-start.2 = (f32[160,128]{1,0:T(8,128)S(1)}, f32[160,128]{1,0:T(8,128)S(1)}, u32[]{:S(2)}, u32[]{:S(2)}) collective-permute-start(f32[160,128]{1,0:T(8,128)S(1)} %get-tuple-element.13.own), channel_id=1, source_target_pairs={{0,2},{1,3},{2,0},{3,1},{4,6},{5,7},{6,4},{7,5},{8,10},{9,11},{10,... | collective-permute-start | bytes 245768 | tf_op jit(solution)/shard_map/ppermute | solution.py:20
  17.2 1.3 %collective-permute-start.3 = (f32[64,128]{1,0:T(8,128)S(1)}, f32[64,128]{1,0:T(8,128)S(1)}, u32[]{:S(2)}, u32[]{:S(2)}) collective-permute-start(f32[64,128]{1,0:T(8,128)S(1)} %get-tuple-element.16), channel_id=1, source_target_pairs={{0,4},{1,5},{2,6},{3,7},{4,0},{5,1},{6,2},{7,3},{8,12},{9,13},{10,... | collective-permute-start | bytes 98312 | tf_op jit(solution)/shard_map/ppermute | solution.py:20
  18.5 3.3 %collective-permute-start.4 = (f32[64,128]{1,0:T(8,128)S(1)}, f32[64,128]{1,0:T(8,128)S(1)}, u32[]{:S(2)}, u32[]{:S(2)}) collective-permute-start(f32[64,128]{1,0:T(8,128)S(1)} %add.9), channel_id=1, source_target_pairs={{0,5},{1,4},{2,7},{3,6},{4,1},{5,0},{6,3},{7,2},{8,13},{9,12},{10,... | collective-permute-start | bytes 98312 | tf_op jit(solution)/shard_map/ppermute | solution.py:20
  21.8 3.3 %collective-permute-start.5 = (f32[64,128]{1,0:T(8,128)S(1)}, f32[64,128]{1,0:T(8,128)S(1)}, u32[]{:S(2)}, u32[]{:S(2)}) collective-permute-start(f32[64,128]{1,0:T(8,128)S(1)} %add.10), channel_id=1, source_target_pairs={{0,12},{1,13},{2,14},{3,15},{4,8},{5,9},{6,10},{7,11},{8,4},{9,5},... | collective-permute-start | bytes 98312 | tf_op jit(solution)/shard_map/ppermute | solution.py:20
  25.2 3.3 %collective-permute-start.6 = (f32[64,128]{1,0:T(8,128)S(1)}, f32[64,128]{1,0:T(8,128)S(1)}, u32[]{:S(2)}, u32[]{:S(2)}) collective-permute-start(f32[64,128]{1,0:T(8,128)S(1)} %add.11.own), channel_id=1, source_target_pairs={{0,20},{1,21},{2,22},{3,23},{4,16},{5,17},{6,18},{7,19},{8,28},{9,... | collective-permute-start | bytes 98312 | tf_op jit(solution)/shard_map/ppermute | solution.py:20

commit v4 on v3

--- a/solution.py
+++ b/solution.py
@@ -65,43 +65,62 @@
         right[K + 3 : K + 4, lanes] = weights[s : s + 1, :]
 
 
-def in_order(lefts, distance):
-    half = len(lefts) // 2
+def left_side(left):
+    index = lax.broadcasted_iota(jnp.int32, (K, LANES), 0).astype(jnp.float32)
+    hot = jnp.where(left[K + 1 : K + 2, :] == index, -1.0, 0.0)
+    side = jnp.concatenate([left[:K, :], hot], axis=0).T.astype(jnp.bfloat16)
+    return side, jnp.broadcast_to(left[K : K + 1, :], (LANES, LANES)).T
+
+
+def right_side(right):
+    index = lax.broadcasted_iota(jnp.int32, (K, right.shape[1]), 0).astype(jnp.float32)
+    pick = jnp.where(right[K + 1 : K + 2, :] == index, 1.0, 0.0)
+    table = jnp.concatenate([pick, right[:K, :]], axis=0).astype(jnp.bfloat16)
+    return table, jnp.where(right[K + 2 : K + 3, :] == index, right[K + 3 : K + 4, :], 0.0).astype(jnp.bfloat16)
+
+
+def sketch_terms(side, freq, table, omega, lam):
+    scale = jnp.concatenate([freq] * (lam.shape[1] // LANES), axis=1) - lam
+    loewner = dot(side, table, 1, 0) / scale
+    return sum(dot(piece, omega, 1, 1) for piece in pieces(loewner))
+
+
+def local_body(*refs):
+    lefts, (right, side_out, freq_out, table_out, omega_out, total, cross) = refs[:-7], refs[-7:]
+    table, omega = right_side(right)
+    table_out[...] = table
+    omega_out[...] = omega
+    for q, left in enumerate(lefts):
+        span = slice(q * LANES, (q + 1) * LANES)
+        side, freq = left_side(left)
+        side_out[span, :] = side
+        freq_out[span, :] = freq
+        total[span, :] = sketch_terms(side, freq, table, omega, right[K : K + 1, :])
+    cross[...] = dot(omega, table[K:, :], 1, 1)
+
+
+def sketch_body(distance, *refs):
+    count = (len(refs) - 11) // 2
+    owns, gots = refs[:count], refs[count : 2 * count]
+    right, other, side_in, freq_in, table_in, omega_in, total_in, cross_in, pay, freq_row, port_row = refs[2 * count :]
+    table, omega = right_side(other)
+    near, far = right[K : K + 1, :], other[K : K + 1, :]
     here = lax.rem(lax.div(lax.axis_index("blk"), distance), 2) == 0
-    own, got = [ref[...] for ref in lefts[:half]], [ref[...] for ref in lefts[half:]]
-    return [jnp.where(here, a, b) for a, b in zip(own, got)] + [jnp.where(here, b, a) for a, b in zip(own, got)]
-
-
-def sketch_body(n_left, distance, *refs):
-    lefts, rights, (pay, freq, ports) = in_order(refs[:n_left], distance), refs[n_left:-3], refs[-3:]
-    index = lax.broadcasted_iota(jnp.int32, (K, LANES), 0).astype(jnp.float32)
-    mus, sides = [], []
-    for q, left in enumerate(lefts):
-        mu, port = left[K : K + 1, :], left[K + 1 : K + 2, :]
-        freq[q : q + 1, :] = mu
-        ports[q : q + 1, :] = port
-        mus.append(jnp.broadcast_to(mu, (LANES, LANES)).T)
-        sides.append(jnp.concatenate([left[:K, :], jnp.where(port == index, -1.0, 0.0)], axis=0).T.astype(jnp.bfloat16))
-    side = jnp.concatenate(sides, axis=0)
-    rows = side.shape[0]
-    total = jnp.zeros((rows, K), jnp.float32)
-    cross = jnp.zeros((K, K), jnp.float32)
-    for right in rights:
-        width = right.shape[1]
-        index = lax.broadcasted_iota(jnp.int32, (K, width), 0).astype(jnp.float32)
-        values = right[:K, :].astype(jnp.bfloat16)
-        lam = right[K : K + 1, :]
-        pick = jnp.where(right[K + 1 : K + 2, :] == index, 1.0, 0.0).astype(jnp.bfloat16)
-        omega = jnp.where(right[K + 2 : K + 3, :] == index, right[K + 3 : K + 4, :], 0.0).astype(jnp.bfloat16)
-        upper = dot(side, jnp.concatenate([pick, values], axis=0), 1, 0)
-        scale = jnp.concatenate([jnp.concatenate([m] * (width // LANES), axis=1) for m in mus], axis=0) - lam
-        loewner = upper / scale
-        for piece in pieces(loewner):
-            total = total + dot(piece, omega, 1, 1)
-        cross = cross + dot(omega, values, 1, 1)
-    for q in range(n_left):
-        pay[q * K : (q + 1) * K, :] = total[q * LANES : (q + 1) * LANES, :].T
-    pay[n_left * K :, :] = jnp.concatenate([cross[: K // 2], cross[K // 2 :]], axis=1)
+    for q in range(count):
+        span = slice(q * LANES, (q + 1) * LANES)
+        side, freq = left_side(gots[q])
+        both = sketch_terms(
+            jnp.concatenate([side_in[span, :], side], axis=0), jnp.concatenate([freq_in[span, :], freq], axis=0), table, omega, far
+        )
+        own = (both[:LANES, :] + total_in[span, :]).T
+        got = (both[LANES:, :] + sketch_terms(side, freq, table_in[...], omega_in[...], near)).T
+        for place, flip in ((q, False), (count + q, True)):
+            spot = slice(place * K, (place + 1) * K)
+            pay[spot, :] = jnp.where(here != flip, own, got)
+            for out, row in ((freq_row, K), (port_row, K + 1)):
+                out[place : place + 1, :] = jnp.where(here != flip, owns[q][row : row + 1, :], gots[q][row : row + 1, :])
+    cross = cross_in[...] + dot(omega, table[K:, :], 1, 1)
+    pay[2 * count * K :, :] = jnp.concatenate([cross[: K // 2], cross[K // 2 :]], axis=1)
 
 
 def moments_body(own, other, freq, ports, gc, full):
@@ -128,7 +147,7 @@
     return jnp.broadcast_to(value, (SUB, LANES))
 
 
-def inverse_factor(gram):
+def inverse_factor(gram, spread):
     lane = lax.broadcasted_iota(jnp.int32, (SUB, LANES), 1)
     sub = lax.broadcasted_iota(jnp.int32, (SUB, LANES), 0)
     count = K // SUB
@@ -138,10 +157,14 @@
     ]
     out = []
     for r in range(count):
-        here, first = blocks[r], r * SUB
+        here, first, base = blocks[r], r * SUB, r * SUB * (SUB + 1)
         below = range(r + 1, count)
-        rows = [full(here[t : t + 1, :]) for t in range(SUB)]
-        part = {(t, u): full(here[t : t + 1, first + u : first + u + 1]) for t in range(SUB) for u in range(t + 1)}
+        for u in range(SUB):
+            spread[base + u * SUB : base + (u + 1) * SUB, :] = full(here[:, first + u : first + u + 1])
+        last = base + SUB * SUB
+        spread[last : last + SUB, :] = here
+        part = {(t, u): full(spread[base + u * SUB + t : base + u * SUB + t + 1, :]) for t in range(SUB) for u in range(t + 1)}
+        rows = [full(spread[last + t : last + t + 1, :]) for t in range(SUB)]
         cols = {q: [full(blocks[q][:, first + u : first + u + 1]) for u in range(SUB)] for q in below}
         inverse = []
         for u in range(SUB):
@@ -149,15 +172,18 @@
             ratio = {t: part[t, u] * inverse[u] for t in range(u + 1, SUB)}
             for t in range(u + 1, SUB):
                 for v in range(u + 1, t + 1):
-                    part[t, v] = part[t, v] - (part[t, u] * part[v, u]) * inverse[u]
+                    if t == u + 1:
+                        part[t, v] = part[t, v] - (part[t, u] * part[v, u]) * inverse[u]
+                    else:
+                        part[t, v] = part[t, v] - ratio[t] * part[v, u]
             for t in range(u + 1, SUB):
                 rows[t] = rows[t] - ratio[t] * rows[u]
                 for q in below:
                     cols[q][t] = cols[q][t] - ratio[t] * cols[q][u]
-        done = jnp.zeros((SUB, LANES), jnp.float32)
-        for t in range(SUB):
-            done = jnp.where(sub == t, rows[t] * lax.rsqrt(part[t, t]), done)
-        out.append(done[:, K:])
+        done, pivot = rows[0], part[0, 0]
+        for t in range(1, SUB):
+            done, pivot = jnp.where(sub == t, rows[t], done), jnp.where(sub == t, part[t, t], pivot)
+        out.append((done * lax.rsqrt(pivot))[:, K:])
         rows = [row * inv for row, inv in zip(rows, inverse)]
         for q in below:
             terms = [col * row for col, row in zip(cols[q], rows)]
@@ -167,9 +193,9 @@
     return jnp.concatenate(out, axis=0)
 
 
-def finish_body(scale, own, other, sketch, basis, projected):
-    gc = (own[...] + other[...]) * scale
-    inverse = inverse_factor(gc)
+def finish_body(scale, own, first, second, third, sketch, basis, projected, spread):
+    gc = ((own[...] + first[...]) + (second[...] + third[...])) * scale
+    inverse = inverse_factor(gc, spread)
     mine = pl.multiple_of(lax.div(lax.axis_index("blk"), 2) * K, K)
     basis[...] = dot(inverse, sketch[pl.ds(mine, K), :], 1, 0, HIGHEST)
     coefficient = dot(inverse, gc[:, K:], 1, 0, HIGHEST)
@@ -216,18 +242,29 @@
         here = (place // distance) % 2 == 0
         lefts = [jnp.where(here, a, b) for a, b in zip(lefts, got)] + [jnp.where(here, b, a) for a, b in zip(lefts, got)]
         distance *= 2
-    lefts = lefts + got
-    rights_held = [right, swap(right, 1)]
-    held = len(lefts)
+    other = swap(right, 1)
+    count = len(lefts)
+    held = 2 * count
+    local = kernel_call(
+        local_body,
+        (
+            jax.ShapeDtypeStruct((count * LANES, LANES), jnp.bfloat16),
+            jax.ShapeDtypeStruct((count * LANES, LANES), f32),
+            jax.ShapeDtypeStruct((2 * K, rights), jnp.bfloat16),
+            jax.ShapeDtypeStruct((K, rights), jnp.bfloat16),
+            jax.ShapeDtypeStruct((count * LANES, K), f32),
+            jax.ShapeDtypeStruct((K, K), f32),
+        ),
+        (*lefts, right),
+    )
     pay, freq, ports = kernel_call(
-        functools.partial(sketch_body, held, distance),
+        functools.partial(sketch_body, distance),
         (
             jax.ShapeDtypeStruct((held * K + K // 2, LANES), f32),
             jax.ShapeDtypeStruct((held, LANES), f32),
             jax.ShapeDtypeStruct((held, LANES), f32),
         ),
-        (*lefts, *rights_held),
-        limit=max(VMEM_LIMIT, held * VMEM_LIMIT // 2),
+        (*lefts, *got, right, other, *local),
     )
     step = 2
     while step < distance:
@@ -243,12 +280,15 @@
     while distance < wide:
         hops.append((0, distance + 1))
         distance *= 2
-    for hop in hops[:-1]:
+    for hop in hops[:-2]:
         gc = gc + swap(gc, *hop)
+    (b0, w0), (b1, w1) = hops[-2:]
+    parts = (gc, swap(gc, b0, w0), swap(gc, b1, w1), swap(gc, b0 ^ b1, w0 ^ w1 ^ 1))
     basis, projected = kernel_call(
         functools.partial(finish_body, 1.0 / (rows * blk * wide)),
         (jax.ShapeDtypeStruct((K, rows), f32), jax.ShapeDtypeStruct((K, K), f32)),
-        (gc, swap(gc, *hops[-1]), sketch),
+        (*parts, sketch),
+        scratch_shapes=[pltpu.VMEM((K * (SUB + 1), LANES), f32)],
     )
     return basis.T, projected
 

time: 31.5 us -> 30.2 us (0.959)
  waiting for transfers between devices: 12.1 us -> 10.7 us
    ppermute x7 -> x8, waiting for transfers between devices: 12.1 us -> 10.7 us  [swap(): return lax.ppermute(value, ('wide', 'blk'), pairs)]
    ppermute x7 -> x8, starting transfers between devices: 13.1 us -> 13.3 us  [swap(): return lax.ppermute(value, ('wide', 'blk'), pairs)]
    pallas_call x4 -> x5, Pallas kernels: 5.49 us -> 5.31 us  [kernel_call(): pl.pallas_call(body, out_shape=out_shape, compiler_params=pltpu.CompilerP...]
  transfers between devices with their start and end apart: 7 -> 8, of which waited for: 6 -> 7; matrix products, arithmetic and copies ran while one was open for 0% -> 0% of each run, Pallas kernels for 0% -> 2%
where the time goes in v4:
time: 30.2 us; the launch traced here: 30 us
  starting transfers between devices  13.3 us (44%)
  waiting for transfers between devices  10.7 us (35%)
  Pallas kernels  5.31 us (18%)
  between operations  0.67 us (2%)
    ppermute x8, starting transfers between devices, swap(): return lax.ppermute(value, ('wide', 'blk'), pairs)  13.3 us
    ppermute x8, waiting for transfers between devices, swap(): return lax.ppermute(value, ('wide', 'blk'), pairs)  10.7 us
    pallas_call x5, Pallas kernels, kernel_call(): pl.pallas_call(body, out_shape=out_shape, compiler_params=pltpu.CompilerP...  5.31 us
  transfers between devices with their start and end apart: 8, of which 7 were waited for; matrix products, arithmetic and copies ran while one was open for 0% of the time, Pallas kernels for 2%

profile of v4, /device:TPU:0, one launch (start us, length us, event | category | flops | bytes accessed | tf_op | source)
XLA Modules:
  0.0 30.0 jit_solution(11836862467845676215)
XLA Ops:
  0.6 1.0 %shard_map.95 = (f32[72,128]{1,0:T(8,128)S(1)}, f32[72,512]{1,0:T(8,128)S(1)}) custom-call(f32[1,128]{1,0:T(1,128)} %bitcast.15, s32[1,128]{1,0:T(1,128)} %bitcast.16, bf16[64,128]{1,0:T(8,128)(2,1)} %bitcast.10, f32[4,128]{1,0:T(4,128)} %bitcast.11, s32[4,128]{1,0:T(4,128)} %bitcast.12, bf16[64,512]{1,0:T(8,128)(2,1)} %bitcast.9, s32[4,128]{1,0:T(4,128)} %bitcast.13, ...), custom_call_target="tpu_custom_call" | custom-call | tf_op jit(solution)/shard_map/pallas_call | solution.py:24
  1.7 3.1 %collective-permute-start.1 = (f32[72,512]{1,0:T(8,128)S(1)}, f32[72,512]{1,0:T(8,128)S(1)}, u32[]{:S(2)}, u32[]{:S(2)}) collective-permute-start(f32[72,512]{1,0:T(8,128)S(1)} %get-tuple-element.18.refs_1_.refs_2_), channel_id=1, source_target_pairs={{0,1},{1,0},{2,3},{3,2},{4,5},{5,4},{6,7},{7,6},{8,9},{9,8},{10,11... | collective-permute-start | bytes 442376 | tf_op jit(solution)/shard_map/ppermute | solution.py:20
  4.8 2.6 %collective-permute-start = (f32[72,128]{1,0:T(8,128)S(1)}, f32[72,128]{1,0:T(8,128)S(1)}, u32[]{:S(2)}, u32[]{:S(2)}) collective-permute-start(f32[72,128]{1,0:T(8,128)S(1)} %get-tuple-element.17.refs_0_), channel_id=1, source_target_pairs={{0,2},{1,3},{2,0},{3,1},{4,6},{5,7},{6,4},{7,5},{8,10},{9,11},{10,... | collective-permute-start | bytes 110600 | tf_op jit(solution)/shard_map/ppermute | solution.py:20
  7.4 0.5 %shard_map.96 = (bf16[128,128]{1,0:T(8,128)(2,1)S(1)}, f32[128,128]{1,0:T(8,128)S(1)}, bf16[128,512]{1,0:T(8,128)(2,1)S(1)}, bf16[64,512]{1,0:T(8,128)(2,1)S(1)}...) custom-call(f32[72,128]{1,0:T(8,128)S(1)} %get-tuple-element.17.refs_0_, f32[72,512]{1,0:T(8,128)S(1)} %get-tuple-element.18.refs_1_.refs_2_), custom_call_target="tpu_custom_call" | custom-call | tf_op jit(solution)/shard_map/pallas_call | solution.py:24
  7.9 1.8 %collective-permute-done.refs_1_ = f32[72,128]{1,0:T(8,128)S(1)} collective-permute-done((f32[72,128]{1,0:T(8,128)S(1)}, f32[72,128]{1,0:T(8,128)S(1)}, u32[]{:S(2)}, u32[]{:S(2)}) %collective-permute-start) | collective-permute-done | bytes 36896 | tf_op jit(solution)/shard_map/ppermute | solution.py:20
  9.6 0.0 collective-permute-done.1.refs_3_
  9.6 0.9 %shard_map.97 = (f32[160,128]{1,0:T(8,128)S(1)}, f32[2,128]{1,0:T(2,128)S(1)}, f32[2,128]{1,0:T(2,128)S(1)}) custom-call(f32[72,128]{1,0:T(8,128)S(1)} %get-tuple-element.17.refs_0_, f32[72,128]{1,0:T(8,128)S(1)} %collective-permute-done.refs_1_, f32[72,512]{1,0:T(8,128)S(1)} %get-tuple-element.18.refs_1_.refs_2_, ...), custom_call_target="tpu_custom_call" | custom-call | tf_op jit(solution)/shard_map/pallas_call | solution.py:24
  10.5 2.7 %collective-permute-start.2 = (f32[160,128]{1,0:T(8,128)S(1)}, f32[160,128]{1,0:T(8,128)S(1)}, u32[]{:S(2)}, u32[]{:S(2)}) collective-permute-start(f32[160,128]{1,0:T(8,128)S(1)} %get-tuple-element.25.own), channel_id=1, source_target_pairs={{0,2},{1,3},{2,0},{3,1},{4,6},{5,7},{6,4},{7,5},{8,10},{9,11},{10,... | collective-permute-start | bytes 245768 | tf_op jit(solution)/shard_map/ppermute | solution.py:20
  13.2 3.3 %collective-permute-done.2.other = f32[160,128]{1,0:T(8,128)S(1)} collective-permute-done((f32[160,128]{1,0:T(8,128)S(1)}, f32[160,128]{1,0:T(8,128)S(1)}, u32[]{:S(2)}, u32[]{:S(2)}) %collective-permute-start.2) | collective-permute-done | bytes 81952 | tf_op jit(solution)/shard_map/ppermute | solution.py:20
  16.5 0.5 %shard_map.98 = (f32[64,128]{1,0:T(8,128)S(1)}, f32[128,128]{1,0:T(8,128)S(1)}) custom-call(f32[160,128]{1,0:T(8,128)S(1)} %get-tuple-element.25.own, f32[160,128]{1,0:T(8,128)S(1)} %collective-permute-done.2.other, f32[2,128]{1,0:T(2,128)S(1)} %get-tuple-element.26.freq, f32[2,128]{1,0:T(2,128)S(1)} %get-tuple-element.27.ports), custom_call_target="tpu_custom_call" | custom-call | tf_op jit(solution)/shard_map/pallas_call | solution.py:24
  16.9 0.1 collective-permute-start.3
  17.0 1.2 %collective-permute-done.3 = f32[64,128]{1,0:T(8,128)S(1)} collective-permute-done((f32[64,128]{1,0:T(8,128)S(1)}, f32[64,128]{1,0:T(8,128)S(1)}, u32[]{:S(2)}, u32[]{:S(2)}) %collective-permute-start.3) | collective-permute-done | bytes 32800 | tf_op jit(solution)/shard_map/ppermute | solution.py:20
  18.2 1.7 %collective-permute-start.4 = (f32[64,128]{1,0:T(8,128)S(1)}, f32[64,128]{1,0:T(8,128)S(1)}, u32[]{:S(2)}, u32[]{:S(2)}) collective-permute-start(f32[64,128]{1,0:T(8,128)S(1)} %add.6), channel_id=1, source_target_pairs={{0,5},{1,4},{2,7},{3,6},{4,1},{5,0},{6,3},{7,2},{8,13},{9,12},{10,... | collective-permute-start | bytes 98312 | tf_op jit(solution)/shard_map/ppermute | solution.py:20
  19.9 1.6 %collective-permute-done.4 = f32[64,128]{1,0:T(8,128)S(1)} collective-permute-done((f32[64,128]{1,0:T(8,128)S(1)}, f32[64,128]{1,0:T(8,128)S(1)}, u32[]{:S(2)}, u32[]{:S(2)}) %collective-permute-start.4) | collective-permute-done | bytes 32800 | tf_op jit(solution)/shard_map/ppermute | solution.py:20
  21.6 2.4 %collective-permute-start.7 = (f32[64,128]{1,0:T(8,128)S(1)}, f32[64,128]{1,0:T(8,128)S(1)}, u32[]{:S(2)}, u32[]{:S(2)}) collective-permute-start(f32[64,128]{1,0:T(8,128)S(1)} %add.7.own), channel_id=1, source_target_pairs={{0,28},{1,29},{2,30},{3,31},{4,24},{5,25},{6,26},{7,27},{8,20},{9,... | collective-permute-start | bytes 98312 | tf_op jit(solution)/shard_map/ppermute | solution.py:20
  23.9 0.3 collective-permute-start.6
  24.2 0.5 %collective-permute-start.5 = (f32[64,128]{1,0:T(8,128)S(1)}, f32[64,128]{1,0:T(8,128)S(1)}, u32[]{:S(2)}, u32[]{:S(2)}) collective-permute-start(f32[64,128]{1,0:T(8,128)S(1)} %add.7.own), channel_id=1, source_target_pairs={{0,12},{1,13},{2,14},{3,15},{4,8},{5,9},{6,10},{7,11},{8,4},{9,5},... | collective-permute-start | bytes 98312 | tf_op jit(solution)/shard_map/ppermute | solution.py:20
  24.7 1.1 %collective-permute-done.7.third = f32[64,128]{1,0:T(8,128)S(1)} collective-permute-done((f32[64,128]{1,0:T(8,128)S(1)}, f32[64,128]{1,0:T(8,128)S(1)}, u32[]{:S(2)}, u32[]{:S(2)}) %collective-permute-start.7) | collective-permute-done | bytes 32800 | tf_op jit(solution)/shard_map/ppermute | solution.py:20
  25.8 1.5 %collective-permute-done.6.second = f32[64,128]{1,0:T(8,128)S(1)} collective-permute-done((f32[64,128]{1,0:T(8,128)S(1)}, f32[64,128]{1,0:T(8,128)S(1)}, u32[]{:S(2)}, u32[]{:S(2)}) %collective-permute-start.6) | collective-permute-done | bytes 32800 | tf_op jit(solution)/shard_map/ppermute | solution.py:20
  27.3 0.3 collective-permute-done.5.first
  27.6 2.5 %shard_map.99 = (f32[64,128]{1,0:T(8,128)}, f32[64,64]{1,0:T(8,128)}) custom-call(f32[64,128]{1,0:T(8,128)S(1)} %add.7.own, f32[64,128]{1,0:T(8,128)S(1)} %collective-permute-done.5.first, f32[64,128]{1,0:T(8,128)S(1)} %collective-permute-done.6.second, f32[64,128]{1,0:T(8,128)S(1)} %collective-permute-done.7.third, f32[128,128]{1,0:T(8,128)S(1)} %get-tuple-element.29.sketch), custom_call_target="tpu_custom_call" | custom-call | tf_op jit(solution)/shard_map/pallas_call | solution.py:24
  (2 shorter events, 0.0 us)
Async XLA Ops:
  1.7 8.0 %collective-permute-start.1 = (f32[72,512]{1,0:T(8,128)S(1)}, f32[72,512]{1,0:T(8,128)S(1)}, u32[]{:S(2)}, u32[]{:S(2)}) collective-permute-start(f32[72,512]{1,0:T(8,128)S(1)} %get-tuple-element.18.refs_1_.refs_2_), channel_id=1, source_target_pairs={{0,1},{1,0},{2,3},{3,2},{4,5},{5,4},{6,7},{7,6},{8,9},{9,8},{10,11... | collective-permute-start | bytes 442376 | tf_op jit(solution)/shard_map/ppermute | solution.py:20
  4.8 4.9 %collective-permute-start = (f32[72,128]{1,0:T(8,128)S(1)}, f32[72,128]{1,0:T(8,128)S(1)}, u32[]{:S(2)}, u32[]{:S(2)}) collective-permute-start(f32[72,128]{1,0:T(8,128)S(1)} %get-tuple-element.17.refs_0_), channel_id=1, source_target_pairs={{0,2},{1,3},{2,0},{3,1},{4,6},{5,7},{6,4},{7,5},{8,10},{9,11},{10,... | collective-permute-start | bytes 110600 | tf_op jit(solution)/shard_map/ppermute | solution.py:20
  10.5 6.0 %collective-permute-start.2 = (f32[160,128]{1,0:T(8,128)S(1)}, f32[160,128]{1,0:T(8,128)S(1)}, u32[]{:S(2)}, u32[]{:S(2)}) collective-permute-start(f32[160,128]{1,0:T(8,128)S(1)} %get-tuple-element.25.own), channel_id=1, source_target_pairs={{0,2},{1,3},{2,0},{3,1},{4,6},{5,7},{6,4},{7,5},{8,10},{9,11},{10,... | collective-permute-start | bytes 245768 | tf_op jit(solution)/shard_map/ppermute | solution.py:20
  16.9 1.3 %collective-permute-start.3 = (f32[64,128]{1,0:T(8,128)S(1)}, f32[64,128]{1,0:T(8,128)S(1)}, u32[]{:S(2)}, u32[]{:S(2)}) collective-permute-start(f32[64,128]{1,0:T(8,128)S(1)} %get-tuple-element.28), channel_id=1, source_target_pairs={{0,4},{1,5},{2,6},{3,7},{4,0},{5,1},{6,2},{7,3},{8,12},{9,13},{10,... | collective-permute-start | bytes 98312 | tf_op jit(solution)/shard_map/ppermute | solution.py:20
  18.2 3.3 %collective-permute-start.4 = (f32[64,128]{1,0:T(8,128)S(1)}, f32[64,128]{1,0:T(8,128)S(1)}, u32[]{:S(2)}, u32[]{:S(2)}) collective-permute-start(f32[64,128]{1,0:T(8,128)S(1)} %add.6), channel_id=1, source_target_pairs={{0,5},{1,4},{2,7},{3,6},{4,1},{5,0},{6,3},{7,2},{8,13},{9,12},{10,... | collective-permute-start | bytes 98312 | tf_op jit(solution)/shard_map/ppermute | solution.py:20
  21.6 4.2 %collective-permute-start.7 = (f32[64,128]{1,0:T(8,128)S(1)}, f32[64,128]{1,0:T(8,128)S(1)}, u32[]{:S(2)}, u32[]{:S(2)}) collective-permute-start(f32[64,128]{1,0:T(8,128)S(1)} %add.7.own), channel_id=1, source_target_pairs={{0,28},{1,29},{2,30},{3,31},{4,24},{5,25},{6,26},{7,27},{8,20},{9,... | collective-permute-start | bytes 98312 | tf_op jit(solution)/shard_map/ppermute | solution.py:20
  23.9 3.3 %collective-permute-start.6 = (f32[64,128]{1,0:T(8,128)S(1)}, f32[64,128]{1,0:T(8,128)S(1)}, u32[]{:S(2)}, u32[]{:S(2)}) collective-permute-start(f32[64,128]{1,0:T(8,128)S(1)} %add.7.own), channel_id=1, source_target_pairs={{0,20},{1,21},{2,22},{3,23},{4,16},{5,17},{6,18},{7,19},{8,28},{9,... | collective-permute-start | bytes 98312 | tf_op jit(solution)/shard_map/ppermute | solution.py:20
  24.2 3.3 %collective-permute-start.5 = (f32[64,128]{1,0:T(8,128)S(1)}, f32[64,128]{1,0:T(8,128)S(1)}, u32[]{:S(2)}, u32[]{:S(2)}) collective-permute-start(f32[64,128]{1,0:T(8,128)S(1)} %add.7.own), channel_id=1, source_target_pairs={{0,12},{1,13},{2,14},{3,15},{4,8},{5,9},{6,10},{7,11},{8,4},{9,5},... | collective-permute-start | bytes 98312 | tf_op jit(solution)/shard_map/ppermute | solution.py:20

commit v5 on v4

--- a/solution.py
+++ b/solution.py
@@ -82,7 +82,8 @@
 def sketch_terms(side, freq, table, omega, lam):
     scale = jnp.concatenate([freq] * (lam.shape[1] // LANES), axis=1) - lam
     loewner = dot(side, table, 1, 0) / scale
-    return sum(dot(piece, omega, 1, 1) for piece in pieces(loewner))
+    terms = dot(jnp.concatenate(pieces(loewner), axis=0), omega, 1, 1)
+    return sum(jnp.split(terms, 3, axis=0))
 
 
 def local_body(*refs):
@@ -99,28 +100,34 @@
     cross[...] = dot(omega, table[K:, :], 1, 1)
 
 
+def remote_body(*refs):
+    side, freq, right, total_in, cross_in, table_out, omega_out, total, cross = refs
+    table, omega = right_side(right)
+    table_out[...] = table
+    omega_out[...] = omega
+    for q in range(side.shape[0] // LANES):
+        span = slice(q * LANES, (q + 1) * LANES)
+        total[span, :] = total_in[span, :] + sketch_terms(side[span, :], freq[span, :], table, omega, right[K : K + 1, :])
+    cross[...] = cross_in[...] + dot(omega, table[K:, :], 1, 1)
+
+
 def sketch_body(distance, *refs):
     count = (len(refs) - 11) // 2
     owns, gots = refs[:count], refs[count : 2 * count]
-    right, other, side_in, freq_in, table_in, omega_in, total_in, cross_in, pay, freq_row, port_row = refs[2 * count :]
-    table, omega = right_side(other)
-    near, far = right[K : K + 1, :], other[K : K + 1, :]
+    near, far, near_table, near_omega, far_table, far_omega, total, cross, pay, freq_row, port_row = refs[2 * count :]
+    table = jnp.concatenate([near_table[...], far_table[...]], axis=1)
+    omega = jnp.concatenate([near_omega[...], far_omega[...]], axis=1)
+    lam = jnp.concatenate([near[K : K + 1, :], far[K : K + 1, :]], axis=1)
     here = lax.rem(lax.div(lax.axis_index("blk"), distance), 2) == 0
     for q in range(count):
-        span = slice(q * LANES, (q + 1) * LANES)
-        side, freq = left_side(gots[q])
-        both = sketch_terms(
-            jnp.concatenate([side_in[span, :], side], axis=0), jnp.concatenate([freq_in[span, :], freq], axis=0), table, omega, far
-        )
-        own = (both[:LANES, :] + total_in[span, :]).T
-        got = (both[LANES:, :] + sketch_terms(side, freq, table_in[...], omega_in[...], near)).T
+        own = total[q * LANES : (q + 1) * LANES, :].T
+        got = sketch_terms(*left_side(gots[q]), table, omega, lam).T
         for place, flip in ((q, False), (count + q, True)):
             spot = slice(place * K, (place + 1) * K)
             pay[spot, :] = jnp.where(here != flip, own, got)
             for out, row in ((freq_row, K), (port_row, K + 1)):
                 out[place : place + 1, :] = jnp.where(here != flip, owns[q][row : row + 1, :], gots[q][row : row + 1, :])
-    cross = cross_in[...] + dot(omega, table[K:, :], 1, 1)
-    pay[2 * count * K :, :] = jnp.concatenate([cross[: K // 2], cross[K // 2 :]], axis=1)
+    pay[2 * count * K :, :] = jnp.concatenate([cross[: K // 2, :], cross[K // 2 :, :]], axis=1)
 
 
 def moments_body(own, other, freq, ports, gc, full):
@@ -197,9 +204,9 @@
     gc = ((own[...] + first[...]) + (second[...] + third[...])) * scale
     inverse = inverse_factor(gc, spread)
     mine = pl.multiple_of(lax.div(lax.axis_index("blk"), 2) * K, K)
-    basis[...] = dot(inverse, sketch[pl.ds(mine, K), :], 1, 0, HIGHEST)
-    coefficient = dot(inverse, gc[:, K:], 1, 0, HIGHEST)
-    projected[...] = dot(inverse, coefficient, 0, 0, HIGHEST)
+    both = dot(inverse, jnp.concatenate([sketch[pl.ds(mine, K), :], gc[:, K:]], axis=1), 1, 0, HIGHEST)
+    basis[...] = both[:, :LANES]
+    projected[...] = dot(inverse, both[:, LANES:], 0, 0, HIGHEST)
 
 
 def per_device(left_points, left_ports, left_values, right_points, right_ports, right_values, sketch_block, sketch_weight):
@@ -257,6 +264,17 @@
         ),
         (*lefts, right),
     )
+    side, freq, table, omega, total, cross = local
+    far_table, far_omega, total, cross = kernel_call(
+        remote_body,
+        (
+            jax.ShapeDtypeStruct(table.shape, table.dtype),
+            jax.ShapeDtypeStruct(omega.shape, omega.dtype),
+            jax.ShapeDtypeStruct(total.shape, f32),
+            jax.ShapeDtypeStruct(cross.shape, f32),
+        ),
+        (side, freq, other, total, cross),
+    )
     pay, freq, ports = kernel_call(
         functools.partial(sketch_body, distance),
         (
@@ -264,7 +282,7 @@
             jax.ShapeDtypeStruct((held, LANES), f32),
             jax.ShapeDtypeStruct((held, LANES), f32),
         ),
-        (*lefts, *got, right, other, *local),
+        (*lefts, *got, right, other, table, omega, far_table, far_omega, total, cross),
     )
     step = 2
     while step < distance:
@@ -283,7 +301,9 @@
     for hop in hops[:-2]:
         gc = gc + swap(gc, *hop)
     (b0, w0), (b1, w1) = hops[-2:]
-    parts = (gc, swap(gc, b0, w0), swap(gc, b1, w1), swap(gc, b0 ^ b1, w0 ^ w1 ^ 1))
+    parts = [gc]
+    for b, w in ((b0, w0), (b1, w1), (b0 ^ b1, w0 ^ w1 ^ 1)):
+        parts.append(swap(gc, b, w))
     basis, projected = kernel_call(
         functools.partial(finish_body, 1.0 / (rows * blk * wide)),
         (jax.ShapeDtypeStruct((K, rows), f32), jax.ShapeDtypeStruct((K, K), f32)),

time: 30.2 us -> 30.9 us (1.023)
  waiting for transfers between devices: 10.7 us -> 11.3 us
    ppermute x8, waiting for transfers between devices: 10.7 us -> 11.3 us  [swap(): return lax.ppermute(value, ('wide', 'blk'), pairs)]
    pallas_call x5 -> x6, Pallas kernels: 5.31 us -> 5.43 us  [kernel_call(): pl.pallas_call(body, out_shape=out_shape, compiler_params=pltpu.CompilerP...]
  transfers between devices with their start and end apart: 8 -> 8, of which waited for: 7 -> 8; matrix products, arithmetic and copies ran while one was open for 0% -> 0% of each run, Pallas kernels for 2% -> 3%
where the time goes in v5:
time: 30.9 us; the launch traced here: 30.8 us
  starting transfers between devices  13.3 us (43%)
  waiting for transfers between devices  11.3 us (37%)
  Pallas kernels  5.43 us (18%)
  between operations  0.68 us (2%)
    ppermute x8, starting transfers between devices, swap(): return lax.ppermute(value, ('wide', 'blk'), pairs)  13.3 us
    ppermute x8, waiting for transfers between devices, swap(): return lax.ppermute(value, ('wide', 'blk'), pairs)  11.3 us
    pallas_call x6, Pallas kernels, kernel_call(): pl.pallas_call(body, out_shape=out_shape, compiler_params=pltpu.CompilerP...  5.43 us
  transfers between devices with their start and end apart: 8, of which 8 were waited for; matrix products, arithmetic and copies ran while one was open for 0% of the time, Pallas kernels for 3%

profile of v5, /device:TPU:0, one launch (start us, length us, event | category | flops | bytes accessed | tf_op | source)
XLA Modules:
  0.0 30.8 jit_solution(17605901180816501860)
XLA Ops:
  0.6 1.0 %shard_map.95 = (f32[72,128]{1,0:T(8,128)S(1)}, f32[72,512]{1,0:T(8,128)S(1)}) custom-call(f32[1,128]{1,0:T(1,128)} %bitcast.15, s32[1,128]{1,0:T(1,128)} %bitcast.16, bf16[64,128]{1,0:T(8,128)(2,1)} %bitcast.10, f32[4,128]{1,0:T(4,128)} %bitcast.11, s32[4,128]{1,0:T(4,128)} %bitcast.12, bf16[64,512]{1,0:T(8,128)(2,1)} %bitcast.9, s32[4,128]{1,0:T(4,128)} %bitcast.13, ...), custom_call_target="tpu_custom_call" | custom-call | tf_op jit(solution)/shard_map/pallas_call | solution.py:24
  1.7 3.1 %collective-permute-start.1 = (f32[72,512]{1,0:T(8,128)S(1)}, f32[72,512]{1,0:T(8,128)S(1)}, u32[]{:S(2)}, u32[]{:S(2)}) collective-permute-start(f32[72,512]{1,0:T(8,128)S(1)} %get-tuple-element.22.refs_1_.refs_2_), channel_id=1, source_target_pairs={{0,1},{1,0},{2,3},{3,2},{4,5},{5,4},{6,7},{7,6},{8,9},{9,8},{10,11... | collective-permute-start | bytes 442376 | tf_op jit(solution)/shard_map/ppermute | solution.py:20
  4.8 2.6 %collective-permute-start = (f32[72,128]{1,0:T(8,128)S(1)}, f32[72,128]{1,0:T(8,128)S(1)}, u32[]{:S(2)}, u32[]{:S(2)}) collective-permute-start(f32[72,128]{1,0:T(8,128)S(1)} %get-tuple-element.21.refs_0_), channel_id=1, source_target_pairs={{0,2},{1,3},{2,0},{3,1},{4,6},{5,7},{6,4},{7,5},{8,10},{9,11},{10,... | collective-permute-start | bytes 110600 | tf_op jit(solution)/shard_map/ppermute | solution.py:20
  7.4 0.5 %shard_map.96 = (bf16[128,128]{1,0:T(8,128)(2,1)S(1)}, f32[128,128]{1,0:T(8,128)S(1)}, bf16[128,512]{1,0:T(8,128)(2,1)S(1)}, bf16[64,512]{1,0:T(8,128)(2,1)S(1)}...) custom-call(f32[72,128]{1,0:T(8,128)S(1)} %get-tuple-element.21.refs_0_, f32[72,512]{1,0:T(8,128)S(1)} %get-tuple-element.22.refs_1_.refs_2_), custom_call_target="tpu_custom_call" | custom-call | tf_op jit(solution)/shard_map/pallas_call | solution.py:24
  7.8 1.2 %collective-permute-done.1.refs_2_.refs_3_ = f32[72,512]{1,0:T(8,128)S(1)} collective-permute-done((f32[72,512]{1,0:T(8,128)S(1)}, f32[72,512]{1,0:T(8,128)S(1)}, u32[]{:S(2)}, u32[]{:S(2)}) %collective-permute-start.1) | collective-permute-done | bytes 147488 | tf_op jit(solution)/shard_map/ppermute | solution.py:20
  9.0 0.4 %shard_map.97 = (bf16[128,512]{1,0:T(8,128)(2,1)S(1)}, bf16[64,512]{1,0:T(8,128)(2,1)S(1)}, f32[128,64]{1,0:T(8,128)S(1)}, f32[64,64]{1,0:T(8,128)S(1)}) custom-call(bf16[128,128]{1,0:T(8,128)(2,1)S(1)} %get-tuple-element.25.refs_0_, f32[128,128]{1,0:T(8,128)S(1)} %get-tuple-element.26.refs_1_, f32[72,512]{1,0:T(8,128)S(1)} %collective-permute-done.1.refs_2_.refs_3_, ...), custom_call_target="tpu_custom_call" | custom-call | tf_op jit(solution)/shard_map/pallas_call | solution.py:24
  9.4 0.2 collective-permute-done.refs_1_
  9.6 0.6 %shard_map.98 = (f32[160,128]{1,0:T(8,128)S(1)}, f32[2,128]{1,0:T(2,128)S(1)}, f32[2,128]{1,0:T(2,128)S(1)}) custom-call(f32[72,128]{1,0:T(8,128)S(1)} %get-tuple-element.21.refs_0_, f32[72,128]{1,0:T(8,128)S(1)} %collective-permute-done.refs_1_, f32[72,512]{1,0:T(8,128)S(1)} %get-tuple-element.22.refs_1_.refs_2_, ...), custom_call_target="tpu_custom_call" | custom-call | tf_op jit(solution)/shard_map/pallas_call | solution.py:24
  10.3 2.7 %collective-permute-start.2 = (f32[160,128]{1,0:T(8,128)S(1)}, f32[160,128]{1,0:T(8,128)S(1)}, u32[]{:S(2)}, u32[]{:S(2)}) collective-permute-start(f32[160,128]{1,0:T(8,128)S(1)} %get-tuple-element.33.own), channel_id=1, source_target_pairs={{0,2},{1,3},{2,0},{3,1},{4,6},{5,7},{6,4},{7,5},{8,10},{9,11},{10,... | collective-permute-start | bytes 245768 | tf_op jit(solution)/shard_map/ppermute | solution.py:20
  12.9 3.3 %collective-permute-done.2.other = f32[160,128]{1,0:T(8,128)S(1)} collective-permute-done((f32[160,128]{1,0:T(8,128)S(1)}, f32[160,128]{1,0:T(8,128)S(1)}, u32[]{:S(2)}, u32[]{:S(2)}) %collective-permute-start.2) | collective-permute-done | bytes 81952 | tf_op jit(solution)/shard_map/ppermute | solution.py:20
  16.2 0.5 %shard_map.99 = (f32[64,128]{1,0:T(8,128)S(1)}, f32[128,128]{1,0:T(8,128)S(1)}) custom-call(f32[160,128]{1,0:T(8,128)S(1)} %get-tuple-element.33.own, f32[160,128]{1,0:T(8,128)S(1)} %collective-permute-done.2.other, f32[2,128]{1,0:T(2,128)S(1)} %get-tuple-element.34.freq, f32[2,128]{1,0:T(2,128)S(1)} %get-tuple-element.35.ports), custom_call_target="tpu_custom_call" | custom-call | tf_op jit(solution)/shard_map/pallas_call | solution.py:24
  16.7 0.1 collective-permute-start.3
  16.8 1.2 %collective-permute-done.3 = f32[64,128]{1,0:T(8,128)S(1)} collective-permute-done((f32[64,128]{1,0:T(8,128)S(1)}, f32[64,128]{1,0:T(8,128)S(1)}, u32[]{:S(2)}, u32[]{:S(2)}) %collective-permute-start.3) | collective-permute-done | bytes 32800 | tf_op jit(solution)/shard_map/ppermute | solution.py:20
  18.0 1.7 %collective-permute-start.4 = (f32[64,128]{1,0:T(8,128)S(1)}, f32[64,128]{1,0:T(8,128)S(1)}, u32[]{:S(2)}, u32[]{:S(2)}) collective-permute-start(f32[64,128]{1,0:T(8,128)S(1)} %add.6), channel_id=1, source_target_pairs={{0,5},{1,4},{2,7},{3,6},{4,1},{5,0},{6,3},{7,2},{8,13},{9,12},{10,... | collective-permute-start | bytes 98312 | tf_op jit(solution)/shard_map/ppermute | solution.py:20
  19.7 1.6 %collective-permute-done.4 = f32[64,128]{1,0:T(8,128)S(1)} collective-permute-done((f32[64,128]{1,0:T(8,128)S(1)}, f32[64,128]{1,0:T(8,128)S(1)}, u32[]{:S(2)}, u32[]{:S(2)}) %collective-permute-start.4) | collective-permute-done | bytes 32800 | tf_op jit(solution)/shard_map/ppermute | solution.py:20
  21.3 1.4 %collective-permute-start.5 = (f32[64,128]{1,0:T(8,128)S(1)}, f32[64,128]{1,0:T(8,128)S(1)}, u32[]{:S(2)}, u32[]{:S(2)}) collective-permute-start(f32[64,128]{1,0:T(8,128)S(1)} %add.7.own), channel_id=1, source_target_pairs={{0,12},{1,13},{2,14},{3,15},{4,8},{5,9},{6,10},{7,11},{8,4},{9,5},... | collective-permute-start | bytes 98312 | tf_op jit(solution)/shard_map/ppermute | solution.py:20
  22.8 1.3 %collective-permute-start.6 = (f32[64,128]{1,0:T(8,128)S(1)}, f32[64,128]{1,0:T(8,128)S(1)}, u32[]{:S(2)}, u32[]{:S(2)}) collective-permute-start(f32[64,128]{1,0:T(8,128)S(1)} %add.7.own), channel_id=1, source_target_pairs={{0,20},{1,21},{2,22},{3,23},{4,16},{5,17},{6,18},{7,19},{8,28},{9,... | collective-permute-start | bytes 98312 | tf_op jit(solution)/shard_map/ppermute | solution.py:20
  24.0 0.4 %collective-permute-start.7 = (f32[64,128]{1,0:T(8,128)S(1)}, f32[64,128]{1,0:T(8,128)S(1)}, u32[]{:S(2)}, u32[]{:S(2)}) collective-permute-start(f32[64,128]{1,0:T(8,128)S(1)} %add.7.own), channel_id=1, source_target_pairs={{0,28},{1,29},{2,30},{3,31},{4,24},{5,25},{6,26},{7,27},{8,20},{9,... | collective-permute-start | bytes 98312 | tf_op jit(solution)/shard_map/ppermute | solution.py:20
  24.5 0.2 collective-permute-done.5.first
  24.7 1.5 %collective-permute-done.6.second = f32[64,128]{1,0:T(8,128)S(1)} collective-permute-done((f32[64,128]{1,0:T(8,128)S(1)}, f32[64,128]{1,0:T(8,128)S(1)}, u32[]{:S(2)}, u32[]{:S(2)}) %collective-permute-start.6) | collective-permute-done | bytes 32800 | tf_op jit(solution)/shard_map/ppermute | solution.py:20
  26.1 2.2 %collective-permute-done.7.third = f32[64,128]{1,0:T(8,128)S(1)} collective-permute-done((f32[64,128]{1,0:T(8,128)S(1)}, f32[64,128]{1,0:T(8,128)S(1)}, u32[]{:S(2)}, u32[]{:S(2)}) %collective-permute-start.7) | collective-permute-done | bytes 32800 | tf_op jit(solution)/shard_map/ppermute | solution.py:20
  28.3 2.5 %shard_map.100 = (f32[64,128]{1,0:T(8,128)}, f32[64,64]{1,0:T(8,128)}) custom-call(f32[64,128]{1,0:T(8,128)S(1)} %add.7.own, f32[64,128]{1,0:T(8,128)S(1)} %collective-permute-done.5.first, f32[64,128]{1,0:T(8,128)S(1)} %collective-permute-done.6.second, f32[64,128]{1,0:T(8,128)S(1)} %collective-permute-done.7.third, f32[128,128]{1,0:T(8,128)S(1)} %get-tuple-element.37.sketch), custom_call_target="tpu_custom_call" | custom-call | tf_op jit(solution)/shard_map/pallas_call | solution.py:24
  (2 shorter events, 0.0 us)
Async XLA Ops:
  1.7 7.4 %collective-permute-start.1 = (f32[72,512]{1,0:T(8,128)S(1)}, f32[72,512]{1,0:T(8,128)S(1)}, u32[]{:S(2)}, u32[]{:S(2)}) collective-permute-start(f32[72,512]{1,0:T(8,128)S(1)} %get-tuple-element.22.refs_1_.refs_2_), channel_id=1, source_target_pairs={{0,1},{1,0},{2,3},{3,2},{4,5},{5,4},{6,7},{7,6},{8,9},{9,8},{10,11... | collective-permute-start | bytes 442376 | tf_op jit(solution)/shard_map/ppermute | solution.py:20
  4.8 4.9 %collective-permute-start = (f32[72,128]{1,0:T(8,128)S(1)}, f32[72,128]{1,0:T(8,128)S(1)}, u32[]{:S(2)}, u32[]{:S(2)}) collective-permute-start(f32[72,128]{1,0:T(8,128)S(1)} %get-tuple-element.21.refs_0_), channel_id=1, source_target_pairs={{0,2},{1,3},{2,0},{3,1},{4,6},{5,7},{6,4},{7,5},{8,10},{9,11},{10,... | collective-permute-start | bytes 110600 | tf_op jit(solution)/shard_map/ppermute | solution.py:20
  10.3 6.0 %collective-permute-start.2 = (f32[160,128]{1,0:T(8,128)S(1)}, f32[160,128]{1,0:T(8,128)S(1)}, u32[]{:S(2)}, u32[]{:S(2)}) collective-permute-start(f32[160,128]{1,0:T(8,128)S(1)} %get-tuple-element.33.own), channel_id=1, source_target_pairs={{0,2},{1,3},{2,0},{3,1},{4,6},{5,7},{6,4},{7,5},{8,10},{9,11},{10,... | collective-permute-start | bytes 245768 | tf_op jit(solution)/shard_map/ppermute | solution.py:20
  16.7 1.3 %collective-permute-start.3 = (f32[64,128]{1,0:T(8,128)S(1)}, f32[64,128]{1,0:T(8,128)S(1)}, u32[]{:S(2)}, u32[]{:S(2)}) collective-permute-start(f32[64,128]{1,0:T(8,128)S(1)} %get-tuple-element.36), channel_id=1, source_target_pairs={{0,4},{1,5},{2,6},{3,7},{4,0},{5,1},{6,2},{7,3},{8,12},{9,13},{10,... | collective-permute-start | bytes 98312 | tf_op jit(solution)/shard_map/ppermute | solution.py:20
  18.0 3.3 %collective-permute-start.4 = (f32[64,128]{1,0:T(8,128)S(1)}, f32[64,128]{1,0:T(8,128)S(1)}, u32[]{:S(2)}, u32[]{:S(2)}) collective-permute-start(f32[64,128]{1,0:T(8,128)S(1)} %add.6), channel_id=1, source_target_pairs={{0,5},{1,4},{2,7},{3,6},{4,1},{5,0},{6,3},{7,2},{8,13},{9,12},{10,... | collective-permute-start | bytes 98312 | tf_op jit(solution)/shard_map/ppermute | solution.py:20
  21.3 3.3 %collective-permute-start.5 = (f32[64,128]{1,0:T(8,128)S(1)}, f32[64,128]{1,0:T(8,128)S(1)}, u32[]{:S(2)}, u32[]{:S(2)}) collective-permute-start(f32[64,128]{1,0:T(8,128)S(1)} %add.7.own), channel_id=1, source_target_pairs={{0,12},{1,13},{2,14},{3,15},{4,8},{5,9},{6,10},{7,11},{8,4},{9,5},... | collective-permute-start | bytes 98312 | tf_op jit(solution)/shard_map/ppermute | solution.py:20
  22.8 3.3 %collective-permute-start.6 = (f32[64,128]{1,0:T(8,128)S(1)}, f32[64,128]{1,0:T(8,128)S(1)}, u32[]{:S(2)}, u32[]{:S(2)}) collective-permute-start(f32[64,128]{1,0:T(8,128)S(1)} %add.7.own), channel_id=1, source_target_pairs={{0,20},{1,21},{2,22},{3,23},{4,16},{5,17},{6,18},{7,19},{8,28},{9,... | collective-permute-start | bytes 98312 | tf_op jit(solution)/shard_map/ppermute | solution.py:20
  24.0 4.2 %collective-permute-start.7 = (f32[64,128]{1,0:T(8,128)S(1)}, f32[64,128]{1,0:T(8,128)S(1)}, u32[]{:S(2)}, u32[]{:S(2)}) collective-permute-start(f32[64,128]{1,0:T(8,128)S(1)} %add.7.own), channel_id=1, source_target_pairs={{0,28},{1,29},{2,30},{3,31},{4,24},{5,25},{6,26},{7,27},{8,20},{9,... | collective-permute-start | bytes 98312 | tf_op jit(solution)/shard_map/ppermute | solution.py:20

commit v6 on v5

--- a/solution.py
+++ b/solution.py
@@ -45,24 +45,27 @@
 def pack_body(*refs):
     sources, (left, right), held, sems = refs[:8], refs[8:10], refs[10:18], refs[18]
     copies = [pltpu.make_async_copy(a, b, sems.at[i]) for i, (a, b) in enumerate(zip(sources, held))]
-    for copy in copies:
-        copy.start()
+    for i in (5, 2, 0, 1, 3, 4, 6, 7):
+        copies[i].start()
     mu, lp, lv, lam, rp, rv, col, w = held
     left[K + 2 :, :] = jnp.zeros((left.shape[0] - K - 2, LANES), jnp.float32)
-    right[K + 4 :, :] = jnp.zeros((right.shape[0] - K - 4, right.shape[1]), jnp.float32)
     for copy in copies:
         copy.wait()
     left[:K, :] = lv[...].astype(jnp.float32)
     left[K : K + 1, :] = mu[...]
     left[K + 1 : K + 2, :] = lp[...].astype(jnp.float32)
-    right[:K, :] = rv[...].astype(jnp.float32)
-    weights = w[...].astype(jnp.float32)
-    for s in range(lam.shape[0]):
-        lanes = pl.ds(s * LANES, LANES)
-        right[K : K + 1, lanes] = lam[s : s + 1, :]
-        right[K + 1 : K + 2, lanes] = rp[s : s + 1, :].astype(jnp.float32)
-        right[K + 2 : K + 3, lanes] = col[s : s + 1, :].astype(jnp.float32)
-        right[K + 3 : K + 4, lanes] = weights[s : s + 1, :]
+    count = lam.shape[0]
+    for s in range(count):
+        right[s * K : (s + 1) * K, :] = rv[:, s * LANES : (s + 1) * LANES].astype(jnp.float32)
+    for place, rows in enumerate((lam, rp, col, w)):
+        right[count * K + place * count : count * K + (place + 1) * count, :] = rows[...].astype(jnp.float32)
+
+
+def of_right(right):
+    count = right.shape[0] // (K + 4)
+    values = jnp.concatenate([right[s * K : (s + 1) * K, :] for s in range(count)], axis=1)
+    rows = [jnp.concatenate([right[count * K + p * count + s : count * K + p * count + s + 1, :] for s in range(count)], axis=1) for p in range(4)]
+    return values, *rows
 
 
 def left_side(left):
@@ -73,10 +76,10 @@
 
 
 def right_side(right):
-    index = lax.broadcasted_iota(jnp.int32, (K, right.shape[1]), 0).astype(jnp.float32)
-    pick = jnp.where(right[K + 1 : K + 2, :] == index, 1.0, 0.0)
-    table = jnp.concatenate([pick, right[:K, :]], axis=0).astype(jnp.bfloat16)
-    return table, jnp.where(right[K + 2 : K + 3, :] == index, right[K + 3 : K + 4, :], 0.0).astype(jnp.bfloat16)
+    values, lam, ports, columns, weights = of_right(right)
+    index = lax.broadcasted_iota(jnp.int32, values.shape, 0).astype(jnp.float32)
+    table = jnp.concatenate([jnp.where(ports == index, 1.0, 0.0), values], axis=0).astype(jnp.bfloat16)
+    return table, jnp.where(columns == index, weights, 0.0).astype(jnp.bfloat16), lam
 
 
 def sketch_terms(side, freq, table, omega, lam):
@@ -88,7 +91,7 @@
 
 def local_body(*refs):
     lefts, (right, side_out, freq_out, table_out, omega_out, total, cross) = refs[:-7], refs[-7:]
-    table, omega = right_side(right)
+    table, omega, lam = right_side(right)
     table_out[...] = table
     omega_out[...] = omega
     for q, left in enumerate(lefts):
@@ -96,18 +99,18 @@
         side, freq = left_side(left)
         side_out[span, :] = side
         freq_out[span, :] = freq
-        total[span, :] = sketch_terms(side, freq, table, omega, right[K : K + 1, :])
+        total[span, :] = sketch_terms(side, freq, table, omega, lam)
     cross[...] = dot(omega, table[K:, :], 1, 1)
 
 
 def remote_body(*refs):
     side, freq, right, total_in, cross_in, table_out, omega_out, total, cross = refs
-    table, omega = right_side(right)
+    table, omega, lam = right_side(right)
     table_out[...] = table
     omega_out[...] = omega
     for q in range(side.shape[0] // LANES):
         span = slice(q * LANES, (q + 1) * LANES)
-        total[span, :] = total_in[span, :] + sketch_terms(side[span, :], freq[span, :], table, omega, right[K : K + 1, :])
+        total[span, :] = total_in[span, :] + sketch_terms(side[span, :], freq[span, :], table, omega, lam)
     cross[...] = cross_in[...] + dot(omega, table[K:, :], 1, 1)
 
 
@@ -117,7 +120,7 @@
     near, far, near_table, near_omega, far_table, far_omega, total, cross, pay, freq_row, port_row = refs[2 * count :]
     table = jnp.concatenate([near_table[...], far_table[...]], axis=1)
     omega = jnp.concatenate([near_omega[...], far_omega[...]], axis=1)
-    lam = jnp.concatenate([near[K : K + 1, :], far[K : K + 1, :]], axis=1)
+    lam = jnp.concatenate([of_right(near)[1], of_right(far)[1]], axis=1)
     here = lax.rem(lax.div(lax.axis_index("blk"), distance), 2) == 0
     for q in range(count):
         own = total[q * LANES : (q + 1) * LANES, :].T
@@ -216,7 +219,7 @@
     along = (rights // LANES, LANES)
     left, right = kernel_call(
         pack_body,
-        (jax.ShapeDtypeStruct((K + SUB, LANES), f32), jax.ShapeDtypeStruct((K + SUB, rights), f32)),
+        (jax.ShapeDtypeStruct((K + SUB, LANES), f32), jax.ShapeDtypeStruct(((K + 4) * along[0], LANES), f32)),
         tuple(pltpu.with_memory_space_constraint(v, pltpu.HBM) for v in (
             left_points.reshape(1, rows),
             left_ports.reshape(1, rows),

time: 30.9 us -> 30.7 us (level)
  no operation moved by 1% of the time
where the time goes in v6:
time: 30.7 us; the launch traced here: 30.5 us
  starting transfers between devices  13.2 us (43%)
  waiting for transfers between devices  11.3 us (37%)
  Pallas kernels  5.36 us (17%)
  between operations  0.68 us (2%)
    ppermute x8, starting transfers between devices, swap(): return lax.ppermute(value, ('wide', 'blk'), pairs)  13.2 us
    ppermute x8, waiting for transfers between devices, swap(): return lax.ppermute(value, ('wide', 'blk'), pairs)  11.3 us
    pallas_call x6, Pallas kernels, kernel_call(): pl.pallas_call(body, out_shape=out_shape, compiler_params=pltpu.CompilerP...  5.36 us
  transfers between devices with their start and end apart: 8, of which 8 were waited for; matrix products, arithmetic and copies ran while one was open for 0% of the time, Pallas kernels for 3%

profile of v6, /device:TPU:0, one launch (start us, length us, event | category | flops | bytes accessed | tf_op | source)
XLA Modules:
  0.0 30.5 jit_solution(852848201375061710)
XLA Ops:
  0.6 0.9 %shard_map.95 = (f32[72,128]{1,0:T(8,128)S(1)}, f32[272,128]{1,0:T(8,128)S(1)}) custom-call(f32[1,128]{1,0:T(1,128)} %bitcast.15, s32[1,128]{1,0:T(1,128)} %bitcast.16, bf16[64,128]{1,0:T(8,128)(2,1)} %bitcast.10, f32[4,128]{1,0:T(4,128)} %bitcast.11, s32[4,128]{1,0:T(4,128)} %bitcast.12, bf16[64,512]{1,0:T(8,128)(2,1)} %bitcast.9, s32[4,128]{1,0:T(4,128)} %bitcast.13, ...), custom_call_target="tpu_custom_call" | custom-call | tf_op jit(solution)/shard_map/pallas_call | solution.py:24
  1.6 3.1 %collective-permute-start.1 = (f32[272,128]{1,0:T(8,128)S(1)}, f32[272,128]{1,0:T(8,128)S(1)}, u32[]{:S(2)}, u32[]{:S(2)}) collective-permute-start(f32[272,128]{1,0:T(8,128)S(1)} %get-tuple-element.22.refs_1_.refs_2_), channel_id=1, source_target_pairs={{0,1},{1,0},{2,3},{3,2},{4,5},{5,4},{6,7},{7,6},{8,9},{9,8},{10,11... | collective-permute-start | bytes 417800 | tf_op jit(solution)/shard_map/ppermute | solution.py:20
  4.7 2.6 %collective-permute-start = (f32[72,128]{1,0:T(8,128)S(1)}, f32[72,128]{1,0:T(8,128)S(1)}, u32[]{:S(2)}, u32[]{:S(2)}) collective-permute-start(f32[72,128]{1,0:T(8,128)S(1)} %get-tuple-element.21.refs_0_), channel_id=1, source_target_pairs={{0,2},{1,3},{2,0},{3,1},{4,6},{5,7},{6,4},{7,5},{8,10},{9,11},{10,... | collective-permute-start | bytes 110600 | tf_op jit(solution)/shard_map/ppermute | solution.py:20
  7.3 0.5 %shard_map.96 = (bf16[128,128]{1,0:T(8,128)(2,1)S(1)}, f32[128,128]{1,0:T(8,128)S(1)}, bf16[128,512]{1,0:T(8,128)(2,1)S(1)}, bf16[64,512]{1,0:T(8,128)(2,1)S(1)}...) custom-call(f32[72,128]{1,0:T(8,128)S(1)} %get-tuple-element.21.refs_0_, f32[272,128]{1,0:T(8,128)S(1)} %get-tuple-element.22.refs_1_.refs_2_), custom_call_target="tpu_custom_call" | custom-call | tf_op jit(solution)/shard_map/pallas_call | solution.py:24
  7.7 1.0 %collective-permute-done.1.refs_2_.refs_3_ = f32[272,128]{1,0:T(8,128)S(1)} collective-permute-done((f32[272,128]{1,0:T(8,128)S(1)}, f32[272,128]{1,0:T(8,128)S(1)}, u32[]{:S(2)}, u32[]{:S(2)}) %collective-permute-start.1) | collective-permute-done | bytes 139296 | tf_op jit(solution)/shard_map/ppermute | solution.py:20
  8.8 0.4 %shard_map.97 = (bf16[128,512]{1,0:T(8,128)(2,1)S(1)}, bf16[64,512]{1,0:T(8,128)(2,1)S(1)}, f32[128,64]{1,0:T(8,128)S(1)}, f32[64,64]{1,0:T(8,128)S(1)}) custom-call(bf16[128,128]{1,0:T(8,128)(2,1)S(1)} %get-tuple-element.25.refs_0_, f32[128,128]{1,0:T(8,128)S(1)} %get-tuple-element.26.refs_1_, f32[272,128]{1,0:T(8,128)S(1)} %collective-permute-done.1.refs_2_.refs_3_, ...), custom_call_target="tpu_custom_call" | custom-call | tf_op jit(solution)/shard_map/pallas_call | solution.py:24
  9.2 0.5 %collective-permute-done.refs_1_ = f32[72,128]{1,0:T(8,128)S(1)} collective-permute-done((f32[72,128]{1,0:T(8,128)S(1)}, f32[72,128]{1,0:T(8,128)S(1)}, u32[]{:S(2)}, u32[]{:S(2)}) %collective-permute-start) | collective-permute-done | bytes 36896 | tf_op jit(solution)/shard_map/ppermute | solution.py:20
  9.7 0.6 %shard_map.98 = (f32[160,128]{1,0:T(8,128)S(1)}, f32[2,128]{1,0:T(2,128)S(1)}, f32[2,128]{1,0:T(2,128)S(1)}) custom-call(f32[72,128]{1,0:T(8,128)S(1)} %get-tuple-element.21.refs_0_, f32[72,128]{1,0:T(8,128)S(1)} %collective-permute-done.refs_1_, f32[272,128]{1,0:T(8,128)S(1)} %get-tuple-element.22.refs_1_.refs_2_, ...), custom_call_target="tpu_custom_call" | custom-call | tf_op jit(solution)/shard_map/pallas_call | solution.py:24
  10.3 2.5 %collective-permute-start.2 = (f32[160,128]{1,0:T(8,128)S(1)}, f32[160,128]{1,0:T(8,128)S(1)}, u32[]{:S(2)}, u32[]{:S(2)}) collective-permute-start(f32[160,128]{1,0:T(8,128)S(1)} %get-tuple-element.33.own), channel_id=1, source_target_pairs={{0,2},{1,3},{2,0},{3,1},{4,6},{5,7},{6,4},{7,5},{8,10},{9,11},{10,... | collective-permute-start | bytes 245768 | tf_op jit(solution)/shard_map/ppermute | solution.py:20
  12.8 3.1 %collective-permute-done.2.other = f32[160,128]{1,0:T(8,128)S(1)} collective-permute-done((f32[160,128]{1,0:T(8,128)S(1)}, f32[160,128]{1,0:T(8,128)S(1)}, u32[]{:S(2)}, u32[]{:S(2)}) %collective-permute-start.2) | collective-permute-done | bytes 81952 | tf_op jit(solution)/shard_map/ppermute | solution.py:20
  16.0 0.5 %shard_map.99 = (f32[64,128]{1,0:T(8,128)S(1)}, f32[128,128]{1,0:T(8,128)S(1)}) custom-call(f32[160,128]{1,0:T(8,128)S(1)} %get-tuple-element.33.own, f32[160,128]{1,0:T(8,128)S(1)} %collective-permute-done.2.other, f32[2,128]{1,0:T(2,128)S(1)} %get-tuple-element.34.freq, f32[2,128]{1,0:T(2,128)S(1)} %get-tuple-element.35.ports), custom_call_target="tpu_custom_call" | custom-call | tf_op jit(solution)/shard_map/pallas_call | solution.py:24
  16.4 0.1 collective-permute-start.3
  16.5 1.2 %collective-permute-done.3 = f32[64,128]{1,0:T(8,128)S(1)} collective-permute-done((f32[64,128]{1,0:T(8,128)S(1)}, f32[64,128]{1,0:T(8,128)S(1)}, u32[]{:S(2)}, u32[]{:S(2)}) %collective-permute-start.3) | collective-permute-done | bytes 32800 | tf_op jit(solution)/shard_map/ppermute | solution.py:20
  17.7 1.7 %collective-permute-start.4 = (f32[64,128]{1,0:T(8,128)S(1)}, f32[64,128]{1,0:T(8,128)S(1)}, u32[]{:S(2)}, u32[]{:S(2)}) collective-permute-start(f32[64,128]{1,0:T(8,128)S(1)} %add.6), channel_id=1, source_target_pairs={{0,5},{1,4},{2,7},{3,6},{4,1},{5,0},{6,3},{7,2},{8,13},{9,12},{10,... | collective-permute-start | bytes 98312 | tf_op jit(solution)/shard_map/ppermute | solution.py:20
  19.4 1.6 %collective-permute-done.4 = f32[64,128]{1,0:T(8,128)S(1)} collective-permute-done((f32[64,128]{1,0:T(8,128)S(1)}, f32[64,128]{1,0:T(8,128)S(1)}, u32[]{:S(2)}, u32[]{:S(2)}) %collective-permute-start.4) | collective-permute-done | bytes 32800 | tf_op jit(solution)/shard_map/ppermute | solution.py:20
  21.1 1.4 %collective-permute-start.5 = (f32[64,128]{1,0:T(8,128)S(1)}, f32[64,128]{1,0:T(8,128)S(1)}, u32[]{:S(2)}, u32[]{:S(2)}) collective-permute-start(f32[64,128]{1,0:T(8,128)S(1)} %add.7.own), channel_id=1, source_target_pairs={{0,12},{1,13},{2,14},{3,15},{4,8},{5,9},{6,10},{7,11},{8,4},{9,5},... | collective-permute-start | bytes 98312 | tf_op jit(solution)/shard_map/ppermute | solution.py:20
  22.5 1.3 %collective-permute-start.6 = (f32[64,128]{1,0:T(8,128)S(1)}, f32[64,128]{1,0:T(8,128)S(1)}, u32[]{:S(2)}, u32[]{:S(2)}) collective-permute-start(f32[64,128]{1,0:T(8,128)S(1)} %add.7.own), channel_id=1, source_target_pairs={{0,20},{1,21},{2,22},{3,23},{4,16},{5,17},{6,18},{7,19},{8,28},{9,... | collective-permute-start | bytes 98312 | tf_op jit(solution)/shard_map/ppermute | solution.py:20
  23.8 0.4 %collective-permute-start.7 = (f32[64,128]{1,0:T(8,128)S(1)}, f32[64,128]{1,0:T(8,128)S(1)}, u32[]{:S(2)}, u32[]{:S(2)}) collective-permute-start(f32[64,128]{1,0:T(8,128)S(1)} %add.7.own), channel_id=1, source_target_pairs={{0,28},{1,29},{2,30},{3,31},{4,24},{5,25},{6,26},{7,27},{8,20},{9,... | collective-permute-start | bytes 98312 | tf_op jit(solution)/shard_map/ppermute | solution.py:20
  24.2 0.2 collective-permute-done.5.first
  24.4 1.4 %collective-permute-done.6.second = f32[64,128]{1,0:T(8,128)S(1)} collective-permute-done((f32[64,128]{1,0:T(8,128)S(1)}, f32[64,128]{1,0:T(8,128)S(1)}, u32[]{:S(2)}, u32[]{:S(2)}) %collective-permute-start.6) | collective-permute-done | bytes 32800 | tf_op jit(solution)/shard_map/ppermute | solution.py:20
  25.8 2.2 %collective-permute-done.7.third = f32[64,128]{1,0:T(8,128)S(1)} collective-permute-done((f32[64,128]{1,0:T(8,128)S(1)}, f32[64,128]{1,0:T(8,128)S(1)}, u32[]{:S(2)}, u32[]{:S(2)}) %collective-permute-start.7) | collective-permute-done | bytes 32800 | tf_op jit(solution)/shard_map/ppermute | solution.py:20
  28.0 2.5 %shard_map.100 = (f32[64,128]{1,0:T(8,128)}, f32[64,64]{1,0:T(8,128)}) custom-call(f32[64,128]{1,0:T(8,128)S(1)} %add.7.own, f32[64,128]{1,0:T(8,128)S(1)} %collective-permute-done.5.first, f32[64,128]{1,0:T(8,128)S(1)} %collective-permute-done.6.second, f32[64,128]{1,0:T(8,128)S(1)} %collective-permute-done.7.third, f32[128,128]{1,0:T(8,128)S(1)} %get-tuple-element.37.sketch), custom_call_target="tpu_custom_call" | custom-call | tf_op jit(solution)/shard_map/pallas_call | solution.py:24
  (2 shorter events, 0.0 us)
Async XLA Ops:
  1.6 7.2 %collective-permute-start.1 = (f32[272,128]{1,0:T(8,128)S(1)}, f32[272,128]{1,0:T(8,128)S(1)}, u32[]{:S(2)}, u32[]{:S(2)}) collective-permute-start(f32[272,128]{1,0:T(8,128)S(1)} %get-tuple-element.22.refs_1_.refs_2_), channel_id=1, source_target_pairs={{0,1},{1,0},{2,3},{3,2},{4,5},{5,4},{6,7},{7,6},{8,9},{9,8},{10,11... | collective-permute-start | bytes 417800 | tf_op jit(solution)/shard_map/ppermute | solution.py:20
  4.7 5.0 %collective-permute-start = (f32[72,128]{1,0:T(8,128)S(1)}, f32[72,128]{1,0:T(8,128)S(1)}, u32[]{:S(2)}, u32[]{:S(2)}) collective-permute-start(f32[72,128]{1,0:T(8,128)S(1)} %get-tuple-element.21.refs_0_), channel_id=1, source_target_pairs={{0,2},{1,3},{2,0},{3,1},{4,6},{5,7},{6,4},{7,5},{8,10},{9,11},{10,... | collective-permute-start | bytes 110600 | tf_op jit(solution)/shard_map/ppermute | solution.py:20
  10.3 5.7 %collective-permute-start.2 = (f32[160,128]{1,0:T(8,128)S(1)}, f32[160,128]{1,0:T(8,128)S(1)}, u32[]{:S(2)}, u32[]{:S(2)}) collective-permute-start(f32[160,128]{1,0:T(8,128)S(1)} %get-tuple-element.33.own), channel_id=1, source_target_pairs={{0,2},{1,3},{2,0},{3,1},{4,6},{5,7},{6,4},{7,5},{8,10},{9,11},{10,... | collective-permute-start | bytes 245768 | tf_op jit(solution)/shard_map/ppermute | solution.py:20
  16.4 1.3 %collective-permute-start.3 = (f32[64,128]{1,0:T(8,128)S(1)}, f32[64,128]{1,0:T(8,128)S(1)}, u32[]{:S(2)}, u32[]{:S(2)}) collective-permute-start(f32[64,128]{1,0:T(8,128)S(1)} %get-tuple-element.36), channel_id=1, source_target_pairs={{0,4},{1,5},{2,6},{3,7},{4,0},{5,1},{6,2},{7,3},{8,12},{9,13},{10,... | collective-permute-start | bytes 98312 | tf_op jit(solution)/shard_map/ppermute | solution.py:20
  17.7 3.3 %collective-permute-start.4 = (f32[64,128]{1,0:T(8,128)S(1)}, f32[64,128]{1,0:T(8,128)S(1)}, u32[]{:S(2)}, u32[]{:S(2)}) collective-permute-start(f32[64,128]{1,0:T(8,128)S(1)} %add.6), channel_id=1, source_target_pairs={{0,5},{1,4},{2,7},{3,6},{4,1},{5,0},{6,3},{7,2},{8,13},{9,12},{10,... | collective-permute-start | bytes 98312 | tf_op jit(solution)/shard_map/ppermute | solution.py:20
  21.1 3.3 %collective-permute-start.5 = (f32[64,128]{1,0:T(8,128)S(1)}, f32[64,128]{1,0:T(8,128)S(1)}, u32[]{:S(2)}, u32[]{:S(2)}) collective-permute-start(f32[64,128]{1,0:T(8,128)S(1)} %add.7.own), channel_id=1, source_target_pairs={{0,12},{1,13},{2,14},{3,15},{4,8},{5,9},{6,10},{7,11},{8,4},{9,5},... | collective-permute-start | bytes 98312 | tf_op jit(solution)/shard_map/ppermute | solution.py:20
  22.5 3.3 %collective-permute-start.6 = (f32[64,128]{1,0:T(8,128)S(1)}, f32[64,128]{1,0:T(8,128)S(1)}, u32[]{:S(2)}, u32[]{:S(2)}) collective-permute-start(f32[64,128]{1,0:T(8,128)S(1)} %add.7.own), channel_id=1, source_target_pairs={{0,20},{1,21},{2,22},{3,23},{4,16},{5,17},{6,18},{7,19},{8,28},{9,... | collective-permute-start | bytes 98312 | tf_op jit(solution)/shard_map/ppermute | solution.py:20
  23.8 4.2 %collective-permute-start.7 = (f32[64,128]{1,0:T(8,128)S(1)}, f32[64,128]{1,0:T(8,128)S(1)}, u32[]{:S(2)}, u32[]{:S(2)}) collective-permute-start(f32[64,128]{1,0:T(8,128)S(1)} %add.7.own), channel_id=1, source_target_pairs={{0,28},{1,29},{2,30},{3,31},{4,24},{5,25},{6,26},{7,27},{8,20},{9,... | collective-permute-start | bytes 98312 | tf_op jit(solution)/shard_map/ppermute | solution.py:20

commit v7 on v6

--- a/solution.py
+++ b/solution.py
@@ -10,7 +10,6 @@
 K = 64
 LANES = 128
 SUB = 8
-HIGHEST = lax.Precision.HIGHEST
 VMEM_LIMIT = 8 << 20
 
 
@@ -40,6 +39,11 @@
     return lax.dot_general(
         a, b, (((ca,), (cb,)), ((), ())), precision=precision, preferred_element_type=jnp.float32
     )
+
+
+def product(a, b):
+    (h, m, l), (p, q, r) = pieces(a), pieces(b)
+    return dot(jnp.concatenate([l, m, h, m, h, h], axis=1), jnp.concatenate([p, q, r, p, q, p], axis=0), 1, 0)
 
 
 def pack_body(*refs):
@@ -85,8 +89,8 @@
 def sketch_terms(side, freq, table, omega, lam):
     scale = jnp.concatenate([freq] * (lam.shape[1] // LANES), axis=1) - lam
     loewner = dot(side, table, 1, 0) / scale
-    terms = dot(jnp.concatenate(pieces(loewner), axis=0), omega, 1, 1)
-    return sum(jnp.split(terms, 3, axis=0))
+    terms = dot(omega, jnp.concatenate(pieces(loewner), axis=0), 1, 1)
+    return sum(jnp.split(terms, 3, axis=1)[::-1])
 
 
 def local_body(*refs):
@@ -99,7 +103,7 @@
         side, freq = left_side(left)
         side_out[span, :] = side
         freq_out[span, :] = freq
-        total[span, :] = sketch_terms(side, freq, table, omega, lam)
+        total[:, span] = sketch_terms(side, freq, table, omega, lam)
     cross[...] = dot(omega, table[K:, :], 1, 1)
 
 
@@ -110,7 +114,7 @@
     omega_out[...] = omega
     for q in range(side.shape[0] // LANES):
         span = slice(q * LANES, (q + 1) * LANES)
-        total[span, :] = total_in[span, :] + sketch_terms(side[span, :], freq[span, :], table, omega, lam)
+        total[:, span] = total_in[:, span] + sketch_terms(side[span, :], freq[span, :], table, omega, lam)
     cross[...] = cross_in[...] + dot(omega, table[K:, :], 1, 1)
 
 
@@ -123,8 +127,8 @@
     lam = jnp.concatenate([of_right(near)[1], of_right(far)[1]], axis=1)
     here = lax.rem(lax.div(lax.axis_index("blk"), distance), 2) == 0
     for q in range(count):
-        own = total[q * LANES : (q + 1) * LANES, :].T
-        got = sketch_terms(*left_side(gots[q]), table, omega, lam).T
+        own = total[:, q * LANES : (q + 1) * LANES]
+        got = sketch_terms(*left_side(gots[q]), table, omega, lam)
         for place, flip in ((q, False), (count + q, True)):
             spot = slice(place * K, (place + 1) * K)
             pay[spot, :] = jnp.where(here != flip, own, got)
@@ -149,7 +153,12 @@
         sketches.append(sketch)
         shifts.append(shift)
     sketch = jnp.concatenate(sketches, axis=1)
-    gc[...] = dot(sketch, jnp.concatenate([sketch, jnp.concatenate(shifts, axis=1)], axis=0), 1, 1, HIGHEST)
+    h, m, l = pieces(sketch)
+    p, q, r = pieces(jnp.concatenate([sketch, jnp.concatenate(shifts, axis=1)], axis=0))
+    terms = jnp.split(dot(jnp.concatenate([l, m, h], axis=0), p, 1, 1), 3, axis=0)
+    terms += jnp.split(dot(jnp.concatenate([m, h], axis=0), q, 1, 1), 2, axis=0)
+    low = (terms[0] + terms[3]) + dot(h, r, 1, 1)
+    gc[...] = terms[2] + ((terms[1] + terms[4]) + low)
     full[...] = both[: n_left * K, :]
 
 
@@ -207,9 +216,9 @@
     gc = ((own[...] + first[...]) + (second[...] + third[...])) * scale
     inverse = inverse_factor(gc, spread)
     mine = pl.multiple_of(lax.div(lax.axis_index("blk"), 2) * K, K)
-    both = dot(inverse, jnp.concatenate([sketch[pl.ds(mine, K), :], gc[:, K:]], axis=1), 1, 0, HIGHEST)
+    both = product(inverse, jnp.concatenate([sketch[pl.ds(mine, K), :], gc[:, K:]], axis=1))
     basis[...] = both[:, :LANES]
-    projected[...] = dot(inverse, both[:, LANES:], 0, 0, HIGHEST)
+    projected[...] = product(inverse.T, both[:, LANES:])
 
 
 def per_device(left_points, left_ports, left_values, right_points, right_ports, right_values, sketch_block, sketch_weight):
@@ -262,7 +271,7 @@
             jax.ShapeDtypeStruct((count * LANES, LANES), f32),
             jax.ShapeDtypeStruct((2 * K, rights), jnp.bfloat16),
             jax.ShapeDtypeStruct((K, rights), jnp.bfloat16),
-            jax.ShapeDtypeStruct((count * LANES, K), f32),
+            jax.ShapeDtypeStruct((K, count * LANES), f32),
             jax.ShapeDtypeStruct((K, K), f32),
         ),
         (*lefts, right),

time: 30.7 us -> 30.5 us (level)
  no operation moved by 1% of the time
where the time goes in v7:
time: 30.5 us; the launch traced here: 30.3 us
  starting transfers between devices  13.2 us (43%)
  waiting for transfers between devices  11.2 us (37%)
  Pallas kernels  5.23 us (17%)
  between operations  0.69 us (2%)
    ppermute x8, starting transfers between devices, swap(): return lax.ppermute(value, ('wide', 'blk'), pairs)  13.2 us
    ppermute x8, waiting for transfers between devices, swap(): return lax.ppermute(value, ('wide', 'blk'), pairs)  11.2 us
    pallas_call x6, Pallas kernels, kernel_call(): pl.pallas_call(body, out_shape=out_shape, compiler_params=pltpu.CompilerP...  5.23 us
  transfers between devices with their start and end apart: 8, of which 8 were waited for; matrix products, arithmetic and copies ran while one was open for 0% of the time, Pallas kernels for 3%

profile of v7, /device:TPU:0, one launch (start us, length us, event | category | flops | bytes accessed | tf_op | source)
XLA Modules:
  0.0 30.3 jit_solution(5847787540845831955)
XLA Ops:
  0.6 0.9 %shard_map.95 = (f32[72,128]{1,0:T(8,128)S(1)}, f32[272,128]{1,0:T(8,128)S(1)}) custom-call(f32[1,128]{1,0:T(1,128)} %bitcast.15, s32[1,128]{1,0:T(1,128)} %bitcast.16, bf16[64,128]{1,0:T(8,128)(2,1)} %bitcast.10, f32[4,128]{1,0:T(4,128)} %bitcast.11, s32[4,128]{1,0:T(4,128)} %bitcast.12, bf16[64,512]{1,0:T(8,128)(2,1)} %bitcast.9, s32[4,128]{1,0:T(4,128)} %bitcast.13, ...), custom_call_target="tpu_custom_call" | custom-call | tf_op jit(solution)/shard_map/pallas_call | solution.py:23
  1.6 3.1 %collective-permute-start.1 = (f32[272,128]{1,0:T(8,128)S(1)}, f32[272,128]{1,0:T(8,128)S(1)}, u32[]{:S(2)}, u32[]{:S(2)}) collective-permute-start(f32[272,128]{1,0:T(8,128)S(1)} %get-tuple-element.22.refs_1_.refs_2_), channel_id=1, source_target_pairs={{0,1},{1,0},{2,3},{3,2},{4,5},{5,4},{6,7},{7,6},{8,9},{9,8},{10,11... | collective-permute-start | bytes 417800 | tf_op jit(solution)/shard_map/ppermute | solution.py:19
  4.7 2.6 %collective-permute-start = (f32[72,128]{1,0:T(8,128)S(1)}, f32[72,128]{1,0:T(8,128)S(1)}, u32[]{:S(2)}, u32[]{:S(2)}) collective-permute-start(f32[72,128]{1,0:T(8,128)S(1)} %get-tuple-element.21.refs_0_), channel_id=1, source_target_pairs={{0,2},{1,3},{2,0},{3,1},{4,6},{5,7},{6,4},{7,5},{8,10},{9,11},{10,... | collective-permute-start | bytes 110600 | tf_op jit(solution)/shard_map/ppermute | solution.py:19
  7.3 0.5 %shard_map.96 = (bf16[128,128]{1,0:T(8,128)(2,1)S(1)}, f32[128,128]{1,0:T(8,128)S(1)}, bf16[128,512]{1,0:T(8,128)(2,1)S(1)}, bf16[64,512]{1,0:T(8,128)(2,1)S(1)}...) custom-call(f32[72,128]{1,0:T(8,128)S(1)} %get-tuple-element.21.refs_0_, f32[272,128]{1,0:T(8,128)S(1)} %get-tuple-element.22.refs_1_.refs_2_), custom_call_target="tpu_custom_call" | custom-call | tf_op jit(solution)/shard_map/pallas_call | solution.py:23
  7.8 1.0 %collective-permute-done.1.refs_2_.refs_3_ = f32[272,128]{1,0:T(8,128)S(1)} collective-permute-done((f32[272,128]{1,0:T(8,128)S(1)}, f32[272,128]{1,0:T(8,128)S(1)}, u32[]{:S(2)}, u32[]{:S(2)}) %collective-permute-start.1) | collective-permute-done | bytes 139296 | tf_op jit(solution)/shard_map/ppermute | solution.py:19
  8.8 0.4 %shard_map.97 = (bf16[128,512]{1,0:T(8,128)(2,1)S(1)}, bf16[64,512]{1,0:T(8,128)(2,1)S(1)}, f32[64,128]{1,0:T(8,128)S(1)}, f32[64,64]{1,0:T(8,128)S(1)}) custom-call(bf16[128,128]{1,0:T(8,128)(2,1)S(1)} %get-tuple-element.25.refs_0_, f32[128,128]{1,0:T(8,128)S(1)} %get-tuple-element.26.refs_1_, f32[272,128]{1,0:T(8,128)S(1)} %collective-permute-done.1.refs_2_.refs_3_, ...), custom_call_target="tpu_custom_call" | custom-call | tf_op jit(solution)/shard_map/pallas_call | solution.py:23
  9.2 0.5 %collective-permute-done.refs_1_ = f32[72,128]{1,0:T(8,128)S(1)} collective-permute-done((f32[72,128]{1,0:T(8,128)S(1)}, f32[72,128]{1,0:T(8,128)S(1)}, u32[]{:S(2)}, u32[]{:S(2)}) %collective-permute-start) | collective-permute-done | bytes 36896 | tf_op jit(solution)/shard_map/ppermute | solution.py:19
  9.7 0.6 %shard_map.98 = (f32[160,128]{1,0:T(8,128)S(1)}, f32[2,128]{1,0:T(2,128)S(1)}, f32[2,128]{1,0:T(2,128)S(1)}) custom-call(f32[72,128]{1,0:T(8,128)S(1)} %get-tuple-element.21.refs_0_, f32[72,128]{1,0:T(8,128)S(1)} %collective-permute-done.refs_1_, f32[272,128]{1,0:T(8,128)S(1)} %get-tuple-element.22.refs_1_.refs_2_, ...), custom_call_target="tpu_custom_call" | custom-call | tf_op jit(solution)/shard_map/pallas_call | solution.py:23
  10.3 2.5 %collective-permute-start.2 = (f32[160,128]{1,0:T(8,128)S(1)}, f32[160,128]{1,0:T(8,128)S(1)}, u32[]{:S(2)}, u32[]{:S(2)}) collective-permute-start(f32[160,128]{1,0:T(8,128)S(1)} %get-tuple-element.33.own), channel_id=1, source_target_pairs={{0,2},{1,3},{2,0},{3,1},{4,6},{5,7},{6,4},{7,5},{8,10},{9,11},{10,... | collective-permute-start | bytes 245768 | tf_op jit(solution)/shard_map/ppermute | solution.py:19
  12.8 3.1 %collective-permute-done.2.other = f32[160,128]{1,0:T(8,128)S(1)} collective-permute-done((f32[160,128]{1,0:T(8,128)S(1)}, f32[160,128]{1,0:T(8,128)S(1)}, u32[]{:S(2)}, u32[]{:S(2)}) %collective-permute-start.2) | collective-permute-done | bytes 81952 | tf_op jit(solution)/shard_map/ppermute | solution.py:19
  15.9 0.4 %shard_map.99 = (f32[64,128]{1,0:T(8,128)S(1)}, f32[128,128]{1,0:T(8,128)S(1)}) custom-call(f32[160,128]{1,0:T(8,128)S(1)} %get-tuple-element.33.own, f32[160,128]{1,0:T(8,128)S(1)} %collective-permute-done.2.other, f32[2,128]{1,0:T(2,128)S(1)} %get-tuple-element.34.freq, f32[2,128]{1,0:T(2,128)S(1)} %get-tuple-element.35.ports), custom_call_target="tpu_custom_call" | custom-call | tf_op jit(solution)/shard_map/pallas_call | solution.py:23
  16.4 0.1 collective-permute-start.3
  16.4 1.2 %collective-permute-done.3 = f32[64,128]{1,0:T(8,128)S(1)} collective-permute-done((f32[64,128]{1,0:T(8,128)S(1)}, f32[64,128]{1,0:T(8,128)S(1)}, u32[]{:S(2)}, u32[]{:S(2)}) %collective-permute-start.3) | collective-permute-done | bytes 32800 | tf_op jit(solution)/shard_map/ppermute | solution.py:19
  17.6 1.7 %collective-permute-start.4 = (f32[64,128]{1,0:T(8,128)S(1)}, f32[64,128]{1,0:T(8,128)S(1)}, u32[]{:S(2)}, u32[]{:S(2)}) collective-permute-start(f32[64,128]{1,0:T(8,128)S(1)} %add.6), channel_id=1, source_target_pairs={{0,5},{1,4},{2,7},{3,6},{4,1},{5,0},{6,3},{7,2},{8,13},{9,12},{10,... | collective-permute-start | bytes 98312 | tf_op jit(solution)/shard_map/ppermute | solution.py:19
  19.4 1.6 %collective-permute-done.4 = f32[64,128]{1,0:T(8,128)S(1)} collective-permute-done((f32[64,128]{1,0:T(8,128)S(1)}, f32[64,128]{1,0:T(8,128)S(1)}, u32[]{:S(2)}, u32[]{:S(2)}) %collective-permute-start.4) | collective-permute-done | bytes 32800 | tf_op jit(solution)/shard_map/ppermute | solution.py:19
  21.0 1.4 %collective-permute-start.5 = (f32[64,128]{1,0:T(8,128)S(1)}, f32[64,128]{1,0:T(8,128)S(1)}, u32[]{:S(2)}, u32[]{:S(2)}) collective-permute-start(f32[64,128]{1,0:T(8,128)S(1)} %add.7.own), channel_id=1, source_target_pairs={{0,12},{1,13},{2,14},{3,15},{4,8},{5,9},{6,10},{7,11},{8,4},{9,5},... | collective-permute-start | bytes 98312 | tf_op jit(solution)/shard_map/ppermute | solution.py:19
  22.4 1.3 %collective-permute-start.6 = (f32[64,128]{1,0:T(8,128)S(1)}, f32[64,128]{1,0:T(8,128)S(1)}, u32[]{:S(2)}, u32[]{:S(2)}) collective-permute-start(f32[64,128]{1,0:T(8,128)S(1)} %add.7.own), channel_id=1, source_target_pairs={{0,20},{1,21},{2,22},{3,23},{4,16},{5,17},{6,18},{7,19},{8,28},{9,... | collective-permute-start | bytes 98312 | tf_op jit(solution)/shard_map/ppermute | solution.py:19
  23.7 0.4 %collective-permute-start.7 = (f32[64,128]{1,0:T(8,128)S(1)}, f32[64,128]{1,0:T(8,128)S(1)}, u32[]{:S(2)}, u32[]{:S(2)}) collective-permute-start(f32[64,128]{1,0:T(8,128)S(1)} %add.7.own), channel_id=1, source_target_pairs={{0,28},{1,29},{2,30},{3,31},{4,24},{5,25},{6,26},{7,27},{8,20},{9,... | collective-permute-start | bytes 98312 | tf_op jit(solution)/shard_map/ppermute | solution.py:19
  24.1 0.2 collective-permute-done.5.first
  24.3 1.4 %collective-permute-done.6.second = f32[64,128]{1,0:T(8,128)S(1)} collective-permute-done((f32[64,128]{1,0:T(8,128)S(1)}, f32[64,128]{1,0:T(8,128)S(1)}, u32[]{:S(2)}, u32[]{:S(2)}) %collective-permute-start.6) | collective-permute-done | bytes 32800 | tf_op jit(solution)/shard_map/ppermute | solution.py:19
  25.8 2.2 %collective-permute-done.7.third = f32[64,128]{1,0:T(8,128)S(1)} collective-permute-done((f32[64,128]{1,0:T(8,128)S(1)}, f32[64,128]{1,0:T(8,128)S(1)}, u32[]{:S(2)}, u32[]{:S(2)}) %collective-permute-start.7) | collective-permute-done | bytes 32800 | tf_op jit(solution)/shard_map/ppermute | solution.py:19
  28.0 2.4 %shard_map.100 = (f32[64,128]{1,0:T(8,128)}, f32[64,64]{1,0:T(8,128)}) custom-call(f32[64,128]{1,0:T(8,128)S(1)} %add.7.own, f32[64,128]{1,0:T(8,128)S(1)} %collective-permute-done.5.first, f32[64,128]{1,0:T(8,128)S(1)} %collective-permute-done.6.second, f32[64,128]{1,0:T(8,128)S(1)} %collective-permute-done.7.third, f32[128,128]{1,0:T(8,128)S(1)} %get-tuple-element.37.sketch), custom_call_target="tpu_custom_call" | custom-call | tf_op jit(solution)/shard_map/pallas_call | solution.py:23
  (2 shorter events, 0.0 us)
Async XLA Ops:
  1.6 7.2 %collective-permute-start.1 = (f32[272,128]{1,0:T(8,128)S(1)}, f32[272,128]{1,0:T(8,128)S(1)}, u32[]{:S(2)}, u32[]{:S(2)}) collective-permute-start(f32[272,128]{1,0:T(8,128)S(1)} %get-tuple-element.22.refs_1_.refs_2_), channel_id=1, source_target_pairs={{0,1},{1,0},{2,3},{3,2},{4,5},{5,4},{6,7},{7,6},{8,9},{9,8},{10,11... | collective-permute-start | bytes 417800 | tf_op jit(solution)/shard_map/ppermute | solution.py:19
  4.7 5.0 %collective-permute-start = (f32[72,128]{1,0:T(8,128)S(1)}, f32[72,128]{1,0:T(8,128)S(1)}, u32[]{:S(2)}, u32[]{:S(2)}) collective-permute-start(f32[72,128]{1,0:T(8,128)S(1)} %get-tuple-element.21.refs_0_), channel_id=1, source_target_pairs={{0,2},{1,3},{2,0},{3,1},{4,6},{5,7},{6,4},{7,5},{8,10},{9,11},{10,... | collective-permute-start | bytes 110600 | tf_op jit(solution)/shard_map/ppermute | solution.py:19
  10.3 5.7 %collective-permute-start.2 = (f32[160,128]{1,0:T(8,128)S(1)}, f32[160,128]{1,0:T(8,128)S(1)}, u32[]{:S(2)}, u32[]{:S(2)}) collective-permute-start(f32[160,128]{1,0:T(8,128)S(1)} %get-tuple-element.33.own), channel_id=1, source_target_pairs={{0,2},{1,3},{2,0},{3,1},{4,6},{5,7},{6,4},{7,5},{8,10},{9,11},{10,... | collective-permute-start | bytes 245768 | tf_op jit(solution)/shard_map/ppermute | solution.py:19
  16.4 1.3 %collective-permute-start.3 = (f32[64,128]{1,0:T(8,128)S(1)}, f32[64,128]{1,0:T(8,128)S(1)}, u32[]{:S(2)}, u32[]{:S(2)}) collective-permute-start(f32[64,128]{1,0:T(8,128)S(1)} %get-tuple-element.36), channel_id=1, source_target_pairs={{0,4},{1,5},{2,6},{3,7},{4,0},{5,1},{6,2},{7,3},{8,12},{9,13},{10,... | collective-permute-start | bytes 98312 | tf_op jit(solution)/shard_map/ppermute | solution.py:19
  17.6 3.3 %collective-permute-start.4 = (f32[64,128]{1,0:T(8,128)S(1)}, f32[64,128]{1,0:T(8,128)S(1)}, u32[]{:S(2)}, u32[]{:S(2)}) collective-permute-start(f32[64,128]{1,0:T(8,128)S(1)} %add.6), channel_id=1, source_target_pairs={{0,5},{1,4},{2,7},{3,6},{4,1},{5,0},{6,3},{7,2},{8,13},{9,12},{10,... | collective-permute-start | bytes 98312 | tf_op jit(solution)/shard_map/ppermute | solution.py:19
  21.0 3.3 %collective-permute-start.5 = (f32[64,128]{1,0:T(8,128)S(1)}, f32[64,128]{1,0:T(8,128)S(1)}, u32[]{:S(2)}, u32[]{:S(2)}) collective-permute-start(f32[64,128]{1,0:T(8,128)S(1)} %add.7.own), channel_id=1, source_target_pairs={{0,12},{1,13},{2,14},{3,15},{4,8},{5,9},{6,10},{7,11},{8,4},{9,5},... | collective-permute-start | bytes 98312 | tf_op jit(solution)/shard_map/ppermute | solution.py:19
  22.4 3.3 %collective-permute-start.6 = (f32[64,128]{1,0:T(8,128)S(1)}, f32[64,128]{1,0:T(8,128)S(1)}, u32[]{:S(2)}, u32[]{:S(2)}) collective-permute-start(f32[64,128]{1,0:T(8,128)S(1)} %add.7.own), channel_id=1, source_target_pairs={{0,20},{1,21},{2,22},{3,23},{4,16},{5,17},{6,18},{7,19},{8,28},{9,... | collective-permute-start | bytes 98312 | tf_op jit(solution)/shard_map/ppermute | solution.py:19
  23.7 4.2 %collective-permute-start.7 = (f32[64,128]{1,0:T(8,128)S(1)}, f32[64,128]{1,0:T(8,128)S(1)}, u32[]{:S(2)}, u32[]{:S(2)}) collective-permute-start(f32[64,128]{1,0:T(8,128)S(1)} %add.7.own), channel_id=1, source_target_pairs={{0,28},{1,29},{2,30},{3,31},{4,24},{5,25},{6,26},{7,27},{8,20},{9,... | collective-permute-start | bytes 98312 | tf_op jit(solution)/shard_map/ppermute | solution.py:19

commit v8 on v7

--- a/solution.py
+++ b/solution.py
@@ -52,12 +52,13 @@
     for i in (5, 2, 0, 1, 3, 4, 6, 7):
         copies[i].start()
     mu, lp, lv, lam, rp, rv, col, w = held
-    left[K + 2 :, :] = jnp.zeros((left.shape[0] - K - 2, LANES), jnp.float32)
     for copy in copies:
         copy.wait()
-    left[:K, :] = lv[...].astype(jnp.float32)
-    left[K : K + 1, :] = mu[...]
-    left[K + 1 : K + 2, :] = lp[...].astype(jnp.float32)
+    values = lv[...].astype(jnp.float32)
+    for i in range(K // 2):
+        left[i, :, :] = values[2 * i : 2 * i + 2, :]
+    left[K // 2, :1, :] = mu[...]
+    left[K // 2, 1:, :] = lp[...].astype(jnp.float32)
     count = lam.shape[0]
     for s in range(count):
         right[s * K : (s + 1) * K, :] = rv[:, s * LANES : (s + 1) * LANES].astype(jnp.float32)
@@ -74,9 +75,10 @@
 
 def left_side(left):
     index = lax.broadcasted_iota(jnp.int32, (K, LANES), 0).astype(jnp.float32)
-    hot = jnp.where(left[K + 1 : K + 2, :] == index, -1.0, 0.0)
-    side = jnp.concatenate([left[:K, :], hot], axis=0).T.astype(jnp.bfloat16)
-    return side, jnp.broadcast_to(left[K : K + 1, :], (LANES, LANES)).T
+    hot = jnp.where(left[K // 2, 1:, :] == index, -1.0, 0.0)
+    values = [left[i, :, :] for i in range(K // 2)]
+    side = jnp.concatenate([*values, hot], axis=0).T.astype(jnp.bfloat16)
+    return side, jnp.broadcast_to(left[K // 2, :1, :], (LANES, LANES)).T
 
 
 def right_side(right):
@@ -132,8 +134,10 @@
         for place, flip in ((q, False), (count + q, True)):
             spot = slice(place * K, (place + 1) * K)
             pay[spot, :] = jnp.where(here != flip, own, got)
-            for out, row in ((freq_row, K), (port_row, K + 1)):
-                out[place : place + 1, :] = jnp.where(here != flip, owns[q][row : row + 1, :], gots[q][row : row + 1, :])
+            for out, row in ((freq_row, 0), (port_row, 1)):
+                out[place : place + 1, :] = jnp.where(
+                    here != flip, owns[q][K // 2, row : row + 1, :], gots[q][K // 2, row : row + 1, :]
+                )
     pay[2 * count * K :, :] = jnp.concatenate([cross[: K // 2, :], cross[K // 2 :, :]], axis=1)
 
 
@@ -228,7 +232,7 @@
     along = (rights // LANES, LANES)
     left, right = kernel_call(
         pack_body,
-        (jax.ShapeDtypeStruct((K + SUB, LANES), f32), jax.ShapeDtypeStruct(((K + 4) * along[0], LANES), f32)),
+        (jax.ShapeDtypeStruct((K // 2 + 1, 2, LANES), f32), jax.ShapeDtypeStruct(((K + 4) * along[0], LANES), f32)),
         tuple(pltpu.with_memory_space_constraint(v, pltpu.HBM) for v in (
             left_points.reshape(1, rows),
             left_ports.reshape(1, rows),

time: 30.5 us -> 30.4 us (level)
  no operation moved by 1% of the time
where the time goes in v8:
time: 30.4 us; the launch traced here: 30.3 us
  starting transfers between devices  13.2 us (43%)
  waiting for transfers between devices  11.1 us (37%)
  Pallas kernels  5.23 us (17%)
  between operations  0.69 us (2%)
    ppermute x8, starting transfers between devices, swap(): return lax.ppermute(value, ('wide', 'blk'), pairs)  13.2 us
    ppermute x8, waiting for transfers between devices, swap(): return lax.ppermute(value, ('wide', 'blk'), pairs)  11.1 us
    pallas_call x6, Pallas kernels, kernel_call(): pl.pallas_call(body, out_shape=out_shape, compiler_params=pltpu.CompilerP...  5.23 us
  transfers between devices with their start and end apart: 8, of which 8 were waited for; matrix products, arithmetic and copies ran while one was open for 0% of the time, Pallas kernels for 3%

profile of v8, /device:TPU:0, one launch (start us, length us, event | category | flops | bytes accessed | tf_op | source)
XLA Modules:
  0.0 30.3 jit_solution(13564968185046936001)
XLA Ops:
  0.6 0.9 %shard_map.95 = (f32[33,2,128]{2,1,0:T(2,128)S(1)}, f32[272,128]{1,0:T(8,128)S(1)}) custom-call(f32[1,128]{1,0:T(1,128)} %bitcast.15, s32[1,128]{1,0:T(1,128)} %bitcast.16, bf16[64,128]{1,0:T(8,128)(2,1)} %bitcast.10, f32[4,128]{1,0:T(4,128)} %bitcast.11, s32[4,128]{1,0:T(4,128)} %bitcast.12, bf16[64,512]{1,0:T(8,128)(2,1)} %bitcast.9, s32[4,128]{1,0:T(4,128)} %bitcast.13, ...), custom_call_target="tpu_custom_call" | custom-call | tf_op jit(solution)/shard_map/pallas_call | solution.py:23
  1.6 3.1 %collective-permute-start.1 = (f32[272,128]{1,0:T(8,128)S(1)}, f32[272,128]{1,0:T(8,128)S(1)}, u32[]{:S(2)}, u32[]{:S(2)}) collective-permute-start(f32[272,128]{1,0:T(8,128)S(1)} %get-tuple-element.22.refs_1_.refs_2_), channel_id=1, source_target_pairs={{0,1},{1,0},{2,3},{3,2},{4,5},{5,4},{6,7},{7,6},{8,9},{9,8},{10,11... | collective-permute-start | bytes 417800 | tf_op jit(solution)/shard_map/ppermute | solution.py:19
  4.7 2.6 %collective-permute-start = (f32[33,2,128]{2,1,0:T(2,128)S(1)}, f32[33,2,128]{2,1,0:T(2,128)S(1)}, u32[]{:S(2)}, u32[]{:S(2)}) collective-permute-start(f32[33,2,128]{2,1,0:T(2,128)S(1)} %get-tuple-element.21.refs_0_), channel_id=1, source_target_pairs={{0,2},{1,3},{2,0},{3,1},{4,6},{5,7},{6,4},{7,5},{8,10},{9,11},{10,... | collective-permute-start | bytes 101384 | tf_op jit(solution)/shard_map/ppermute | solution.py:19
  7.3 0.5 %shard_map.96 = (bf16[128,128]{1,0:T(8,128)(2,1)S(1)}, f32[128,128]{1,0:T(8,128)S(1)}, bf16[128,512]{1,0:T(8,128)(2,1)S(1)}, bf16[64,512]{1,0:T(8,128)(2,1)S(1)}...) custom-call(f32[33,2,128]{2,1,0:T(2,128)S(1)} %get-tuple-element.21.refs_0_, f32[272,128]{1,0:T(8,128)S(1)} %get-tuple-element.22.refs_1_.refs_2_), custom_call_target="tpu_custom_call" | custom-call | tf_op jit(solution)/shard_map/pallas_call | solution.py:23
  7.8 1.0 %collective-permute-done.1.refs_2_.refs_3_ = f32[272,128]{1,0:T(8,128)S(1)} collective-permute-done((f32[272,128]{1,0:T(8,128)S(1)}, f32[272,128]{1,0:T(8,128)S(1)}, u32[]{:S(2)}, u32[]{:S(2)}) %collective-permute-start.1) | collective-permute-done | bytes 139296 | tf_op jit(solution)/shard_map/ppermute | solution.py:19
  8.7 0.4 %shard_map.97 = (bf16[128,512]{1,0:T(8,128)(2,1)S(1)}, bf16[64,512]{1,0:T(8,128)(2,1)S(1)}, f32[64,128]{1,0:T(8,128)S(1)}, f32[64,64]{1,0:T(8,128)S(1)}) custom-call(bf16[128,128]{1,0:T(8,128)(2,1)S(1)} %get-tuple-element.25.refs_0_, f32[128,128]{1,0:T(8,128)S(1)} %get-tuple-element.26.refs_1_, f32[272,128]{1,0:T(8,128)S(1)} %collective-permute-done.1.refs_2_.refs_3_, ...), custom_call_target="tpu_custom_call" | custom-call | tf_op jit(solution)/shard_map/pallas_call | solution.py:23
  9.2 0.5 %collective-permute-done.refs_1_ = f32[33,2,128]{2,1,0:T(2,128)S(1)} collective-permute-done((f32[33,2,128]{2,1,0:T(2,128)S(1)}, f32[33,2,128]{2,1,0:T(2,128)S(1)}, u32[]{:S(2)}, u32[]{:S(2)}) %collective-permute-start) | collective-permute-done | bytes 33824 | tf_op jit(solution)/shard_map/ppermute | solution.py:19
  9.6 0.6 %shard_map.98 = (f32[160,128]{1,0:T(8,128)S(1)}, f32[2,128]{1,0:T(2,128)S(1)}, f32[2,128]{1,0:T(2,128)S(1)}) custom-call(f32[33,2,128]{2,1,0:T(2,128)S(1)} %get-tuple-element.21.refs_0_, f32[33,2,128]{2,1,0:T(2,128)S(1)} %collective-permute-done.refs_1_, f32[272,128]{1,0:T(8,128)S(1)} %get-tuple-element.22.refs_1_.refs_2_, ...), custom_call_target="tpu_custom_call" | custom-call | tf_op jit(solution)/shard_map/pallas_call | solution.py:23
  10.2 2.6 %collective-permute-start.2 = (f32[160,128]{1,0:T(8,128)S(1)}, f32[160,128]{1,0:T(8,128)S(1)}, u32[]{:S(2)}, u32[]{:S(2)}) collective-permute-start(f32[160,128]{1,0:T(8,128)S(1)} %get-tuple-element.33.own), channel_id=1, source_target_pairs={{0,2},{1,3},{2,0},{3,1},{4,6},{5,7},{6,4},{7,5},{8,10},{9,11},{10,... | collective-permute-start | bytes 245768 | tf_op jit(solution)/shard_map/ppermute | solution.py:19
  12.8 3.1 %collective-permute-done.2.other = f32[160,128]{1,0:T(8,128)S(1)} collective-permute-done((f32[160,128]{1,0:T(8,128)S(1)}, f32[160,128]{1,0:T(8,128)S(1)}, u32[]{:S(2)}, u32[]{:S(2)}) %collective-permute-start.2) | collective-permute-done | bytes 81952 | tf_op jit(solution)/shard_map/ppermute | solution.py:19
  15.9 0.4 %shard_map.99 = (f32[64,128]{1,0:T(8,128)S(1)}, f32[128,128]{1,0:T(8,128)S(1)}) custom-call(f32[160,128]{1,0:T(8,128)S(1)} %get-tuple-element.33.own, f32[160,128]{1,0:T(8,128)S(1)} %collective-permute-done.2.other, f32[2,128]{1,0:T(2,128)S(1)} %get-tuple-element.34.freq, f32[2,128]{1,0:T(2,128)S(1)} %get-tuple-element.35.ports), custom_call_target="tpu_custom_call" | custom-call | tf_op jit(solution)/shard_map/pallas_call | solution.py:23
  16.3 0.1 collective-permute-start.3
  16.4 1.2 %collective-permute-done.3 = f32[64,128]{1,0:T(8,128)S(1)} collective-permute-done((f32[64,128]{1,0:T(8,128)S(1)}, f32[64,128]{1,0:T(8,128)S(1)}, u32[]{:S(2)}, u32[]{:S(2)}) %collective-permute-start.3) | collective-permute-done | bytes 32800 | tf_op jit(solution)/shard_map/ppermute | solution.py:19
  17.6 1.7 %collective-permute-start.4 = (f32[64,128]{1,0:T(8,128)S(1)}, f32[64,128]{1,0:T(8,128)S(1)}, u32[]{:S(2)}, u32[]{:S(2)}) collective-permute-start(f32[64,128]{1,0:T(8,128)S(1)} %add.6), channel_id=1, source_target_pairs={{0,5},{1,4},{2,7},{3,6},{4,1},{5,0},{6,3},{7,2},{8,13},{9,12},{10,... | collective-permute-start | bytes 98312 | tf_op jit(solution)/shard_map/ppermute | solution.py:19
  19.3 1.6 %collective-permute-done.4 = f32[64,128]{1,0:T(8,128)S(1)} collective-permute-done((f32[64,128]{1,0:T(8,128)S(1)}, f32[64,128]{1,0:T(8,128)S(1)}, u32[]{:S(2)}, u32[]{:S(2)}) %collective-permute-start.4) | collective-permute-done | bytes 32800 | tf_op jit(solution)/shard_map/ppermute | solution.py:19
  20.9 1.4 %collective-permute-start.5 = (f32[64,128]{1,0:T(8,128)S(1)}, f32[64,128]{1,0:T(8,128)S(1)}, u32[]{:S(2)}, u32[]{:S(2)}) collective-permute-start(f32[64,128]{1,0:T(8,128)S(1)} %add.7.own), channel_id=1, source_target_pairs={{0,12},{1,13},{2,14},{3,15},{4,8},{5,9},{6,10},{7,11},{8,4},{9,5},... | collective-permute-start | bytes 98312 | tf_op jit(solution)/shard_map/ppermute | solution.py:19
  22.4 1.3 %collective-permute-start.6 = (f32[64,128]{1,0:T(8,128)S(1)}, f32[64,128]{1,0:T(8,128)S(1)}, u32[]{:S(2)}, u32[]{:S(2)}) collective-permute-start(f32[64,128]{1,0:T(8,128)S(1)} %add.7.own), channel_id=1, source_target_pairs={{0,20},{1,21},{2,22},{3,23},{4,16},{5,17},{6,18},{7,19},{8,28},{9,... | collective-permute-start | bytes 98312 | tf_op jit(solution)/shard_map/ppermute | solution.py:19
  23.6 0.4 %collective-permute-start.7 = (f32[64,128]{1,0:T(8,128)S(1)}, f32[64,128]{1,0:T(8,128)S(1)}, u32[]{:S(2)}, u32[]{:S(2)}) collective-permute-start(f32[64,128]{1,0:T(8,128)S(1)} %add.7.own), channel_id=1, source_target_pairs={{0,28},{1,29},{2,30},{3,31},{4,24},{5,25},{6,26},{7,27},{8,20},{9,... | collective-permute-start | bytes 98312 | tf_op jit(solution)/shard_map/ppermute | solution.py:19
  24.1 0.2 collective-permute-done.5.first
  24.3 1.4 %collective-permute-done.6.second = f32[64,128]{1,0:T(8,128)S(1)} collective-permute-done((f32[64,128]{1,0:T(8,128)S(1)}, f32[64,128]{1,0:T(8,128)S(1)}, u32[]{:S(2)}, u32[]{:S(2)}) %collective-permute-start.6) | collective-permute-done | bytes 32800 | tf_op jit(solution)/shard_map/ppermute | solution.py:19
  25.7 2.2 %collective-permute-done.7.third = f32[64,128]{1,0:T(8,128)S(1)} collective-permute-done((f32[64,128]{1,0:T(8,128)S(1)}, f32[64,128]{1,0:T(8,128)S(1)}, u32[]{:S(2)}, u32[]{:S(2)}) %collective-permute-start.7) | collective-permute-done | bytes 32800 | tf_op jit(solution)/shard_map/ppermute | solution.py:19
  27.9 2.4 %shard_map.100 = (f32[64,128]{1,0:T(8,128)}, f32[64,64]{1,0:T(8,128)}) custom-call(f32[64,128]{1,0:T(8,128)S(1)} %add.7.own, f32[64,128]{1,0:T(8,128)S(1)} %collective-permute-done.5.first, f32[64,128]{1,0:T(8,128)S(1)} %collective-permute-done.6.second, f32[64,128]{1,0:T(8,128)S(1)} %collective-permute-done.7.third, f32[128,128]{1,0:T(8,128)S(1)} %get-tuple-element.37.sketch), custom_call_target="tpu_custom_call" | custom-call | tf_op jit(solution)/shard_map/pallas_call | solution.py:23
  (2 shorter events, 0.0 us)
Async XLA Ops:
  1.6 7.2 %collective-permute-start.1 = (f32[272,128]{1,0:T(8,128)S(1)}, f32[272,128]{1,0:T(8,128)S(1)}, u32[]{:S(2)}, u32[]{:S(2)}) collective-permute-start(f32[272,128]{1,0:T(8,128)S(1)} %get-tuple-element.22.refs_1_.refs_2_), channel_id=1, source_target_pairs={{0,1},{1,0},{2,3},{3,2},{4,5},{5,4},{6,7},{7,6},{8,9},{9,8},{10,11... | collective-permute-start | bytes 417800 | tf_op jit(solution)/shard_map/ppermute | solution.py:19
  4.7 4.9 %collective-permute-start = (f32[33,2,128]{2,1,0:T(2,128)S(1)}, f32[33,2,128]{2,1,0:T(2,128)S(1)}, u32[]{:S(2)}, u32[]{:S(2)}) collective-permute-start(f32[33,2,128]{2,1,0:T(2,128)S(1)} %get-tuple-element.21.refs_0_), channel_id=1, source_target_pairs={{0,2},{1,3},{2,0},{3,1},{4,6},{5,7},{6,4},{7,5},{8,10},{9,11},{10,... | collective-permute-start | bytes 101384 | tf_op jit(solution)/shard_map/ppermute | solution.py:19
  10.2 5.7 %collective-permute-start.2 = (f32[160,128]{1,0:T(8,128)S(1)}, f32[160,128]{1,0:T(8,128)S(1)}, u32[]{:S(2)}, u32[]{:S(2)}) collective-permute-start(f32[160,128]{1,0:T(8,128)S(1)} %get-tuple-element.33.own), channel_id=1, source_target_pairs={{0,2},{1,3},{2,0},{3,1},{4,6},{5,7},{6,4},{7,5},{8,10},{9,11},{10,... | collective-permute-start | bytes 245768 | tf_op jit(solution)/shard_map/ppermute | solution.py:19
  16.3 1.3 %collective-permute-start.3 = (f32[64,128]{1,0:T(8,128)S(1)}, f32[64,128]{1,0:T(8,128)S(1)}, u32[]{:S(2)}, u32[]{:S(2)}) collective-permute-start(f32[64,128]{1,0:T(8,128)S(1)} %get-tuple-element.36), channel_id=1, source_target_pairs={{0,4},{1,5},{2,6},{3,7},{4,0},{5,1},{6,2},{7,3},{8,12},{9,13},{10,... | collective-permute-start | bytes 98312 | tf_op jit(solution)/shard_map/ppermute | solution.py:19
  17.6 3.3 %collective-permute-start.4 = (f32[64,128]{1,0:T(8,128)S(1)}, f32[64,128]{1,0:T(8,128)S(1)}, u32[]{:S(2)}, u32[]{:S(2)}) collective-permute-start(f32[64,128]{1,0:T(8,128)S(1)} %add.6), channel_id=1, source_target_pairs={{0,5},{1,4},{2,7},{3,6},{4,1},{5,0},{6,3},{7,2},{8,13},{9,12},{10,... | collective-permute-start | bytes 98312 | tf_op jit(solution)/shard_map/ppermute | solution.py:19
  20.9 3.3 %collective-permute-start.5 = (f32[64,128]{1,0:T(8,128)S(1)}, f32[64,128]{1,0:T(8,128)S(1)}, u32[]{:S(2)}, u32[]{:S(2)}) collective-permute-start(f32[64,128]{1,0:T(8,128)S(1)} %add.7.own), channel_id=1, source_target_pairs={{0,12},{1,13},{2,14},{3,15},{4,8},{5,9},{6,10},{7,11},{8,4},{9,5},... | collective-permute-start | bytes 98312 | tf_op jit(solution)/shard_map/ppermute | solution.py:19
  22.4 3.3 %collective-permute-start.6 = (f32[64,128]{1,0:T(8,128)S(1)}, f32[64,128]{1,0:T(8,128)S(1)}, u32[]{:S(2)}, u32[]{:S(2)}) collective-permute-start(f32[64,128]{1,0:T(8,128)S(1)} %add.7.own), channel_id=1, source_target_pairs={{0,20},{1,21},{2,22},{3,23},{4,16},{5,17},{6,18},{7,19},{8,28},{9,... | collective-permute-start | bytes 98312 | tf_op jit(solution)/shard_map/ppermute | solution.py:19
  23.6 4.2 %collective-permute-start.7 = (f32[64,128]{1,0:T(8,128)S(1)}, f32[64,128]{1,0:T(8,128)S(1)}, u32[]{:S(2)}, u32[]{:S(2)}) collective-permute-start(f32[64,128]{1,0:T(8,128)S(1)} %add.7.own), channel_id=1, source_target_pairs={{0,28},{1,29},{2,30},{3,31},{4,24},{5,25},{6,26},{7,27},{8,20},{9,... | collective-permute-start | bytes 98312 | tf_op jit(solution)/shard_map/ppermute | solution.py:19
